TPU v7x, 32 devices: a whole 2x2x4 slice. The times are simulated.
32 devices in a mesh: ga: 2 (over y), col: 16 (over z, x, core).
Axes of the slice: x: 2, y: 2, z: 4, core: 2. Of those that a mesh axis runs over, the one named last changes fastest.
Arguments:
- query_nope: bfloat16 [128, 4096], P(('ga', 'col')), parts along dimension 0, may hold values from -6 to 6
- query_rope: bfloat16 [128, 2048], P(('ga', 'col')), parts along dimension 0, may hold values from -104 to 104, as said below
- cache: bfloat16 [8192, 576], P(('ga', 'col')), parts along dimension 0, may hold values from -6 to 6, as said below
- key_docs: int32 [8192], P(('ga', 'col')), parts along dimension 0, may hold values from 0 to 7, as said below
- query_docs: int32 [128], P(('ga', 'col')), parts along dimension 0, may hold values from 0 to 7, as said below
- query_pos: int32 [128], P(('ga', 'col')), parts along dimension 0, may hold values from 1 to 4095, as said below
- w_uk: bfloat16 [512, 4096], replicated, may hold values from -0.25 to 0.25
- w_uv: bfloat16 [512, 4096], replicated, may hold values from -0.25 to 0.25
Outputs:
- attended: bfloat16 [128, 4096], P(('ga', 'col')), parts along dimension 0
There are 2 independent parts, one for each index of `ga`. A program takes and returns all parts, laid end to end along the dimension named above; an argument that names none is the same for every part. Nothing has to cross between parts.
Inputs may be any that keep to these rules, and one draw needn't show every extreme that they name: `key_docs`: ids start at 0 and never fall along the cache; a document is a run of equal ids; eight documents. query_docs[i] equals key_docs[query_pos[i]]. `query_pos`: a position from 1 to 4095, never the first token of a document. `query_rope`: real values. `cache`: real values.
All inputs are finite; a program needn't handle non-finite values.
Results may differ from a plain program's by a relative error of at most 0.001.
Values may be sent and summed in bfloat16 or wider, within the bound.
No kernel may reach another device: no remote copies, remote signals or barrier semaphores. Data moves between devices by JAX's collectives and lax.ppermute only.
A program may use at most 192 MiB of HBM per device.

v0:
```python
import math

import jax
import jax.numpy as jnp
from jax import lax
from jax.sharding import PartitionSpec as P

H = 32
DN = 128
DR = 64
DV = 128
R = 512


def shards(query_nope, query_rope, cache, key_docs, query_docs, query_pos, w_uk, w_uv):
    scale = 1.0 / math.sqrt(DN + DR)
    highest = lax.Precision.HIGHEST
    own_rows = query_nope.shape[0]
    q_flat = query_nope.astype(jnp.float32).reshape(own_rows, H, DN)
    absorbed = jnp.einsum(
        "qhd,rhd->qhr", q_flat, w_uk.astype(jnp.float32).reshape(R, H, DN), precision=highest
    )
    q_turn = query_rope.reshape(own_rows, H, DR).astype(jnp.float32)
    q_whole = jnp.concatenate([absorbed, q_turn], axis=2).reshape(own_rows * H, R + DR)
    row_docs = jnp.repeat(query_docs, H)
    row_pos = jnp.repeat(query_pos, H)
    rows_all = own_rows * H
    best = jnp.full((rows_all,), -1e30, jnp.float32)
    piece = lax.all_gather(cache, "col", axis=0, tiled=True)
    piece_docs = lax.all_gather(key_docs, "col", axis=0, tiled=True)
    count = piece.shape[0]
    wide_piece = piece.astype(jnp.float32)
    scores = jnp.einsum("rc,kc->rk", q_whole, wide_piece, precision=highest) * scale
    key_place = jnp.arange(count, dtype=jnp.int32)
    visible = (piece_docs[None, :] == row_docs[:, None]) & (key_place[None, :] <= row_pos[:, None])
    scores = jnp.where(visible, scores, -1e30)
    new_best = jnp.maximum(best, jnp.max(scores, axis=1))
    weights = jnp.where(visible, jnp.exp(scores - new_best[:, None]), 0.0)
    total = jnp.sum(weights, axis=1)
    added = jnp.dot(weights, wide_piece[:, :R], precision=highest)
    accum = added
    best, total, accum = (new_best, total, accum)
    mixed = (accum / total[:, None]).reshape(own_rows, H, R)
    result = jnp.einsum(
        "qhr,rhv->qhv", mixed, w_uv.reshape(R, H, DV).astype(jnp.float32), precision=highest
    )
    return result.reshape(own_rows, H * DV).astype(jnp.bfloat16)


def solution(mesh):
    placed = (
        P(("ga", "col"), None),
        P(("ga", "col"), None),
        P(("ga", "col"), None),
        P(("ga", "col")),
        P(("ga", "col")),
        P(("ga", "col")),
        P(),
        P(),
    )
    return jax.shard_map(
        shards, mesh=mesh, in_specs=placed, out_specs=P(("ga", "col"), None), check_vma=False
    )
```

profile of v0, /device:TPU:0, one launch (start us, length us, event | category | flops | bytes accessed | tf_op | source)
XLA Modules:
  0.0 87.9 jit_solution(14045177649011529404)
XLA Ops:
  6.5 0.0 copy-start
  6.5 0.0 all-gather.3.cloned.1.call-start
  6.5 0.7 all-gather.3.cloned.1.call-update
  7.3 0.7 broadcast_in_dim.20
  8.0 0.1 eq.16
  8.1 0.7 broadcast_in_dim.21
  8.8 0.1 le.16
  8.9 0.8 reshape.32
  9.7 0.0 copy-done
  9.7 0.0 copy-start.2
  9.8 3.4 %fusion.11 = f32[4,32,512]{2,0,1:T(4,128)S(1)} fusion(bf16[4,4096]{1,0:T(4,128)(2,1)S(1)} %copy-done, bf16[512,4096]{1,0:T(8,128)(2,1)} %param.14), kind=kOutput, calls=%fused_computation.14 | convolution fusion | flops 16777216 | bytes 4489216 | tf_op jit(solution)/shard_map/qhd,rhd->qhr/dot_general | solution.py:20
  13.1 0.1 pad_maximum_fusion
  13.3 0.0 copy-done.2
  13.3 23.5 %all-gather = s32[16,1,256]{2,1,0:T(1,128)S(1)} all-gather(s32[1,1,256]{2,1,0:T(1,128)S(1)} %bitcast.40), channel_id=1, replica_groups=mesh['ga'=2,'col'=16] {'col'}, dimensions={0}, use_global_device_ids=true | all-gather | bytes 17408 | tf_op jit(solution)/shard_map/all_gather | solution.py:30
  36.7 31.4 %all-gather.3.cloned.1.call-done = bf16[4096,576]{0,1:T(8,128)(2,1)} async-done(((bf16[256,576]{0,1:T(8,128)(2,1)}), bf16[4096,576]{0,1:T(8,128)(2,1)}) %all-gather.3.cloned.1.call-update) | async-done | bytes 4718608 | tf_op jit(solution)/shard_map/all_gather | solution.py:29
  68.1 0.0 slice-start
  68.1 0.0 slice-start.1
  68.1 5.0 %fusion.31 = (f32[128]{0:T(128)S(1)}, f32[128,4096]{1,0:T(8,128)S(1)}) fusion(f32[128,576]{1,0:T(8,128)S(1)} %bitcast.35, bf16[4096,576]{0,1:T(8,128)(2,1)} %all-gather.3.cloned.1.call-done, s32[128]{0:T(128)S(1)} %le.16, s32[128]{0:T(128)S(1)} %eq.16, s32[4096]{0:T(1024)S(1)} %bitcast.37), kind=kOutput, calls=%fused_computation.28 | convolution fusion | flops 3627024384 | bytes 7128576 | tf_op jit(solution)/shard_map/rc,kc->rk/dot_general | solution.py:33
  73.1 0.8 fusion.10
  73.9 0.0 slice-done
  73.9 0.0 slice-done.1
  73.9 0.0 copy-start.1
  73.9 4.3 %fusion.14 = f32[128,512]{1,0:T(8,128)S(1)} fusion(bf16[4096,576]{0,1:T(8,128)(2,1)S(1)} %bitcast.42, f32[128,4096]{1,0:T(8,128)S(1)} %get-tuple-element.6, f32[128]{0:T(128)S(1)} %broadcast_maximum_fusion, s32[128]{0:T(128)S(1)} %le.16, s32[4096]{0:T(1024)S(1)} %bitcast.39, s32[128]{0:T(128)S(1)} %eq.16, f32[128]{0:T(128)S(1)} %fusion.10), kind=kOutput, calls=%fused_computation.15 | convolution fusion | flops 3223912448 | bytes 6572032 | tf_op jit(solution)/shard_map/dot_general | solution.py:40
  78.2 0.0 copy-done.1
  78.2 2.8 %fusion.20 = bf16[4,4096]{1,0:T(4,128)(2,1)} fusion(f32[4,32,512]{2,1,0:T(8,128)S(1)} %bitcast.36, bf16[512,4096]{1,0:T(8,128)(2,1)S(1)} %copy-done.1), kind=kOutput, calls=%fused_computation.17 | convolution fusion | flops 100679680 | bytes 4489216 | tf_op jit(solution)/shard_map/qhr,rhv->qhv/dot_general | solution.py:44
  (4 shorter events, 0.1 us)
Async XLA Ops:
  6.5 3.2 %copy-start = (bf16[4,4096]{1,0:T(4,128)(2,1)S(1)}, bf16[4,4096]{1,0:T(4,128)(2,1)}, u32[]{:S(2)}) copy-start(bf16[4,4096]{1,0:T(4,128)(2,1)} %param.8) | copy-start | bytes 98308
  6.5 61.6 %all-gather.3.cloned.1.call-start = ((), (), s32[]{:S(2)}) async-start(), calls=%async_computation | async-start | bytes 5013504 | tf_op jit(solution)/shard_map/all_gather | solution.py:29
  9.7 3.5 %copy-start.2 = (s32[256]{0:T(256)S(1)}, s32[256]{0:T(256)}, u32[]{:S(2)}) copy-start(s32[256]{0:T(256)} %param.11) | copy-start | bytes 3076
  68.1 5.7 %slice-start = ((s8[4718592]{0:T(1024)(128)(4,1)}), s8[4194304]{0:T(1024)(128)(4,1)S(1)}, s32[]{:S(2)}) async-start(s8[4718592]{0:T(1024)(128)(4,1)} %bitcast.41), calls=%async_computation.1 | async-start | bytes 8388608
  68.1 5.7 %slice-start.1 = ((s8[4718592]{0:T(1024)(128)(4,1)}), s8[524288]{0:T(1024)(128)(4,1)S(1)}, s32[]{:S(2)}) async-start(s8[4718592]{0:T(1024)(128)(4,1)} %bitcast.41), calls=%async_computation.2 | async-start | bytes 1048576
  73.9 4.3 %copy-start.1 = (bf16[512,4096]{1,0:T(8,128)(2,1)S(1)}, bf16[512,4096]{1,0:T(8,128)(2,1)}, u32[]{:S(2)}) copy-start(bf16[512,4096]{1,0:T(8,128)(2,1)} %param.15) | copy-start | bytes 12582916
Sparse Core Ops, SparseCore 0:
  9.5 58.5 all-gather.2
where the time goes:
time: 88.1 us; the launch traced here: 87.9 us
  waiting for transfers between devices  32.1 us (36%)
  blocking collectives  23.5 us (27%)
  matrix products  15.4 us (17%)
  between operations  13.5 us (15%)
  local copies, waits for them, and re-layouts  2.52 us (3%)
    all_gather x1, waiting for transfers between devices, shards(): piece = lax.all_gather(cache, 'col', axis=0, tiled=True)  31.4 us
    all_gather x1, blocking collectives, shards(): piece_docs = lax.all_gather(key_docs, 'col', axis=0, tiled=True)  23.5 us
    dot_general x1, matrix products, shards(): jnp.einsum('rc,kc->rk', q_whole, wide_piece, precision=highest) * scale  4.96 us
    dot_general x1, matrix products, shards(): added = jnp.dot(weights, wide_piece[:, :R], precision=highest)  4.28 us
    dot_general x1, matrix products, shards(): jnp.einsum('qhd,rhd->qhr', q_flat, w_uk.astype(jnp.float32).reshape(R, H,...  3.38 us
    dot_general x1, matrix products, shards(): jnp.einsum('qhr,rhv->qhv', mixed, w_uv.reshape(R, H, DV).astype(jnp.float...  2.82 us
  transfers between devices with their start and end apart: 1, of which 1 were waited for; matrix products, arithmetic and copies ran while one was open for 7% of the time, Pallas kernels for 0%

commit v1 on v0

v1 whole, which is shorter than its diff:
```python
import math

import jax
import jax.numpy as jnp
from jax import lax
from jax.sharding import PartitionSpec as P

H = 32
DN = 128
DR = 64
DV = 128
R = 512
META = 128


def split(x):
    high = lax.reduce_precision(x, 8, 7)
    return high.astype(jnp.bfloat16), (x - high).astype(jnp.bfloat16)


def shards(size, query_nope, query_rope, cache, key_docs, query_docs, query_pos, w_uk, w_uv):
    scale = 1.0 / math.sqrt(DN + DR)
    near = math.gcd(size, 4)
    far = size // near
    own_rows = query_nope.shape[0]
    tokens = cache.shape[0]
    me = lax.axis_index("col")

    def swap(x, mask):
        return lax.ppermute(x, "col", [(i, i ^ mask) for i in range(size)])

    blocks, docs = [cache], [key_docs]
    step = 1
    while step < near:
        blocks = blocks + [swap(b, step) for b in blocks]
        docs = docs + [swap(d, step) for d in docs]
        step *= 2
    keys = jnp.concatenate(blocks, axis=0)
    key_doc = jnp.concatenate(docs, axis=0)
    places = [((me ^ k) * tokens) + jnp.arange(tokens, dtype=jnp.int32) for k in range(near)]
    key_place = jnp.concatenate(places, axis=0)

    meta = jnp.stack(
        [query_docs, lax.shift_right_logical(query_pos, 8), lax.bitwise_and(query_pos, 255)], axis=1
    ).astype(jnp.bfloat16)
    meta = jnp.pad(meta, ((0, 0), (0, META - 3)))
    mine = jnp.concatenate([query_nope, query_rope, meta], axis=1)
    groups = [mine] + [swap(mine, near * k) for k in range(1, far)]
    query = jnp.concatenate(groups, axis=0)
    rows = far * own_rows
    q_nope = query[:, : H * DN].reshape(rows, H, DN)
    q_rope = query[:, H * DN : H * (DN + DR)].reshape(rows, H, DR)
    meta = query[:, H * (DN + DR) :].astype(jnp.int32)
    q_doc = meta[:, 0]
    q_pos = meta[:, 1] * 256 + meta[:, 2]

    absorbed = jnp.einsum(
        "qhd,rhd->qhr", q_nope, w_uk.reshape(R, H, DN), preferred_element_type=jnp.float32
    )
    high, low = split(absorbed)
    high = jnp.concatenate([high, q_rope], axis=2)
    low = jnp.concatenate([low, jnp.zeros_like(q_rope)], axis=2)
    both = jnp.stack([high, low]).reshape(2 * rows * H, R + DR)
    scores = jnp.einsum("rc,kc->rk", both, keys, preferred_element_type=jnp.float32)
    scores = scores.reshape(2, rows, H, near * tokens)
    scores = (scores[0] + scores[1]) * scale
    visible = (key_doc[None, :] == q_doc[:, None]) & (key_place[None, :] <= q_pos[:, None])
    scores = jnp.where(visible[:, None, :], scores, -1e30)
    best = jnp.max(scores, axis=2)
    weights = jnp.where(visible[:, None, :], jnp.exp(scores - best[:, :, None]), 0.0)
    total = jnp.sum(weights, axis=2)
    high, low = split(weights)
    both = jnp.stack([high, low]).reshape(2 * rows * H, near * tokens)
    mixed = jnp.dot(both, keys[:, :R], preferred_element_type=jnp.float32)
    mixed = mixed.reshape(2, rows, H, R)
    high, low = split(mixed[0] + mixed[1])
    both = jnp.stack([high, low]).reshape(2 * rows, H, R)
    part = jnp.einsum(
        "qhr,rhv->qhv", both, w_uv.reshape(R, H, DV), preferred_element_type=jnp.float32
    )
    part = part.reshape(2, rows, H * DV)
    part = jnp.concatenate([part[0] + part[1], best, total], axis=1)

    parts = [part[:own_rows]]
    for k in range(1, far):
        parts.append(swap(part[k * own_rows : (k + 1) * own_rows], near * k))
    parts = jnp.stack(parts)
    value = parts[:, :, : H * DV].reshape(far, own_rows, H, DV)
    best = parts[:, :, H * DV : H * DV + H]
    total = parts[:, :, H * DV + H :]
    factor = jnp.exp(best - jnp.max(best, axis=0))
    total = jnp.sum(total * factor, axis=0)
    result = jnp.sum(value * factor[..., None], axis=0) / total[..., None]
    return result.reshape(own_rows, H * DV).astype(jnp.bfloat16)


def solution(mesh):
    split_rows = P(("ga", "col"), None)
    split_flat = P(("ga", "col"))
    placed = (split_rows, split_rows, split_rows, split_flat, split_flat, split_flat, P(), P())
    size = mesh.shape["col"]

    def body(*arrays):
        return shards(size, *arrays)

    return jax.shard_map(body, mesh=mesh, in_specs=placed, out_specs=split_rows, check_vma=False)
```

time: 88.1 us -> 46.9 us (0.53)
  blocking collectives: 23.5 us -> 0 us
  waiting for transfers between devices: 32.1 us -> 12.9 us
  starting transfers between devices: 0.01 us -> 14.5 us
  between operations: 13.5 us -> 0.32 us
  matrix products: 15.4 us -> 7.23 us
  other arithmetic: 0.85 us -> 7.25 us
  local copies, waits for them, and re-layouts: 2.52 us -> 4.4 us
    all_gather x1 -> x0, waiting for transfers between devices: 31.4 us -> none  [shards(): piece = lax.all_gather(cache, 'col', axis=0, tiled=True)]
    all_gather x1 -> x0, blocking collectives: 23.5 us -> none  [shards(): piece_docs = lax.all_gather(key_docs, 'col', axis=0, tiled=True)]
    ppermute x0 -> x12, starting transfers between devices: none -> 14.5 us  [swap(): return lax.ppermute(x, 'col', [(i, i ^ mask) for i in range(size)])]
    ppermute x0 -> x12, waiting for transfers between devices: none -> 12.9 us  [swap(): return lax.ppermute(x, 'col', [(i, i ^ mask) for i in range(size)])]
    dot_general x4, matrix products: 15.4 us -> 7.23 us  [the longest x1 3.4 us: shards(): jnp.einsum('qhd,rhd->qhr', q_nope, w_uk.reshape(R, H, DN), preferred_elem...]
    unnamed x10 -> x11, local copies, waits for them, and re-layouts: 0.02 us -> 2.74 us
    concatenate x1 -> x4, other arithmetic: 0.09 us -> 2.4 us  [the longest x1 0.91 us: shards(): query = jnp.concatenate(groups, axis=0)]
    convert_element_type x0 -> x4, other arithmetic: none -> 1.68 us  [the longest x2 0.98 us: split(): return (high.astype(jnp.bfloat16), (x - high).astype(jnp.bfloat16))]
  transfers between devices with their start and end apart: 1 -> 12, of which waited for: 1 -> 4; matrix products, arithmetic and copies ran while one was open for 7% -> 19% of each run, Pallas kernels for 0% -> 0%
where the time goes in v1:
time: 46.9 us; the launch traced here: 46.6 us
  starting transfers between devices  14.5 us (31%)
  waiting for transfers between devices  12.9 us (28%)
  other arithmetic  7.25 us (15%)
  matrix products  7.23 us (15%)
  local copies, waits for them, and re-layouts  4.4 us (9%)
    ppermute x12, starting transfers between devices, swap(): return lax.ppermute(x, 'col', [(i, i ^ mask) for i in range(size)])  14.5 us
    ppermute x12, waiting for transfers between devices, swap(): return lax.ppermute(x, 'col', [(i, i ^ mask) for i in range(size)])  12.9 us
    dot_general x1, matrix products, shards(): jnp.einsum('qhd,rhd->qhr', q_nope, w_uk.reshape(R, H, DN), preferred_elem...  3.4 us
    unnamed x11, local copies, waits for them, and re-layouts  2.74 us
    dot_general x1, matrix products, shards(): jnp.einsum('rc,kc->rk', both, keys, preferred_element_type=jnp.float32)  1.81 us
    dot_general x1, matrix products, shards(): mixed = jnp.dot(both, keys[:, :R], preferred_element_type=jnp.float32)  1.28 us
    convert_element_type x2, other arithmetic, split(): return (high.astype(jnp.bfloat16), (x - high).astype(jnp.bfloat16))  0.98 us
  transfers between devices with their start and end apart: 12, of which 4 were waited for; matrix products, arithmetic and copies ran while one was open for 19% of the time, Pallas kernels for 0%

profile of v1, /device:TPU:0, one launch (start us, length us, event | category | flops | bytes accessed | tf_op | source)
XLA Modules:
  0.0 46.6 jit_solution(15129852028328563460)
XLA Ops:
  0.0 0.5 %collective-permute-start = (s32[256]{0:T(256)}, s32[256]{0:T(256)S(1)}, u32[]{:S(2)}, u32[]{:S(2)}) collective-permute-start(s32[256]{0:T(256)} %param.11), channel_id=1, source_target_pairs={{0,1},{1,0},{2,3},{3,2},{4,5},{5,4},{6,7},{7,6},{8,9},{9,8},{10,11... | collective-permute-start | bytes 3080 | tf_op jit(solution)/shard_map/ppermute | solution.py:30
  0.5 2.5 %collective-permute-start.1 = (s32[256]{0:T(256)}, s32[256]{0:T(256)S(1)}, u32[]{:S(2)}, u32[]{:S(2)}) collective-permute-start(s32[256]{0:T(256)} %param.11), channel_id=1, source_target_pairs={{0,2},{1,3},{2,0},{3,1},{4,6},{5,7},{6,4},{7,5},{8,10},{9,11},{10,... | collective-permute-start | bytes 3080 | tf_op jit(solution)/shard_map/ppermute | solution.py:30
  3.0 0.7 %convert_bitcast_fusion.1 = (bf16[4,1]{0,1:T(2,128)(2,1)S(1)}, bf16[4,1]{0,1:T(2,128)(2,1)S(1)}, bf16[4,1]{0,1:T(2,128)(2,1)S(1)}) fusion(s32[4]{0:T(128)} %param.13, s32[4]{0:T(128)} %param.12), kind=kLoop, calls=%fused_computation.70 | loop fusion | flops 20 | bytes 56 | tf_op jit(solution)/shard_map/stack | solution.py:43
  3.7 0.1 copy.21
  3.8 0.8 %pad_maximum_fusion.6 = bf16[4,6272]{1,0:T(4,128)(2,1)S(1)} fusion(bf16[4,128]{1,0:T(4,128)(2,1)S(1)} %pad.5.clone, bf16[4,2048]{1,0:T(4,128)(2,1)} %param.9, bf16[4,4096]{1,0:T(4,128)(2,1)} %param.8), kind=kLoop, calls=%fused_computation.47 | loop fusion | flops 150528 | bytes 100352 | tf_op jit(solution)/shard_map/concatenate | solution.py:47
  4.6 3.7 %collective-permute-start.5 = (bf16[4,6272]{1,0:T(4,128)(2,1)S(1)}, bf16[4,6272]{1,0:T(4,128)(2,1)S(1)}, u32[]{:S(2)}, u32[]{:S(2)}) collective-permute-start(bf16[4,6272]{1,0:T(4,128)(2,1)S(1)} %pad_maximum_fusion.6), channel_id=1, source_target_pairs={{0,12},{1,13},{2,14},{3,15},{4,8},{5,9},{6,10},{7,11},{8,4},{9,5},... | collective-permute-start | bytes 150536 | tf_op jit(solution)/shard_map/ppermute | solution.py:30
  8.2 0.0 collective-permute-start.4
  8.3 0.8 %collective-permute-start.3 = (bf16[4,6272]{1,0:T(4,128)(2,1)S(1)}, bf16[4,6272]{1,0:T(4,128)(2,1)S(1)}, u32[]{:S(2)}, u32[]{:S(2)}) collective-permute-start(bf16[4,6272]{1,0:T(4,128)(2,1)S(1)} %pad_maximum_fusion.6), channel_id=1, source_target_pairs={{0,4},{1,5},{2,6},{3,7},{4,0},{5,1},{6,2},{7,3},{8,12},{9,13},{10,... | collective-permute-start | bytes 150536 | tf_op jit(solution)/shard_map/ppermute | solution.py:30
  9.0 1.0 %constant_dynamic-update-slice_fusion.3 = bf16[1024,576]{0,1:T(8,128)(2,1)S(1)} fusion(bf16[256,576]{0,1:T(8,128)(2,1)} %param.10), kind=kLoop, calls=%fused_computation.52 | loop fusion | bytes 589824
  10.1 0.0 collective-permute-done
  10.1 0.5 collective-permute-start.2
  10.5 0.0 collective-permute-done.1
  10.5 0.1 collective-permute-start.6
  10.6 3.1 %collective-permute-done.2 = s32[256]{0:T(256)S(1)} collective-permute-done((s32[256]{0:T(256)S(1)}, s32[256]{0:T(256)S(1)}, u32[]{:S(2)}, u32[]{:S(2)}) %collective-permute-start.2) | collective-permute-done | bytes 1056 | tf_op jit(solution)/shard_map/ppermute | solution.py:30
  13.7 0.4 collective-permute-start.7
  14.1 0.7 %pad_add_fusion = s32[1024]{0:T(1024)S(1)} fusion(s32[256]{0:T(256)S(1)} %collective-permute-done.2, s32[256]{0:T(256)S(1)} %collective-permute-done.1, s32[256]{0:T(256)S(1)} %collective-permute-done, s32[256]{0:T(256)} %param.11), kind=kLoop, calls=%fused_computation.62 | loop fusion | flops 3072 | bytes 8192 | tf_op jit(solution)/shard_map/concatenate | solution.py:39
  14.8 0.0 collective-permute-done.5
  14.8 0.0 collective-permute-done.4
  14.8 0.0 collective-permute-done.3
  14.8 0.2 slice_reduce_fusion
  15.0 0.9 %pad_maximum_fusion.4 = bf16[16,6272]{1,0:T(8,128)(2,1)S(1)} fusion(bf16[4,6272]{1,0:T(4,128)(2,1)S(1)} %collective-permute-done.5, bf16[4,6272]{1,0:T(4,128)(2,1)S(1)} %collective-permute-done.4, bf16[4,6272]{1,0:T(4,128)(2,1)S(1)} %collective-permute-done.3, bf16[4,128]{1,0:T(4,128)(2,1)S(1)} %pad.5.clone, bf16[4,2048]{1,0:T(4,128)(2,1)} %param.9, ...), kind=kLoop, calls=%fused_computation.38 | loop fusion | flops 1204224 | bytes 401408 | tf_op jit(solution)/shard_map/concatenate | solution.py:49
  15.9 0.0 copy-start.1
  15.9 0.0 copy-start.2
  15.9 3.4 %reduce-precision_convert_fusion.2 = (bf16[16,32,512]{2,0,1:T(8,128)(2,1)S(1)}, bf16[16,32,512]{2,0,1:T(8,128)(2,1)S(1)}) fusion(bf16[512,4096]{1,0:T(8,128)(2,1)} %param.14, bf16[16,6272]{1,0:T(8,128)(2,1)S(1)} %pad_maximum_fusion.4), kind=kOutput, calls=%fused_computation.20 | convolution fusion | flops 68157440 | bytes 5373952 | tf_op jit(solution)/shard_map/qhd,rhd->qhr/dot_general | solution.py:57
  19.3 0.0 copy-done.1
  19.4 0.1 compare_and_fusion
  19.5 0.2 reshape.200
  19.7 0.1 copy.16
  19.8 0.1 pad_bitcast_fusion
  19.8 0.1 maximum_bitcast_fusion
  19.9 0.0 collective-permute-done.6
  19.9 1.7 %collective-permute-start.8 = (bf16[256,576]{0,1:T(8,128)(2,1)S(1)}, bf16[256,576]{0,1:T(8,128)(2,1)S(1)}, u32[]{:S(2)}, u32[]{:S(2)}) collective-permute-start(bf16[256,576]{0,1:T(8,128)(2,1)S(1)} %collective-permute-done.6), channel_id=1, source_target_pairs={{0,2},{1,3},{2,0},{3,1},{4,6},{5,7},{6,4},{7,5},{8,10},{9,11},{10,... | collective-permute-start | bytes 884744 | tf_op jit(solution)/shard_map/ppermute | solution.py:30
  21.6 0.2 pad_maximum_fusion.1
  21.8 0.3 copy.17
  22.1 0.0 collective-permute-done.7
  22.1 5.7 %collective-permute-done.8 = bf16[256,576]{0,1:T(8,128)(2,1)S(1)} collective-permute-done((bf16[256,576]{0,1:T(8,128)(2,1)S(1)}, bf16[256,576]{0,1:T(8,128)(2,1)S(1)}, u32[]{:S(2)}, u32[]{:S(2)}) %collective-permute-start.8) | collective-permute-done | bytes 294944 | tf_op jit(solution)/shard_map/ppermute | solution.py:30
  27.9 1.8 %fusion.29 = f32[1024,1024]{1,0:T(8,128)S(1)} fusion(bf16[1024,576]{1,0:T(8,128)(2,1)S(1)} %bitcast.83, bf16[1024,576]{0,1:T(8,128)(2,1)S(1)} %constant_dynamic-update-slice_fusion), kind=kOutput, calls=%fused_computation.73 | convolution fusion | flops 1207959552 | bytes 6553600 | tf_op jit(solution)/shard_map/rc,kc->rk/dot_general | solution.py:64
  29.7 0.5 fusion.9
  30.1 0.1 sub.58
  30.2 0.7 %fusion.7 = f32[512]{0:T(512)S(1)} fusion(f32[512,1024]{1,0:T(8,128)S(1)} %get-tuple-element.10, f32[512]{0:T(512)S(1)} %get-tuple-element.9, pred[16,1024]{1,0:T(8,128)(4,1)S(1)} %compare_and_fusion), kind=kLoop, calls=%fused_computation.11 | loop fusion | flops 2096640 | bytes 2117632 | tf_op jit(solution)/shard_map/reduce_sum | solution.py:71
  30.9 0.8 %reduce-precision_convert_fusion = (bf16[1,16,32,1024]{3,2,1,0:T(8,128)(2,1)S(1)}, bf16[1,16,32,1024]{3,2,1,0:T(8,128)(2,1)S(1)}) fusion(f32[1,16,32,1024]{3,2,1,0:T(8,128)S(1)} %bitcast.79, f32[16,32]{1,0:T(8,128)S(1)} %sub.58, pred[16,1024]{1,0:T(8,128)(4,1)S(1)} %compare_and_fusion), kind=kLoop, calls=%fused_computation.9 | loop fusion | flops 3670016 | bytes 4212736 | tf_op jit(solution)/shard_map/convert_element_type | solution.py:18
  31.7 0.2 pad_maximum_fusion
  31.9 1.3 %fusion.18 = f32[1024,512]{1,0:T(8,128)S(1)} fusion(bf16[1024,1024]{1,0:T(8,128)(2,1)S(1)} %bitcast.82, bf16[1024,576]{0,1:T(8,128)(2,1)S(1)} %constant_dynamic-update-slice_fusion), kind=kOutput, calls=%fused_computation.27 | convolution fusion | flops 1073741824 | bytes 5242880 | tf_op jit(solution)/shard_map/dot_general | solution.py:74
  33.2 0.2 slice_add_fusion.1
  33.4 0.2 reduce-precision_convert_fusion.1
  33.6 0.0 copy-start
  33.6 0.1 pad_maximum_fusion.2
  33.7 0.6 %copy.18 = bf16[2,16,32,512]{3,1,0,2:T(8,128)(2,1)S(1)} copy(bf16[2,16,32,512]{3,2,1,0:T(8,128)(2,1)S(1)} %pad_maximum_fusion.2) | data formatting | bytes 2097152 | tf_op jit(solution)/shard_map/stack | solution.py:77
  34.3 1.5 %copy-done = bf16[512,4096]{1,0:T(8,128)(2,1)S(1)} copy-done((bf16[512,4096]{1,0:T(8,128)(2,1)S(1)}, bf16[512,4096]{1,0:T(8,128)(2,1)}, u32[]{:S(2)}) %copy-start) | copy-done | bytes 4194328
  35.8 0.7 %fusion.13 = f32[32,32,128]{2,0,1:T(8,128)S(1)} fusion(bf16[32,32,512]{2,0,1:T(8,128)(2,1)S(1)} %bitcast.81, bf16[512,4096]{1,0:T(8,128)(2,1)S(1)} %copy-done), kind=kOutput, calls=%fused_computation.23 | convolution fusion | flops 134217728 | bytes 5767168 | tf_op jit(solution)/shard_map/qhr,rhv->qhv/dot_general | solution.py:78
  36.6 0.1 reduce_sum.30
  36.6 0.1 concatenate.31
  36.8 3.4 %collective-permute-start.11 = (f32[4,4160]{1,0:T(4,128)S(1)}, f32[4,4160]{1,0:T(4,128)S(1)}, u32[]{:S(2)}, u32[]{:S(2)}) collective-permute-start(f32[4,4160]{1,0:T(4,128)S(1)} %get-tuple-element.18), channel_id=1, source_target_pairs={{0,12},{1,13},{2,14},{3,15},{4,8},{5,9},{6,10},{7,11},{8,4},{9,5},... | collective-permute-start | bytes 199688 | tf_op jit(solution)/shard_map/ppermute | solution.py:30
  40.1 1.1 %collective-permute-start.9 = (f32[4,4160]{1,0:T(4,128)S(1)}, f32[4,4160]{1,0:T(4,128)S(1)}, u32[]{:S(2)}, u32[]{:S(2)}) collective-permute-start(f32[4,4160]{1,0:T(4,128)S(1)} %get-tuple-element.20), channel_id=1, source_target_pairs={{0,4},{1,5},{2,6},{3,7},{4,0},{5,1},{6,2},{7,3},{8,12},{9,13},{10,... | collective-permute-start | bytes 199688 | tf_op jit(solution)/shard_map/ppermute | solution.py:30
  41.2 2.4 %collective-permute-done.11 = f32[4,4160]{1,0:T(4,128)S(1)} collective-permute-done((f32[4,4160]{1,0:T(4,128)S(1)}, f32[4,4160]{1,0:T(4,128)S(1)}, u32[]{:S(2)}, u32[]{:S(2)}) %collective-permute-start.11) | collective-permute-done | bytes 66592 | tf_op jit(solution)/shard_map/ppermute | solution.py:30
  43.6 1.7 %collective-permute-done.10 = f32[4,4160]{1,0:T(4,128)S(1)} collective-permute-done((f32[4,4160]{1,0:T(4,128)S(1)}, f32[4,4160]{1,0:T(4,128)S(1)}, u32[]{:S(2)}, u32[]{:S(2)}) %collective-permute-start.10) | collective-permute-done | bytes 66592 | tf_op jit(solution)/shard_map/ppermute | solution.py:30
  45.3 0.0 collective-permute-done.9
  45.3 0.1 pad_maximum_fusion.3
  45.4 0.1 fusion.25
  45.5 0.1 broadcast_bitcast_fusion
  45.6 0.1 mul.60
  45.7 0.1 mul.61
  45.8 0.1 fusion.20
  45.9 0.7 %fusion.24 = bf16[4,4096]{1,0:T(4,128)(2,1)} fusion(f32[4,4096]{1,0:T(4,128)S(1)} %fusion.20, f32[1,4,32,128]{3,2,1,0:T(8,128)S(1)} %broadcast_bitcast_fusion), kind=kLoop, calls=%fused_computation.45 | loop fusion | flops 32768 | bytes 163840 | tf_op jit(solution)/shard_map/convert_element_type | solution.py:94
  (15 shorter events, 0.3 us)
Async XLA Ops:
  0.0 10.1 %collective-permute-start = (s32[256]{0:T(256)}, s32[256]{0:T(256)S(1)}, u32[]{:S(2)}, u32[]{:S(2)}) collective-permute-start(s32[256]{0:T(256)} %param.11), channel_id=1, source_target_pairs={{0,1},{1,0},{2,3},{3,2},{4,5},{5,4},{6,7},{7,6},{8,9},{9,8},{10,11... | collective-permute-start | bytes 3080 | tf_op jit(solution)/shard_map/ppermute | solution.py:30
  0.5 10.0 %collective-permute-start.1 = (s32[256]{0:T(256)}, s32[256]{0:T(256)S(1)}, u32[]{:S(2)}, u32[]{:S(2)}) collective-permute-start(s32[256]{0:T(256)} %param.11), channel_id=1, source_target_pairs={{0,2},{1,3},{2,0},{3,1},{4,6},{5,7},{6,4},{7,5},{8,10},{9,11},{10,... | collective-permute-start | bytes 3080 | tf_op jit(solution)/shard_map/ppermute | solution.py:30
  4.6 10.2 %collective-permute-start.5 = (bf16[4,6272]{1,0:T(4,128)(2,1)S(1)}, bf16[4,6272]{1,0:T(4,128)(2,1)S(1)}, u32[]{:S(2)}, u32[]{:S(2)}) collective-permute-start(bf16[4,6272]{1,0:T(4,128)(2,1)S(1)} %pad_maximum_fusion.6), channel_id=1, source_target_pairs={{0,12},{1,13},{2,14},{3,15},{4,8},{5,9},{6,10},{7,11},{8,4},{9,5},... | collective-permute-start | bytes 150536 | tf_op jit(solution)/shard_map/ppermute | solution.py:30
  8.2 6.5 %collective-permute-start.4 = (bf16[4,6272]{1,0:T(4,128)(2,1)S(1)}, bf16[4,6272]{1,0:T(4,128)(2,1)S(1)}, u32[]{:S(2)}, u32[]{:S(2)}) collective-permute-start(bf16[4,6272]{1,0:T(4,128)(2,1)S(1)} %pad_maximum_fusion.6), channel_id=1, source_target_pairs={{0,8},{1,9},{2,10},{3,11},{4,12},{5,13},{6,14},{7,15},{8,0},{9,1},... | collective-permute-start | bytes 150536 | tf_op jit(solution)/shard_map/ppermute | solution.py:30
  8.3 6.5 %collective-permute-start.3 = (bf16[4,6272]{1,0:T(4,128)(2,1)S(1)}, bf16[4,6272]{1,0:T(4,128)(2,1)S(1)}, u32[]{:S(2)}, u32[]{:S(2)}) collective-permute-start(bf16[4,6272]{1,0:T(4,128)(2,1)S(1)} %pad_maximum_fusion.6), channel_id=1, source_target_pairs={{0,4},{1,5},{2,6},{3,7},{4,0},{5,1},{6,2},{7,3},{8,12},{9,13},{10,... | collective-permute-start | bytes 150536 | tf_op jit(solution)/shard_map/ppermute | solution.py:30
  10.1 3.6 %collective-permute-start.2 = (s32[256]{0:T(256)S(1)}, s32[256]{0:T(256)S(1)}, u32[]{:S(2)}, u32[]{:S(2)}) collective-permute-start(s32[256]{0:T(256)S(1)} %collective-permute-done), channel_id=1, source_target_pairs={{0,2},{1,3},{2,0},{3,1},{4,6},{5,7},{6,4},{7,5},{8,10},{9,11},{10,... | collective-permute-start | bytes 3080 | tf_op jit(solution)/shard_map/ppermute | solution.py:30
  10.5 9.3 %collective-permute-start.6 = (bf16[256,576]{0,1:T(8,128)(2,1)}, bf16[256,576]{0,1:T(8,128)(2,1)S(1)}, u32[]{:S(2)}, u32[]{:S(2)}) collective-permute-start(bf16[256,576]{0,1:T(8,128)(2,1)} %param.10), channel_id=1, source_target_pairs={{0,1},{1,0},{2,3},{3,2},{4,5},{5,4},{6,7},{7,6},{8,9},{9,8},{10,11... | collective-permute-start | bytes 884744 | tf_op jit(solution)/shard_map/ppermute | solution.py:30
  13.7 8.4 %collective-permute-start.7 = (bf16[256,576]{0,1:T(8,128)(2,1)}, bf16[256,576]{0,1:T(8,128)(2,1)S(1)}, u32[]{:S(2)}, u32[]{:S(2)}) collective-permute-start(bf16[256,576]{0,1:T(8,128)(2,1)} %param.10), channel_id=1, source_target_pairs={{0,2},{1,3},{2,0},{3,1},{4,6},{5,7},{6,4},{7,5},{8,10},{9,11},{10,... | collective-permute-start | bytes 884744 | tf_op jit(solution)/shard_map/ppermute | solution.py:30
  15.9 3.4 %copy-start.1 = (bf16[4,4096]{1,0:T(4,128)(2,1)S(1)}, bf16[4,4096]{1,0:T(4,128)(2,1)}, u32[]{:S(2)}) copy-start(bf16[4,4096]{1,0:T(4,128)(2,1)} %param.8) | copy-start | bytes 98308
  15.9 3.4 %copy-start.2 = (bf16[4,2048]{1,0:T(4,128)(2,1)S(1)}, bf16[4,2048]{1,0:T(4,128)(2,1)}, u32[]{:S(2)}) copy-start(bf16[4,2048]{1,0:T(4,128)(2,1)} %param.9) | copy-start | bytes 49156
  19.9 7.9 %collective-permute-start.8 = (bf16[256,576]{0,1:T(8,128)(2,1)S(1)}, bf16[256,576]{0,1:T(8,128)(2,1)S(1)}, u32[]{:S(2)}, u32[]{:S(2)}) collective-permute-start(bf16[256,576]{0,1:T(8,128)(2,1)S(1)} %collective-permute-done.6), channel_id=1, source_target_pairs={{0,2},{1,3},{2,0},{3,1},{4,6},{5,7},{6,4},{7,5},{8,10},{9,11},{10,... | collective-permute-start | bytes 884744 | tf_op jit(solution)/shard_map/ppermute | solution.py:30
  33.6 2.2 %copy-start = (bf16[512,4096]{1,0:T(8,128)(2,1)S(1)}, bf16[512,4096]{1,0:T(8,128)(2,1)}, u32[]{:S(2)}) copy-start(bf16[512,4096]{1,0:T(8,128)(2,1)} %param.15) | copy-start | bytes 12582916
  36.8 6.9 %collective-permute-start.11 = (f32[4,4160]{1,0:T(4,128)S(1)}, f32[4,4160]{1,0:T(4,128)S(1)}, u32[]{:S(2)}, u32[]{:S(2)}) collective-permute-start(f32[4,4160]{1,0:T(4,128)S(1)} %get-tuple-element.18), channel_id=1, source_target_pairs={{0,12},{1,13},{2,14},{3,15},{4,8},{5,9},{6,10},{7,11},{8,4},{9,5},... | collective-permute-start | bytes 199688 | tf_op jit(solution)/shard_map/ppermute | solution.py:30
  40.1 5.2 %collective-permute-start.10 = (f32[4,4160]{1,0:T(4,128)S(1)}, f32[4,4160]{1,0:T(4,128)S(1)}, u32[]{:S(2)}, u32[]{:S(2)}) collective-permute-start(f32[4,4160]{1,0:T(4,128)S(1)} %get-tuple-element.19), channel_id=1, source_target_pairs={{0,8},{1,9},{2,10},{3,11},{4,12},{5,13},{6,14},{7,15},{8,0},{9,1},... | collective-permute-start | bytes 199688 | tf_op jit(solution)/shard_map/ppermute | solution.py:30
  40.1 5.2 %collective-permute-start.9 = (f32[4,4160]{1,0:T(4,128)S(1)}, f32[4,4160]{1,0:T(4,128)S(1)}, u32[]{:S(2)}, u32[]{:S(2)}) collective-permute-start(f32[4,4160]{1,0:T(4,128)S(1)} %get-tuple-element.20), channel_id=1, source_target_pairs={{0,4},{1,5},{2,6},{3,7},{4,0},{5,1},{6,2},{7,3},{8,12},{9,13},{10,... | collective-permute-start | bytes 199688 | tf_op jit(solution)/shard_map/ppermute | solution.py:30

commit v2 on v1

v2 whole, which is shorter than its diff:
```python
import functools
import math

import jax
import jax.numpy as jnp
from jax import lax
from jax.experimental import pallas as pl
from jax.experimental.pallas import tpu as pltpu
from jax.sharding import PartitionSpec as P

H = 32
DN = 128
DR = 64
DV = 128
R = 512
META = 128
PAIRS = H // 2
HIDDEN = -1e30
FLOOR = -1e29
VMEM = pl.BlockSpec(memory_space=pltpu.VMEM)
SMEM = pl.BlockSpec(memory_space=pltpu.SMEM)
PARAMS = pltpu.CompilerParams(vmem_limit_bytes=24 * 1024 * 1024)


def iota(shape, axis):
    return lax.broadcasted_iota(jnp.int32, shape, axis)


def split(x):
    high = x.astype(jnp.bfloat16).astype(jnp.float32)
    return high, x - high


def diagonal(x):
    wide = jnp.concatenate([x, x], axis=0)
    own, half = x.shape[0], x.shape[1] // 2
    keep = (iota(wide.shape, 0) // own) == (iota(wide.shape, 1) // half)
    return jnp.where(keep, wide, 0.0)


def absorb_kernel(count, *refs):
    queries, w_ref, a_ref, r_ref = refs[:count], refs[count], refs[count + 1], refs[count + 2]
    half = a_ref.shape[1] // 2
    step = 2 * half // PAIRS
    for duo in range(PAIRS // 2):
        found = []
        for pair in (2 * duo, 2 * duo + 1):
            cols = slice(pair * 2 * DN, (pair + 1) * 2 * DN)
            lhs = [diagonal(q[:, cols].astype(jnp.float32)) for q in queries]
            lhs = jnp.concatenate(lhs, axis=0).astype(jnp.bfloat16)
            found.append(
                lax.dot_general(
                    lhs, w_ref[:, cols], (((1,), (1,)), ((), ())), preferred_element_type=jnp.float32
                )
            )
        rows = slice(duo * step, (duo + 1) * step)
        low_rows = slice(half + duo * step, half + (duo + 1) * step)
        small = step // 2
        for g in range(count):
            own = slice(g * small, (g + 1) * small)
            high, low = split(jnp.concatenate([f[own] for f in found], axis=0))
            a_ref[g, rows] = high.astype(jnp.bfloat16)
            a_ref[g, low_rows] = low.astype(jnp.bfloat16)
            turned = []
            for pair in (2 * duo, 2 * duo + 1):
                cols = slice(H * DN + pair * 2 * DR, H * DN + (pair + 1) * 2 * DR)
                turned.append(diagonal(queries[g][:, cols].astype(jnp.float32)))
            r_ref[g, rows] = jnp.concatenate(turned, axis=0).astype(jnp.bfloat16)


def absorb(queries, w_uk):
    count = len(queries)
    rows = queries[0].shape[0] * H
    return pl.pallas_call(
        functools.partial(absorb_kernel, count),
        out_shape=(
            jax.ShapeDtypeStruct((count, 2 * rows, R), jnp.bfloat16),
            jax.ShapeDtypeStruct((count, rows, 2 * DR), jnp.bfloat16),
        ),
        in_specs=[VMEM] * (count + 1),
        out_specs=(VMEM, VMEM),
        compiler_params=PARAMS,
        name="absorb",
    )(*queries, w_uk)


def attend_kernel(near, me_ref, a_ref, r_ref, q_ref, w_ref, *refs):
    keys, docs, out_ref = refs[:near], refs[near : 2 * near], refs[2 * near]
    rows = r_ref.shape[0]
    own = q_ref.shape[0]
    eight = 2 * own
    tokens = keys[0].shape[1]
    scale = 1.0 / math.sqrt(DN + DR)
    meta = q_ref[:, H * (DN + DR) :].astype(jnp.float32)
    meta = jnp.concatenate([meta, meta], axis=0)
    q_doc = meta[:, 0:1]
    q_pos = meta[:, 1:2] * 256.0 + meta[:, 2:3]
    me = me_ref[0]
    scores = []
    for k in range(near):
        latent = keys[k][:R, :]
        rope = keys[k][R:, :]
        both = jnp.dot(a_ref[...], latent, preferred_element_type=jnp.float32)
        turn = jnp.dot(
            r_ref[...], jnp.concatenate([rope, rope], axis=0), preferred_element_type=jnp.float32
        )
        found = (both[:rows] + both[rows:] + turn) * scale
        place = lax.bitwise_xor(me, k) * tokens + iota((eight, tokens), 1)
        visible = (docs[k][...].astype(jnp.float32) == q_doc) & (place.astype(jnp.float32) <= q_pos)
        found = jnp.where(visible[None], found.reshape(rows // eight, eight, tokens), HIDDEN)
        scores.append(found.reshape(rows, tokens))
    best = scores[0]
    for found in scores[1:]:
        best = jnp.maximum(best, found)
    best = jnp.maximum(jnp.max(best, axis=1, keepdims=True), FLOOR)
    total = None
    mixed = None
    for k in range(near):
        weights = jnp.exp(scores[k] - best)
        total = weights if total is None else total + weights
        high, low = split(weights)
        both = jnp.concatenate([high, low], axis=0).astype(jnp.bfloat16)
        part = lax.dot_general(
            both, keys[k][:R, :], (((1,), (1,)), ((), ())), preferred_element_type=jnp.float32
        )
        mixed = part if mixed is None else mixed + part
    total = jnp.sum(total, axis=1, keepdims=True)
    high, low = split(mixed[:rows] + mixed[rows:])
    lane = iota((eight, META), 1)
    stats = jnp.zeros((eight, META), jnp.float32)
    for pair in range(PAIRS):
        take = slice(pair * eight, (pair + 1) * eight)
        cols = slice(pair * 2 * DV, (pair + 1) * 2 * DV)
        lhs = jnp.concatenate([high[take], low[take]], axis=0).astype(jnp.bfloat16)
        res = jnp.dot(lhs, w_ref[:, cols], preferred_element_type=jnp.float32)
        res = res[:eight] + res[eight:]
        out_ref[:, cols] = jnp.concatenate([res[:own, :DV], res[own:, DV:]], axis=1)
        stats = jnp.where(lane == pair, best[take], stats)
        stats = jnp.where(lane == PAIRS + pair, total[take], stats)
    out_ref[:, H * DV : H * DV + META] = stats[:own]
    out_ref[:, H * DV + META :] = stats[own:]


def attend(me, absorbed, turned, query, w_uv, keys, docs):
    near = len(keys)
    return pl.pallas_call(
        functools.partial(attend_kernel, near),
        out_shape=jax.ShapeDtypeStruct((query.shape[0], H * DV + 2 * META), jnp.float32),
        in_specs=[SMEM] + [VMEM] * (4 + 2 * near),
        out_specs=VMEM,
        compiler_params=PARAMS,
        name="attend",
    )(me, absorbed, turned, query, w_uv, *keys, *docs)


def combine_kernel(count, *refs):
    parts, out_ref = refs[:count], refs[count]
    stats = [p[:, H * DV :] for p in parts]
    top = functools.reduce(jnp.maximum, stats)
    factors = [jnp.exp(s - top) for s in stats]
    total = None
    for s, f in zip(stats, factors):
        ends = [
            f[:, half * META : half * META + PAIRS]
            * s[:, half * META + PAIRS : half * META + 2 * PAIRS]
            for half in range(2)
        ]
        ends = jnp.concatenate(ends, axis=1)
        total = ends if total is None else total + ends
    for head in range(H):
        pair, half = head // 2, head % 2
        cols = slice(head * DV, (head + 1) * DV)
        lane = half * META + pair
        acc = None
        for p, f in zip(parts, factors):
            term = p[:, cols] * f[:, lane : lane + 1]
            acc = term if acc is None else acc + term
        lane = half * PAIRS + pair
        out_ref[:, cols] = (acc / total[:, lane : lane + 1]).astype(out_ref.dtype)


def combine(parts):
    return pl.pallas_call(
        functools.partial(combine_kernel, len(parts)),
        out_shape=jax.ShapeDtypeStruct((parts[0].shape[0], H * DV), jnp.bfloat16),
        in_specs=[VMEM] * len(parts),
        out_specs=VMEM,
        compiler_params=PARAMS,
        name="combine",
    )(*parts)


def shards(size, query_nope, query_rope, cache, key_docs, query_docs, query_pos, w_uk, w_uv):
    near = math.gcd(size, 4)
    far = size // near
    me = lax.axis_index("col")

    def swap(x, mask):
        return lax.ppermute(x, "col", [(i, i ^ mask) for i in range(size)])

    def gather(block):
        found = {0: block}
        if near == 4:
            found[2] = swap(block, 2)
        if near > 1:
            found[1] = swap(block, 1)
        if near == 4:
            found[3] = swap(found[2], 1)
        return [found[k] for k in range(near)]

    keys = gather(cache.T)
    docs = gather(key_docs.reshape(1, -1))

    meta = jnp.stack(
        [query_docs, lax.shift_right_logical(query_pos, 8), lax.bitwise_and(query_pos, 255)], axis=1
    ).astype(jnp.bfloat16)
    meta = jnp.pad(meta, ((0, 0), (0, META - 3)))
    mine = jnp.concatenate([query_nope, query_rope, meta], axis=1)
    groups = [mine] + [swap(mine, near * k) for k in range(1, far)]
    where = jnp.reshape(me, (1,)).astype(jnp.int32)
    parts = [None] * far
    for start in range(0, far, 4):
        some = groups[start : start + 4]
        absorbed, turned = absorb(some, w_uk)
        for g, query in enumerate(some):
            k = start + g
            part = attend(where, absorbed[g], turned[g], query, w_uv, keys, docs)
            parts[k] = part if k == 0 else swap(part, near * k)
    return combine(parts)


def solution(mesh):
    split_rows = P(("ga", "col"), None)
    split_flat = P(("ga", "col"))
    placed = (split_rows, split_rows, split_rows, split_flat, split_flat, split_flat, P(), P())
    size = mesh.shape["col"]

    def body(*arrays):
        return shards(size, *arrays)

    return jax.shard_map(body, mesh=mesh, in_specs=placed, out_specs=split_rows, check_vma=False)
```

time: 46.9 us -> 34.4 us (0.73)
  Pallas kernels: 0 us -> 8.71 us
  matrix products: 7.23 us -> 0 us
  waiting for transfers between devices: 12.9 us -> 7.7 us
  other arithmetic: 7.25 us -> 2.2 us
  local copies, waits for them, and re-layouts: 4.4 us -> 2.61 us
  starting transfers between devices: 14.5 us -> 12.8 us
    pallas_call x0 -> x6, Pallas kernels: none -> 8.71 us  [the longest x4 6.43 us: attend(): pl.pallas_call(functools.partial(attend_kernel, near), out_shape=jax.Shap...]
    dot_general x4 -> x0, matrix products: 7.23 us -> none  [the longest x1 3.4 us: shards(): jnp.einsum('qhd,rhd->qhr', q_nope, w_uk.reshape(R, H, DN), preferred_elem...]
    ppermute x12, waiting for transfers between devices: 12.9 us -> 7.7 us  [swap(): return lax.ppermute(x, 'col', [(i, i ^ mask) for i in range(size)])]
    ppermute x12, starting transfers between devices: 14.5 us -> 12.8 us  [swap(): return lax.ppermute(x, 'col', [(i, i ^ mask) for i in range(size)])]
    convert_element_type x4 -> x0, other arithmetic: 1.68 us -> none  [the longest x2 0.98 us: split(): return (high.astype(jnp.bfloat16), (x - high).astype(jnp.bfloat16))]
    concatenate x3 -> x0, other arithmetic: 1.6 us -> none  [the longest x1 0.91 us: shards(): query = jnp.concatenate(groups, axis=0)]
    reduce_sum x3 -> x0, other arithmetic: 0.84 us -> none  [the longest x1 0.67 us: shards(): total = jnp.sum(weights, axis=2)]
    another operation x2 -> x3, other arithmetic: 0.69 us -> 1.4 us  [shards(): jnp.stack([query_docs, lax.shift_right_logical(query_pos, 8), lax.bitwise...]
  transfers between devices with their start and end apart: 12 -> 12, of which waited for: 4 -> 5; matrix products, arithmetic and copies ran while one was open for 19% -> 8% of each run, Pallas kernels for 0% -> 18%
where the time goes in v2:
time: 34.4 us; the launch traced here: 34.1 us
  starting transfers between devices  12.8 us (37%)
  Pallas kernels  8.71 us (25%)
  waiting for transfers between devices  7.7 us (22%)
  local copies, waits for them, and re-layouts  2.61 us (8%)
  other arithmetic  2.2 us (6%)
    ppermute x12, starting transfers between devices, swap(): return lax.ppermute(x, 'col', [(i, i ^ mask) for i in range(size)])  12.8 us
    ppermute x12, waiting for transfers between devices, swap(): return lax.ppermute(x, 'col', [(i, i ^ mask) for i in range(size)])  7.7 us
    pallas_call x4, Pallas kernels, attend(): pl.pallas_call(functools.partial(attend_kernel, near), out_shape=jax.Shap...  6.43 us
    unnamed x8, local copies, waits for them, and re-layouts  2.2 us
    another operation x3, other arithmetic, shards(): jnp.stack([query_docs, lax.shift_right_logical(query_pos, 8), lax.bitwise...  1.4 us
    pallas_call x1, Pallas kernels, absorb(): pl.pallas_call(functools.partial(absorb_kernel, count), out_shape=(jax.Sh...  1.39 us
    pallas_call x1, Pallas kernels, combine(): pl.pallas_call(functools.partial(combine_kernel, len(parts)), out_shape=j...  0.89 us
    concatenate x1, other arithmetic, shards(): mine = jnp.concatenate([query_nope, query_rope, meta], axis=1)  0.8 us
  transfers between devices with their start and end apart: 12, of which 5 were waited for; matrix products, arithmetic and copies ran while one was open for 8% of the time, Pallas kernels for 18%

profile of v2, /device:TPU:0, one launch (start us, length us, event | category | flops | bytes accessed | tf_op | source)
XLA Modules:
  0.0 34.1 jit_solution(7040861539419494909)
XLA Ops:
  0.0 0.0 copy-start.1
  0.0 3.0 %collective-permute-start.4 = (bf16[576,256]{1,0:T(8,128)(2,1)}, bf16[576,256]{1,0:T(8,128)(2,1)S(1)}, u32[]{:S(2)}, u32[]{:S(2)}) collective-permute-start(bf16[576,256]{1,0:T(8,128)(2,1)} %bitcast.25), channel_id=1, source_target_pairs={{0,2},{1,3},{2,0},{3,1},{4,6},{5,7},{6,4},{7,5},{8,10},{9,11},{10,... | collective-permute-start | bytes 884744 | tf_op jit(solution)/shard_map/ppermute | solution.py:199
  3.0 0.7 %convert_bitcast_fusion.1 = (bf16[4,1]{0,1:T(2,128)(2,1)S(1)}, bf16[4,1]{0,1:T(2,128)(2,1)S(1)}) fusion(s32[4]{0:T(128)} %param.13), kind=kLoop, calls=%fused_computation.16 | loop fusion | flops 16 | bytes 32 | tf_op jit(solution)/shard_map/stack | solution.py:214
  3.6 0.1 copy.10
  3.7 0.1 copy.11
  3.8 0.7 %convert_bitcast_fusion.2 = bf16[4,1]{0,1:T(2,128)(2,1)S(1)} fusion(s32[4]{0:T(128)} %param.12), kind=kLoop, calls=%fused_computation.17 | loop fusion | flops 4 | bytes 24 | tf_op jit(solution)/shard_map/stack | solution.py:214
  4.5 0.1 copy.9
  4.6 0.1 fusion.4
  4.7 0.8 %pad_maximum_fusion.refs_0_.q_ref = bf16[4,6272]{1,0:T(4,128)(2,1)S(1)} fusion(bf16[4,128]{1,0:T(4,128)(2,1)S(1)} %fusion.4, bf16[4,2048]{1,0:T(4,128)(2,1)} %param.9, bf16[4,4096]{1,0:T(4,128)(2,1)} %param.8), kind=kLoop, calls=%fused_computation.4 | loop fusion | flops 150528 | bytes 100352 | tf_op jit(solution)/shard_map/concatenate | solution.py:218
  5.5 1.6 %collective-permute-start = (bf16[4,6272]{1,0:T(4,128)(2,1)S(1)}, bf16[4,6272]{1,0:T(4,128)(2,1)S(1)}, u32[]{:S(2)}, u32[]{:S(2)}) collective-permute-start(bf16[4,6272]{1,0:T(4,128)(2,1)S(1)} %pad_maximum_fusion.refs_0_.q_ref), channel_id=1, source_target_pairs={{0,4},{1,5},{2,6},{3,7},{4,0},{5,1},{6,2},{7,3},{8,12},{9,13},{10,... | collective-permute-start | bytes 150536 | tf_op jit(solution)/shard_map/ppermute | solution.py:199
  7.1 2.6 %collective-permute-start.1 = (bf16[4,6272]{1,0:T(4,128)(2,1)S(1)}, bf16[4,6272]{1,0:T(4,128)(2,1)S(1)}, u32[]{:S(2)}, u32[]{:S(2)}) collective-permute-start(bf16[4,6272]{1,0:T(4,128)(2,1)S(1)} %pad_maximum_fusion.refs_0_.q_ref), channel_id=1, source_target_pairs={{0,8},{1,9},{2,10},{3,11},{4,12},{5,13},{6,14},{7,15},{8,0},{9,1},... | collective-permute-start | bytes 150536 | tf_op jit(solution)/shard_map/ppermute | solution.py:199
  9.7 0.2 collective-permute-start.2
  9.9 0.3 collective-permute-start.7
  10.3 0.0 copy-start
  10.3 3.5 %collective-permute-done.7.refs_6_ = s32[1,256]{1,0:T(1,128)S(1)} collective-permute-done((s32[1,256]{1,0:T(1,128)}, s32[1,256]{1,0:T(1,128)S(1)}, u32[]{:S(2)}, u32[]{:S(2)}) %collective-permute-start.7) | collective-permute-done | bytes 1056 | tf_op jit(solution)/shard_map/ppermute | solution.py:199
  13.7 0.0 collective-permute-start.3
  13.7 0.0 collective-permute-done.refs_1_.q_ref
  13.7 0.5 %collective-permute-start.6 = (s32[1,256]{1,0:T(1,128)}, s32[1,256]{1,0:T(1,128)S(1)}, u32[]{:S(2)}, u32[]{:S(2)}) collective-permute-start(s32[1,256]{1,0:T(1,128)} %bitcast.32), channel_id=1, source_target_pairs={{0,1},{1,0},{2,3},{3,2},{4,5},{5,4},{6,7},{7,6},{8,9},{9,8},{10,11... | collective-permute-start | bytes 3080 | tf_op jit(solution)/shard_map/ppermute | solution.py:199
  14.2 0.0 collective-permute-done.1.refs_2_.q_ref
  14.3 0.1 collective-permute-start.8
  14.3 1.3 %collective-permute-done.2.refs_3_.q_ref = bf16[4,6272]{1,0:T(4,128)(2,1)S(1)} collective-permute-done((bf16[4,6272]{1,0:T(4,128)(2,1)S(1)}, bf16[4,6272]{1,0:T(4,128)(2,1)S(1)}, u32[]{:S(2)}, u32[]{:S(2)}) %collective-permute-start.2) | collective-permute-done | bytes 50208 | tf_op jit(solution)/shard_map/ppermute | solution.py:199
  15.6 0.0 copy-start.2
  15.6 2.2 %copy-done.2 = bf16[512,4096]{1,0:T(8,128)(2,1)S(1)} copy-done((bf16[512,4096]{1,0:T(8,128)(2,1)S(1)}, bf16[512,4096]{1,0:T(8,128)(2,1)}, u32[]{:S(2)}) %copy-start.2) | copy-done | bytes 4194328
  17.8 0.0 copy-start.3
  17.8 1.4 %absorb.1 = (bf16[4,256,512]{2,1,0:T(8,128)(2,1)S(1)}, bf16[4,128,128]{2,1,0:T(8,128)(2,1)S(1)}) custom-call(bf16[4,6272]{1,0:T(4,128)(2,1)S(1)} %pad_maximum_fusion.refs_0_.q_ref, bf16[4,6272]{1,0:T(4,128)(2,1)S(1)} %collective-permute-done.refs_1_.q_ref, bf16[4,6272]{1,0:T(4,128)(2,1)S(1)} %collective-permute-done.1.refs_2_.q_ref, ...), custom_call_target="tpu_custom_call" | custom-call | tf_op jit(solution)/shard_map/absorb/pallas_call | solution.py:74
  19.2 0.0 collective-permute-done.4.refs_2_
  19.2 0.1 collective-permute-start.5
  19.3 0.1 slice_bitcast_fusion
  19.4 0.0 collective-permute-done.6.refs_5_
  19.4 0.0 collective-permute-done.8.refs_7_
  19.4 0.0 collective-permute-done.3.refs_1_
  19.4 1.4 %collective-permute-done.5.refs_3_ = bf16[576,256]{1,0:T(8,128)(2,1)S(1)} collective-permute-done((bf16[576,256]{1,0:T(8,128)(2,1)S(1)}, bf16[576,256]{1,0:T(8,128)(2,1)S(1)}, u32[]{:S(2)}, u32[]{:S(2)}) %collective-permute-start.5) | collective-permute-done | bytes 294944 | tf_op jit(solution)/shard_map/ppermute | solution.py:199
  20.9 0.0 copy-done.1
  20.9 0.0 copy-done
  20.9 0.0 copy-done.3
  20.9 1.6 %attend.7 = f32[4,4352]{1,0:T(4,128)S(1)} custom-call(s32[1]{0:T(128)} %bitcast.me_ref, bf16[256,512]{1,0:T(8,128)(2,1)S(1)} %get-tuple-element.9.a_ref, bf16[128,128]{1,0:T(8,128)(2,1)S(1)} %get-tuple-element.13.r_ref, bf16[4,6272]{1,0:T(4,128)(2,1)S(1)} %collective-permute-done.2.refs_3_.q_ref, bf16[512,4096]{1,0:T(8,128)(2,1)S(1)} %copy-done, ...), custom_call_target="tpu_custom_call" | custom-call | tf_op jit(solution)/shard_map/attend/pallas_call | solution.py:146
  22.5 2.4 %collective-permute-start.11 = (f32[4,4352]{1,0:T(4,128)S(1)}, f32[4,4352]{1,0:T(4,128)S(1)}, u32[]{:S(2)}, u32[]{:S(2)}) collective-permute-start(f32[4,4352]{1,0:T(4,128)S(1)} %attend.7), channel_id=1, source_target_pairs={{0,12},{1,13},{2,14},{3,15},{4,8},{5,9},{6,10},{7,11},{8,4},{9,5},... | collective-permute-start | bytes 208904 | tf_op jit(solution)/shard_map/ppermute | solution.py:199
  24.9 1.6 %attend.6 = f32[4,4352]{1,0:T(4,128)S(1)} custom-call(s32[1]{0:T(128)} %bitcast.me_ref, bf16[256,512]{1,0:T(8,128)(2,1)S(1)} %get-tuple-element.10.a_ref, bf16[128,128]{1,0:T(8,128)(2,1)S(1)} %get-tuple-element.14.r_ref, bf16[4,6272]{1,0:T(4,128)(2,1)S(1)} %collective-permute-done.1.refs_2_.q_ref, bf16[512,4096]{1,0:T(8,128)(2,1)S(1)} %copy-done, ...), custom_call_target="tpu_custom_call" | custom-call | tf_op jit(solution)/shard_map/attend/pallas_call | solution.py:146
  26.5 0.0 collective-permute-start.10
  26.5 1.6 %attend.5 = f32[4,4352]{1,0:T(4,128)S(1)} custom-call(s32[1]{0:T(128)} %bitcast.me_ref, bf16[256,512]{1,0:T(8,128)(2,1)S(1)} %get-tuple-element.11.a_ref, bf16[128,128]{1,0:T(8,128)(2,1)S(1)} %get-tuple-element.15.r_ref, bf16[4,6272]{1,0:T(4,128)(2,1)S(1)} %collective-permute-done.refs_1_.q_ref, bf16[512,4096]{1,0:T(8,128)(2,1)S(1)} %copy-done, ...), custom_call_target="tpu_custom_call" | custom-call | tf_op jit(solution)/shard_map/attend/pallas_call | solution.py:146
  28.1 2.0 %collective-permute-start.9 = (f32[4,4352]{1,0:T(4,128)S(1)}, f32[4,4352]{1,0:T(4,128)S(1)}, u32[]{:S(2)}, u32[]{:S(2)}) collective-permute-start(f32[4,4352]{1,0:T(4,128)S(1)} %attend.5), channel_id=1, source_target_pairs={{0,4},{1,5},{2,6},{3,7},{4,0},{5,1},{6,2},{7,3},{8,12},{9,13},{10,... | collective-permute-start | bytes 208904 | tf_op jit(solution)/shard_map/ppermute | solution.py:199
  30.1 1.6 %attend.4.refs_0_ = f32[4,4352]{1,0:T(4,128)S(1)} custom-call(s32[1]{0:T(128)} %bitcast.me_ref, bf16[256,512]{1,0:T(8,128)(2,1)S(1)} %get-tuple-element.12.a_ref, bf16[128,128]{1,0:T(8,128)(2,1)S(1)} %get-tuple-element.16.r_ref, bf16[4,6272]{1,0:T(4,128)(2,1)S(1)} %pad_maximum_fusion.refs_0_.q_ref, bf16[512,4096]{1,0:T(8,128)(2,1)S(1)} %copy-done, ...), custom_call_target="tpu_custom_call" | custom-call | tf_op jit(solution)/shard_map/attend/pallas_call | solution.py:146
  31.8 0.0 collective-permute-done.11.refs_3_
  31.8 0.1 collective-permute-done.10.refs_2_
  31.8 1.4 %collective-permute-done.9.refs_1_ = f32[4,4352]{1,0:T(4,128)S(1)} collective-permute-done((f32[4,4352]{1,0:T(4,128)S(1)}, f32[4,4352]{1,0:T(4,128)S(1)}, u32[]{:S(2)}, u32[]{:S(2)}) %collective-permute-start.9) | collective-permute-done | bytes 69664 | tf_op jit(solution)/shard_map/ppermute | solution.py:199
  33.2 0.9 %combine.1 = bf16[4,4096]{1,0:T(4,128)(2,1)} custom-call(f32[4,4352]{1,0:T(4,128)S(1)} %attend.4.refs_0_, f32[4,4352]{1,0:T(4,128)S(1)} %collective-permute-done.9.refs_1_, f32[4,4352]{1,0:T(4,128)S(1)} %collective-permute-done.10.refs_2_, f32[4,4352]{1,0:T(4,128)S(1)} %collective-permute-done.11.refs_3_), custom_call_target="tpu_custom_call" | custom-call | tf_op jit(solution)/shard_map/combine/pallas_call | solution.py:183
  (1 shorter events, 0.0 us)
Async XLA Ops:
  0.0 20.9 %copy-start.1 = (bf16[256,576]{0,1:T(8,128)(2,1)S(1)}, bf16[256,576]{0,1:T(8,128)(2,1)}, u32[]{:S(2)}) copy-start(bf16[256,576]{0,1:T(8,128)(2,1)} %param.10) | copy-start | bytes 884740
  0.0 19.2 %collective-permute-start.4 = (bf16[576,256]{1,0:T(8,128)(2,1)}, bf16[576,256]{1,0:T(8,128)(2,1)S(1)}, u32[]{:S(2)}, u32[]{:S(2)}) collective-permute-start(bf16[576,256]{1,0:T(8,128)(2,1)} %bitcast.25), channel_id=1, source_target_pairs={{0,2},{1,3},{2,0},{3,1},{4,6},{5,7},{6,4},{7,5},{8,10},{9,11},{10,... | collective-permute-start | bytes 884744 | tf_op jit(solution)/shard_map/ppermute | solution.py:199
  5.5 8.2 %collective-permute-start = (bf16[4,6272]{1,0:T(4,128)(2,1)S(1)}, bf16[4,6272]{1,0:T(4,128)(2,1)S(1)}, u32[]{:S(2)}, u32[]{:S(2)}) collective-permute-start(bf16[4,6272]{1,0:T(4,128)(2,1)S(1)} %pad_maximum_fusion.refs_0_.q_ref), channel_id=1, source_target_pairs={{0,4},{1,5},{2,6},{3,7},{4,0},{5,1},{6,2},{7,3},{8,12},{9,13},{10,... | collective-permute-start | bytes 150536 | tf_op jit(solution)/shard_map/ppermute | solution.py:199
  7.1 7.1 %collective-permute-start.1 = (bf16[4,6272]{1,0:T(4,128)(2,1)S(1)}, bf16[4,6272]{1,0:T(4,128)(2,1)S(1)}, u32[]{:S(2)}, u32[]{:S(2)}) collective-permute-start(bf16[4,6272]{1,0:T(4,128)(2,1)S(1)} %pad_maximum_fusion.refs_0_.q_ref), channel_id=1, source_target_pairs={{0,8},{1,9},{2,10},{3,11},{4,12},{5,13},{6,14},{7,15},{8,0},{9,1},... | collective-permute-start | bytes 150536 | tf_op jit(solution)/shard_map/ppermute | solution.py:199
  9.7 5.9 %collective-permute-start.2 = (bf16[4,6272]{1,0:T(4,128)(2,1)S(1)}, bf16[4,6272]{1,0:T(4,128)(2,1)S(1)}, u32[]{:S(2)}, u32[]{:S(2)}) collective-permute-start(bf16[4,6272]{1,0:T(4,128)(2,1)S(1)} %pad_maximum_fusion.refs_0_.q_ref), channel_id=1, source_target_pairs={{0,12},{1,13},{2,14},{3,15},{4,8},{5,9},{6,10},{7,11},{8,4},{9,5},... | collective-permute-start | bytes 150536 | tf_op jit(solution)/shard_map/ppermute | solution.py:199
  9.9 3.8 %collective-permute-start.7 = (s32[1,256]{1,0:T(1,128)}, s32[1,256]{1,0:T(1,128)S(1)}, u32[]{:S(2)}, u32[]{:S(2)}) collective-permute-start(s32[1,256]{1,0:T(1,128)} %bitcast.31), channel_id=1, source_target_pairs={{0,2},{1,3},{2,0},{3,1},{4,6},{5,7},{6,4},{7,5},{8,10},{9,11},{10,... | collective-permute-start | bytes 3080 | tf_op jit(solution)/shard_map/ppermute | solution.py:199
  10.3 10.6 %copy-start = (bf16[512,4096]{1,0:T(8,128)(2,1)S(1)}, bf16[512,4096]{1,0:T(8,128)(2,1)}, u32[]{:S(2)}) copy-start(bf16[512,4096]{1,0:T(8,128)(2,1)} %w_ref.7) | copy-start | bytes 12582916
  13.7 5.7 %collective-permute-start.3 = (bf16[576,256]{1,0:T(8,128)(2,1)}, bf16[576,256]{1,0:T(8,128)(2,1)S(1)}, u32[]{:S(2)}, u32[]{:S(2)}) collective-permute-start(bf16[576,256]{1,0:T(8,128)(2,1)} %bitcast.26), channel_id=1, source_target_pairs={{0,1},{1,0},{2,3},{3,2},{4,5},{5,4},{6,7},{7,6},{8,9},{9,8},{10,11... | collective-permute-start | bytes 884744 | tf_op jit(solution)/shard_map/ppermute | solution.py:199
  13.7 5.7 %collective-permute-start.6 = (s32[1,256]{1,0:T(1,128)}, s32[1,256]{1,0:T(1,128)S(1)}, u32[]{:S(2)}, u32[]{:S(2)}) collective-permute-start(s32[1,256]{1,0:T(1,128)} %bitcast.32), channel_id=1, source_target_pairs={{0,1},{1,0},{2,3},{3,2},{4,5},{5,4},{6,7},{7,6},{8,9},{9,8},{10,11... | collective-permute-start | bytes 3080 | tf_op jit(solution)/shard_map/ppermute | solution.py:199
  14.3 5.2 %collective-permute-start.8 = (s32[1,256]{1,0:T(1,128)S(1)}, s32[1,256]{1,0:T(1,128)S(1)}, u32[]{:S(2)}, u32[]{:S(2)}) collective-permute-start(s32[1,256]{1,0:T(1,128)S(1)} %collective-permute-done.7.refs_6_), channel_id=1, source_target_pairs={{0,1},{1,0},{2,3},{3,2},{4,5},{5,4},{6,7},{7,6},{8,9},{9,8},{10,11... | collective-permute-start | bytes 3080 | tf_op jit(solution)/shard_map/ppermute | solution.py:199
  15.6 2.2 %copy-start.2 = (bf16[512,4096]{1,0:T(8,128)(2,1)S(1)}, bf16[512,4096]{1,0:T(8,128)(2,1)}, u32[]{:S(2)}) copy-start(bf16[512,4096]{1,0:T(8,128)(2,1)} %refs_4_.1) | copy-start | bytes 12582916
  17.8 3.1 %copy-start.3 = (s32[256]{0:T(256)S(1)}, s32[256]{0:T(256)}, u32[]{:S(2)}) copy-start(s32[256]{0:T(256)} %param.11) | copy-start | bytes 3076
  19.2 1.6 %collective-permute-start.5 = (bf16[576,256]{1,0:T(8,128)(2,1)S(1)}, bf16[576,256]{1,0:T(8,128)(2,1)S(1)}, u32[]{:S(2)}, u32[]{:S(2)}) collective-permute-start(bf16[576,256]{1,0:T(8,128)(2,1)S(1)} %collective-permute-done.4.refs_2_), channel_id=1, source_target_pairs={{0,1},{1,0},{2,3},{3,2},{4,5},{5,4},{6,7},{7,6},{8,9},{9,8},{10,11... | collective-permute-start | bytes 884744 | tf_op jit(solution)/shard_map/ppermute | solution.py:199
  22.5 9.3 %collective-permute-start.11 = (f32[4,4352]{1,0:T(4,128)S(1)}, f32[4,4352]{1,0:T(4,128)S(1)}, u32[]{:S(2)}, u32[]{:S(2)}) collective-permute-start(f32[4,4352]{1,0:T(4,128)S(1)} %attend.7), channel_id=1, source_target_pairs={{0,12},{1,13},{2,14},{3,15},{4,8},{5,9},{6,10},{7,11},{8,4},{9,5},... | collective-permute-start | bytes 208904 | tf_op jit(solution)/shard_map/ppermute | solution.py:199
  26.5 5.4 %collective-permute-start.10 = (f32[4,4352]{1,0:T(4,128)S(1)}, f32[4,4352]{1,0:T(4,128)S(1)}, u32[]{:S(2)}, u32[]{:S(2)}) collective-permute-start(f32[4,4352]{1,0:T(4,128)S(1)} %attend.6), channel_id=1, source_target_pairs={{0,8},{1,9},{2,10},{3,11},{4,12},{5,13},{6,14},{7,15},{8,0},{9,1},... | collective-permute-start | bytes 208904 | tf_op jit(solution)/shard_map/ppermute | solution.py:199
  28.1 5.1 %collective-permute-start.9 = (f32[4,4352]{1,0:T(4,128)S(1)}, f32[4,4352]{1,0:T(4,128)S(1)}, u32[]{:S(2)}, u32[]{:S(2)}) collective-permute-start(f32[4,4352]{1,0:T(4,128)S(1)} %attend.5), channel_id=1, source_target_pairs={{0,4},{1,5},{2,6},{3,7},{4,0},{5,1},{6,2},{7,3},{8,12},{9,13},{10,... | collective-permute-start | bytes 208904 | tf_op jit(solution)/shard_map/ppermute | solution.py:199

commit v3 on v2

--- a/solution.py
+++ b/solution.py
@@ -7,6 +7,7 @@
 from jax.experimental import pallas as pl
 from jax.experimental.pallas import tpu as pltpu
 from jax.sharding import PartitionSpec as P
+
 
 H = 32
 DN = 128
@@ -38,8 +39,23 @@
     return jnp.where(keep, wide, 0.0)
 
 
+def touch_kernel(w_ref, out_ref):
+    out_ref[...] = jnp.zeros_like(out_ref)
+
+
+def touch(weights):
+    return pl.pallas_call(
+        touch_kernel,
+        out_shape=jax.ShapeDtypeStruct((8, META), jnp.float32),
+        in_specs=[VMEM],
+        out_specs=VMEM,
+        compiler_params=PARAMS,
+        name="touch",
+    )(weights)
+
+
 def absorb_kernel(count, *refs):
-    queries, w_ref, a_ref, r_ref = refs[:count], refs[count], refs[count + 1], refs[count + 2]
+    queries, (w_ref, _, a_ref, r_ref) = refs[:count], refs[count:]
     half = a_ref.shape[1] // 2
     step = 2 * half // PAIRS
     for duo in range(PAIRS // 2):
@@ -68,7 +84,7 @@
             r_ref[g, rows] = jnp.concatenate(turned, axis=0).astype(jnp.bfloat16)
 
 
-def absorb(queries, w_uk):
+def absorb(queries, w_uk, touched):
     count = len(queries)
     rows = queries[0].shape[0] * H
     return pl.pallas_call(
@@ -77,24 +93,25 @@
             jax.ShapeDtypeStruct((count, 2 * rows, R), jnp.bfloat16),
             jax.ShapeDtypeStruct((count, rows, 2 * DR), jnp.bfloat16),
         ),
-        in_specs=[VMEM] * (count + 1),
+        in_specs=[VMEM] * (count + 2),
         out_specs=(VMEM, VMEM),
         compiler_params=PARAMS,
         name="absorb",
-    )(*queries, w_uk)
+    )(*queries, w_uk, touched)
 
 
 def attend_kernel(near, me_ref, a_ref, r_ref, q_ref, w_ref, *refs):
-    keys, docs, out_ref = refs[:near], refs[near : 2 * near], refs[2 * near]
+    keys, docs, out_ref = refs[:near], refs[near:-1], refs[-1]
     rows = r_ref.shape[0]
     own = q_ref.shape[0]
     eight = 2 * own
     tokens = keys[0].shape[1]
     scale = 1.0 / math.sqrt(DN + DR)
     meta = q_ref[:, H * (DN + DR) :].astype(jnp.float32)
-    meta = jnp.concatenate([meta, meta], axis=0)
-    q_doc = meta[:, 0:1]
-    q_pos = meta[:, 1:2] * 256.0 + meta[:, 2:3]
+    pick = (iota((eight, META), 0) % own) == iota((eight, META), 1)
+    meta = [jnp.sum(jnp.where(pick, meta[i : i + 1], 0.0), axis=1, keepdims=True) for i in range(3)]
+    q_doc = meta[0]
+    q_pos = meta[1] * 256.0 + meta[2]
     me = me_ref[0]
     scores = []
     for k in range(near):
@@ -106,7 +123,8 @@
         )
         found = (both[:rows] + both[rows:] + turn) * scale
         place = lax.bitwise_xor(me, k) * tokens + iota((eight, tokens), 1)
-        visible = (docs[k][...].astype(jnp.float32) == q_doc) & (place.astype(jnp.float32) <= q_pos)
+        doc = docs[k // 2][:, (k % 2) * tokens : (k % 2 + 1) * tokens]
+        visible = (doc.astype(jnp.float32) == q_doc) & (place.astype(jnp.float32) <= q_pos)
         found = jnp.where(visible[None], found.reshape(rows // eight, eight, tokens), HIDDEN)
         scores.append(found.reshape(rows, tokens))
     best = scores[0]
@@ -146,7 +164,7 @@
     return pl.pallas_call(
         functools.partial(attend_kernel, near),
         out_shape=jax.ShapeDtypeStruct((query.shape[0], H * DV + 2 * META), jnp.float32),
-        in_specs=[SMEM] + [VMEM] * (4 + 2 * near),
+        in_specs=[SMEM] + [VMEM] * (4 + near + len(docs)),
         out_specs=VMEM,
         compiler_params=PARAMS,
         name="attend",
@@ -198,30 +216,30 @@
     def swap(x, mask):
         return lax.ppermute(x, "col", [(i, i ^ mask) for i in range(size)])
 
-    def gather(block):
-        found = {0: block}
-        if near == 4:
-            found[2] = swap(block, 2)
-        if near > 1:
-            found[1] = swap(block, 1)
-        if near == 4:
-            found[3] = swap(found[2], 1)
-        return [found[k] for k in range(near)]
-
-    keys = gather(cache.T)
-    docs = gather(key_docs.reshape(1, -1))
-
-    meta = jnp.stack(
-        [query_docs, lax.shift_right_logical(query_pos, 8), lax.bitwise_and(query_pos, 255)], axis=1
-    ).astype(jnp.bfloat16)
-    meta = jnp.pad(meta, ((0, 0), (0, META - 3)))
-    mine = jnp.concatenate([query_nope, query_rope, meta], axis=1)
-    groups = [mine] + [swap(mine, near * k) for k in range(1, far)]
+    block, doc = cache.T, key_docs.reshape(1, -1)
+    keys, docs = {0: block}, [doc]
+    if near == 4:
+        keys[2] = swap(block, 2)
+    if near > 1:
+        keys[1] = swap(block, 1)
+        docs = [jnp.concatenate([doc, swap(doc, 1)], axis=1)]
+    own_rows = query_nope.shape[0]
+    meta = [query_docs, lax.shift_right_logical(query_pos, 8), lax.bitwise_and(query_pos, 255)]
+    meta = jnp.pad(jnp.stack(meta), ((0, own_rows - 3), (0, META - own_rows)))
+    mine = jnp.concatenate([query_nope, query_rope, meta.astype(query_nope.dtype)], axis=1)
+    touched = touch(w_uk)
+    groups = [mine]
+    for k in range(1, far):
+        groups.append(swap(mine, near * k))
+    if near == 4:
+        docs.append(swap(docs[0], 2))
+        keys[3] = swap(keys[2], 1)
+    keys = [keys[k] for k in range(near)]
     where = jnp.reshape(me, (1,)).astype(jnp.int32)
     parts = [None] * far
     for start in range(0, far, 4):
         some = groups[start : start + 4]
-        absorbed, turned = absorb(some, w_uk)
+        absorbed, turned = absorb(some, w_uk, touched)
         for g, query in enumerate(some):
             k = start + g
             part = attend(where, absorbed[g], turned[g], query, w_uv, keys, docs)

time: 34.4 us -> 33.3 us (0.968)
  local copies, waits for them, and re-layouts: 2.61 us -> 5.42 us
  waiting for transfers between devices: 7.7 us -> 4.97 us
  other arithmetic: 2.2 us -> 1.49 us
  starting transfers between devices: 12.8 us -> 12.3 us
    unnamed x8 -> x10, local copies, waits for them, and re-layouts: 2.2 us -> 5.33 us
    ppermute x12 -> x11, waiting for transfers between devices: 7.7 us -> 4.97 us  [swap(): return lax.ppermute(x, 'col', [(i, i ^ mask) for i in range(size)])]
    another operation x3 -> x2, other arithmetic: 1.4 us -> 0.69 us  [shards(): meta = jnp.pad(jnp.stack(meta), ((0, own_rows - 3), (0, META - own_rows)))]
    ppermute x12 -> x11, starting transfers between devices: 12.8 us -> 12.3 us  [swap(): return lax.ppermute(x, 'col', [(i, i ^ mask) for i in range(size)])]
    concatenate x1 -> x2, other arithmetic: 0.8 us -> 0.8 us  [the longest x1 0.8 us: shards(): jnp.concatenate([query_nope, query_rope, meta.astype(query_nope.dtype)],...]
  transfers between devices with their start and end apart: 12 -> 11, of which waited for: 5 -> 3; matrix products, arithmetic and copies ran while one was open for 8% -> 5% of each run, Pallas kernels for 18% -> 19%
where the time goes in v3:
time: 33.3 us; the launch traced here: 33 us
  starting transfers between devices  12.3 us (37%)
  Pallas kernels  8.7 us (26%)
  local copies, waits for them, and re-layouts  5.42 us (16%)
  waiting for transfers between devices  4.97 us (15%)
  other arithmetic  1.49 us (4%)
    ppermute x11, starting transfers between devices, swap(): return lax.ppermute(x, 'col', [(i, i ^ mask) for i in range(size)])  12.3 us
    pallas_call x4, Pallas kernels, attend(): pl.pallas_call(functools.partial(attend_kernel, near), out_shape=jax.Shap...  6.42 us
    unnamed x10, local copies, waits for them, and re-layouts  5.33 us
    ppermute x11, waiting for transfers between devices, swap(): return lax.ppermute(x, 'col', [(i, i ^ mask) for i in range(size)])  4.97 us
    pallas_call x1, Pallas kernels, absorb(): pl.pallas_call(functools.partial(absorb_kernel, count), out_shape=(jax.Sh...  1.39 us
    pallas_call x1, Pallas kernels, combine(): pl.pallas_call(functools.partial(combine_kernel, len(parts)), out_shape=j...  0.89 us
    concatenate x1, other arithmetic, shards(): jnp.concatenate([query_nope, query_rope, meta.astype(query_nope.dtype)],...  0.8 us
    another operation x2, other arithmetic, shards(): meta = jnp.pad(jnp.stack(meta), ((0, own_rows - 3), (0, META - own_rows)))  0.69 us
  transfers between devices with their start and end apart: 11, of which 3 were waited for; matrix products, arithmetic and copies ran while one was open for 5% of the time, Pallas kernels for 19%

profile of v3, /device:TPU:0, one launch (start us, length us, event | category | flops | bytes accessed | tf_op | source)
XLA Modules:
  0.0 33.0 jit_solution(14944014239882430806)
XLA Ops:
  0.0 0.0 copy-start.4
  0.0 3.0 %collective-permute-start.4 = (bf16[576,256]{1,0:T(8,128)(2,1)}, bf16[576,256]{1,0:T(8,128)(2,1)S(1)}, u32[]{:S(2)}, u32[]{:S(2)}) collective-permute-start(bf16[576,256]{1,0:T(8,128)(2,1)} %bitcast.25), channel_id=1, source_target_pairs={{0,2},{1,3},{2,0},{3,1},{4,6},{5,7},{6,4},{7,5},{8,10},{9,11},{10,... | collective-permute-start | bytes 884744 | tf_op jit(solution)/shard_map/ppermute | solution.py:217
  3.0 0.0 collective-permute-start.6
  3.0 0.7 %convert_bitcast_fusion.1 = (bf16[1,4]{1,0:T(2,128)(2,1)S(1)}, bf16[1,4]{1,0:T(2,128)(2,1)S(1)}, bf16[1,4]{1,0:T(2,128)(2,1)S(1)}) fusion(s32[4]{0:T(128)} %param.13, s32[4]{0:T(128)} %param.12), kind=kLoop, calls=%fused_computation.22 | loop fusion | flops 20 | bytes 56 | tf_op jit(solution)/shard_map/stack | solution.py:228
  3.7 0.8 %pad_maximum_fusion.refs_0_.q_ref = bf16[4,6272]{1,0:T(4,128)(2,1)S(1)} fusion(bf16[4,128]{1,0:T(4,128)(2,1)S(1)} %fusion.6, bf16[4,2048]{1,0:T(4,128)(2,1)} %param.9, bf16[4,4096]{1,0:T(4,128)(2,1)} %param.8), kind=kLoop, calls=%fused_computation.4 | loop fusion | flops 150528 | bytes 100352 | tf_op jit(solution)/shard_map/concatenate | solution.py:229
  4.5 1.6 %collective-permute-start = (bf16[4,6272]{1,0:T(4,128)(2,1)S(1)}, bf16[4,6272]{1,0:T(4,128)(2,1)S(1)}, u32[]{:S(2)}, u32[]{:S(2)}) collective-permute-start(bf16[4,6272]{1,0:T(4,128)(2,1)S(1)} %pad_maximum_fusion.refs_0_.q_ref), channel_id=1, source_target_pairs={{0,4},{1,5},{2,6},{3,7},{4,0},{5,1},{6,2},{7,3},{8,12},{9,13},{10,... | collective-permute-start | bytes 150536 | tf_op jit(solution)/shard_map/ppermute | solution.py:217
  6.1 2.6 %collective-permute-start.1 = (bf16[4,6272]{1,0:T(4,128)(2,1)S(1)}, bf16[4,6272]{1,0:T(4,128)(2,1)S(1)}, u32[]{:S(2)}, u32[]{:S(2)}) collective-permute-start(bf16[4,6272]{1,0:T(4,128)(2,1)S(1)} %pad_maximum_fusion.refs_0_.q_ref), channel_id=1, source_target_pairs={{0,8},{1,9},{2,10},{3,11},{4,12},{5,13},{6,14},{7,15},{8,0},{9,1},... | collective-permute-start | bytes 150536 | tf_op jit(solution)/shard_map/ppermute | solution.py:217
  8.7 0.2 collective-permute-start.2
  8.9 0.0 copy-start.1
  8.9 2.2 %copy-done.1 = bf16[512,4096]{1,0:T(8,128)(2,1)S(1)} copy-done((bf16[512,4096]{1,0:T(8,128)(2,1)S(1)}, bf16[512,4096]{1,0:T(8,128)(2,1)}, u32[]{:S(2)}) %copy-start.1) | copy-done | bytes 4194328
  11.1 0.0 copy-start.3
  11.1 0.0 copy-start
  11.1 0.0 collective-permute-done.6
  11.1 0.9 %copy-done.3 = bf16[256,576]{0,1:T(8,128)(2,1)S(1)} copy-done((bf16[256,576]{0,1:T(8,128)(2,1)S(1)}, bf16[256,576]{0,1:T(8,128)(2,1)}, u32[]{:S(2)}) %copy-start.3) | copy-done | bytes 294936
  12.1 0.0 collective-permute-start.3
  12.1 0.0 copy-done.4
  12.1 0.0 collective-permute-done.refs_1_.q_ref
  12.1 0.4 %collective-permute-start.7 = (s32[1,512]{1,0:T(1,128)S(1)}, s32[1,512]{1,0:T(1,128)S(1)}, u32[]{:S(2)}, u32[]{:S(2)}) collective-permute-start(s32[1,512]{1,0:T(1,128)S(1)} %pad_add_fusion.refs_4_), channel_id=1, source_target_pairs={{0,2},{1,3},{2,0},{3,1},{4,6},{5,7},{6,4},{7,5},{8,10},{9,11},{10,... | collective-permute-start | bytes 6152 | tf_op jit(solution)/shard_map/ppermute | solution.py:217
  12.5 0.0 collective-permute-done.1.refs_2_.q_ref
  12.5 2.1 %collective-permute-done.2.refs_3_.q_ref = bf16[4,6272]{1,0:T(4,128)(2,1)S(1)} collective-permute-done((bf16[4,6272]{1,0:T(4,128)(2,1)S(1)}, bf16[4,6272]{1,0:T(4,128)(2,1)S(1)}, u32[]{:S(2)}, u32[]{:S(2)}) %collective-permute-start.2) | collective-permute-done | bytes 50208 | tf_op jit(solution)/shard_map/ppermute | solution.py:217
  14.6 0.0 copy-start.2
  14.6 2.2 %copy-done.2 = bf16[512,4096]{1,0:T(8,128)(2,1)S(1)} copy-done((bf16[512,4096]{1,0:T(8,128)(2,1)S(1)}, bf16[512,4096]{1,0:T(8,128)(2,1)}, u32[]{:S(2)}) %copy-start.2) | copy-done | bytes 4194328
  16.8 1.4 %absorb.1 = (bf16[4,256,512]{2,1,0:T(8,128)(2,1)S(1)}, bf16[4,128,128]{2,1,0:T(8,128)(2,1)S(1)}) custom-call(bf16[4,6272]{1,0:T(4,128)(2,1)S(1)} %pad_maximum_fusion.refs_0_.q_ref, bf16[4,6272]{1,0:T(4,128)(2,1)S(1)} %collective-permute-done.refs_1_.q_ref, bf16[4,6272]{1,0:T(4,128)(2,1)S(1)} %collective-permute-done.1.refs_2_.q_ref, ...), custom_call_target="tpu_custom_call" | custom-call | tf_op jit(solution)/shard_map/absorb/pallas_call | solution.py:90
  18.2 0.0 collective-permute-done.4.refs_2_
  18.2 0.1 collective-permute-start.5
  18.3 0.1 slice_bitcast_fusion
  18.4 0.0 collective-permute-done.7.refs_5_
  18.4 0.0 collective-permute-done.3.refs_1_
  18.4 1.4 %collective-permute-done.5.refs_3_ = bf16[576,256]{1,0:T(8,128)(2,1)S(1)} collective-permute-done((bf16[576,256]{1,0:T(8,128)(2,1)S(1)}, bf16[576,256]{1,0:T(8,128)(2,1)S(1)}, u32[]{:S(2)}, u32[]{:S(2)}) %collective-permute-start.5) | collective-permute-done | bytes 294944 | tf_op jit(solution)/shard_map/ppermute | solution.py:217
  19.8 0.0 copy-done
  19.8 1.6 %attend.7 = f32[4,4352]{1,0:T(4,128)S(1)} custom-call(s32[1]{0:T(128)} %bitcast.me_ref, bf16[256,512]{1,0:T(8,128)(2,1)S(1)} %get-tuple-element.9.a_ref, bf16[128,128]{1,0:T(8,128)(2,1)S(1)} %get-tuple-element.13.r_ref, bf16[4,6272]{1,0:T(4,128)(2,1)S(1)} %collective-permute-done.2.refs_3_.q_ref, bf16[512,4096]{1,0:T(8,128)(2,1)S(1)} %copy-done, ...), custom_call_target="tpu_custom_call" | custom-call | tf_op jit(solution)/shard_map/attend/pallas_call | solution.py:164
  21.4 1.7 %collective-permute-start.10 = (f32[4,4352]{1,0:T(4,128)S(1)}, f32[4,4352]{1,0:T(4,128)S(1)}, u32[]{:S(2)}, u32[]{:S(2)}) collective-permute-start(f32[4,4352]{1,0:T(4,128)S(1)} %attend.7), channel_id=1, source_target_pairs={{0,12},{1,13},{2,14},{3,15},{4,8},{5,9},{6,10},{7,11},{8,4},{9,5},... | collective-permute-start | bytes 208904 | tf_op jit(solution)/shard_map/ppermute | solution.py:217
  23.2 1.6 %attend.6 = f32[4,4352]{1,0:T(4,128)S(1)} custom-call(s32[1]{0:T(128)} %bitcast.me_ref, bf16[256,512]{1,0:T(8,128)(2,1)S(1)} %get-tuple-element.10.a_ref, bf16[128,128]{1,0:T(8,128)(2,1)S(1)} %get-tuple-element.14.r_ref, bf16[4,6272]{1,0:T(4,128)(2,1)S(1)} %collective-permute-done.1.refs_2_.q_ref, bf16[512,4096]{1,0:T(8,128)(2,1)S(1)} %copy-done, ...), custom_call_target="tpu_custom_call" | custom-call | tf_op jit(solution)/shard_map/attend/pallas_call | solution.py:164
  24.8 0.0 collective-permute-start.9
  24.8 1.6 %attend.5 = f32[4,4352]{1,0:T(4,128)S(1)} custom-call(s32[1]{0:T(128)} %bitcast.me_ref, bf16[256,512]{1,0:T(8,128)(2,1)S(1)} %get-tuple-element.11.a_ref, bf16[128,128]{1,0:T(8,128)(2,1)S(1)} %get-tuple-element.15.r_ref, bf16[4,6272]{1,0:T(4,128)(2,1)S(1)} %collective-permute-done.refs_1_.q_ref, bf16[512,4096]{1,0:T(8,128)(2,1)S(1)} %copy-done, ...), custom_call_target="tpu_custom_call" | custom-call | tf_op jit(solution)/shard_map/attend/pallas_call | solution.py:164
  26.4 2.7 %collective-permute-start.8 = (f32[4,4352]{1,0:T(4,128)S(1)}, f32[4,4352]{1,0:T(4,128)S(1)}, u32[]{:S(2)}, u32[]{:S(2)}) collective-permute-start(f32[4,4352]{1,0:T(4,128)S(1)} %attend.5), channel_id=1, source_target_pairs={{0,4},{1,5},{2,6},{3,7},{4,0},{5,1},{6,2},{7,3},{8,12},{9,13},{10,... | collective-permute-start | bytes 208904 | tf_op jit(solution)/shard_map/ppermute | solution.py:217
  29.1 1.6 %attend.4.refs_0_ = f32[4,4352]{1,0:T(4,128)S(1)} custom-call(s32[1]{0:T(128)} %bitcast.me_ref, bf16[256,512]{1,0:T(8,128)(2,1)S(1)} %get-tuple-element.12.a_ref, bf16[128,128]{1,0:T(8,128)(2,1)S(1)} %get-tuple-element.16.r_ref, bf16[4,6272]{1,0:T(4,128)(2,1)S(1)} %pad_maximum_fusion.refs_0_.q_ref, bf16[512,4096]{1,0:T(8,128)(2,1)S(1)} %copy-done, ...), custom_call_target="tpu_custom_call" | custom-call | tf_op jit(solution)/shard_map/attend/pallas_call | solution.py:164
  30.7 0.0 collective-permute-done.10.refs_3_
  30.7 0.0 collective-permute-done.9.refs_2_
  30.7 1.4 %collective-permute-done.8.refs_1_ = f32[4,4352]{1,0:T(4,128)S(1)} collective-permute-done((f32[4,4352]{1,0:T(4,128)S(1)}, f32[4,4352]{1,0:T(4,128)S(1)}, u32[]{:S(2)}, u32[]{:S(2)}) %collective-permute-start.8) | collective-permute-done | bytes 69664 | tf_op jit(solution)/shard_map/ppermute | solution.py:217
  32.1 0.9 %combine.1 = bf16[4,4096]{1,0:T(4,128)(2,1)} custom-call(f32[4,4352]{1,0:T(4,128)S(1)} %attend.4.refs_0_, f32[4,4352]{1,0:T(4,128)S(1)} %collective-permute-done.8.refs_1_, f32[4,4352]{1,0:T(4,128)S(1)} %collective-permute-done.9.refs_2_, f32[4,4352]{1,0:T(4,128)S(1)} %collective-permute-done.10.refs_3_), custom_call_target="tpu_custom_call" | custom-call | tf_op jit(solution)/shard_map/combine/pallas_call | solution.py:201
  (4 shorter events, 0.0 us)
Async XLA Ops:
  0.0 12.1 %copy-start.4 = (s32[256]{0:T(256)S(1)}, s32[256]{0:T(256)}, u32[]{:S(2)}) copy-start(s32[256]{0:T(256)} %param.11) | copy-start | bytes 3076
  0.0 18.2 %collective-permute-start.4 = (bf16[576,256]{1,0:T(8,128)(2,1)}, bf16[576,256]{1,0:T(8,128)(2,1)S(1)}, u32[]{:S(2)}, u32[]{:S(2)}) collective-permute-start(bf16[576,256]{1,0:T(8,128)(2,1)} %bitcast.25), channel_id=1, source_target_pairs={{0,2},{1,3},{2,0},{3,1},{4,6},{5,7},{6,4},{7,5},{8,10},{9,11},{10,... | collective-permute-start | bytes 884744 | tf_op jit(solution)/shard_map/ppermute | solution.py:217
  3.0 8.1 %collective-permute-start.6 = (s32[1,256]{1,0:T(1,128)}, s32[1,256]{1,0:T(1,128)S(1)}, u32[]{:S(2)}, u32[]{:S(2)}) collective-permute-start(s32[1,256]{1,0:T(1,128)} %bitcast.31), channel_id=1, source_target_pairs={{0,1},{1,0},{2,3},{3,2},{4,5},{5,4},{6,7},{7,6},{8,9},{9,8},{10,11... | collective-permute-start | bytes 3080 | tf_op jit(solution)/shard_map/ppermute | solution.py:217
  4.5 7.6 %collective-permute-start = (bf16[4,6272]{1,0:T(4,128)(2,1)S(1)}, bf16[4,6272]{1,0:T(4,128)(2,1)S(1)}, u32[]{:S(2)}, u32[]{:S(2)}) collective-permute-start(bf16[4,6272]{1,0:T(4,128)(2,1)S(1)} %pad_maximum_fusion.refs_0_.q_ref), channel_id=1, source_target_pairs={{0,4},{1,5},{2,6},{3,7},{4,0},{5,1},{6,2},{7,3},{8,12},{9,13},{10,... | collective-permute-start | bytes 150536 | tf_op jit(solution)/shard_map/ppermute | solution.py:217
  6.1 6.4 %collective-permute-start.1 = (bf16[4,6272]{1,0:T(4,128)(2,1)S(1)}, bf16[4,6272]{1,0:T(4,128)(2,1)S(1)}, u32[]{:S(2)}, u32[]{:S(2)}) collective-permute-start(bf16[4,6272]{1,0:T(4,128)(2,1)S(1)} %pad_maximum_fusion.refs_0_.q_ref), channel_id=1, source_target_pairs={{0,8},{1,9},{2,10},{3,11},{4,12},{5,13},{6,14},{7,15},{8,0},{9,1},... | collective-permute-start | bytes 150536 | tf_op jit(solution)/shard_map/ppermute | solution.py:217
  8.7 5.9 %collective-permute-start.2 = (bf16[4,6272]{1,0:T(4,128)(2,1)S(1)}, bf16[4,6272]{1,0:T(4,128)(2,1)S(1)}, u32[]{:S(2)}, u32[]{:S(2)}) collective-permute-start(bf16[4,6272]{1,0:T(4,128)(2,1)S(1)} %pad_maximum_fusion.refs_0_.q_ref), channel_id=1, source_target_pairs={{0,12},{1,13},{2,14},{3,15},{4,8},{5,9},{6,10},{7,11},{8,4},{9,5},... | collective-permute-start | bytes 150536 | tf_op jit(solution)/shard_map/ppermute | solution.py:217
  8.9 2.2 %copy-start.1 = (bf16[512,4096]{1,0:T(8,128)(2,1)S(1)}, bf16[512,4096]{1,0:T(8,128)(2,1)}, u32[]{:S(2)}) copy-start(bf16[512,4096]{1,0:T(8,128)(2,1)} %refs_4_.1) | copy-start | bytes 12582916
  11.1 1.0 %copy-start.3 = (bf16[256,576]{0,1:T(8,128)(2,1)S(1)}, bf16[256,576]{0,1:T(8,128)(2,1)}, u32[]{:S(2)}) copy-start(bf16[256,576]{0,1:T(8,128)(2,1)} %param.10) | copy-start | bytes 884740
  11.1 8.7 %copy-start = (bf16[512,4096]{1,0:T(8,128)(2,1)S(1)}, bf16[512,4096]{1,0:T(8,128)(2,1)}, u32[]{:S(2)}) copy-start(bf16[512,4096]{1,0:T(8,128)(2,1)} %w_ref.9) | copy-start | bytes 12582916
  12.1 6.3 %collective-permute-start.3 = (bf16[576,256]{1,0:T(8,128)(2,1)S(1)}, bf16[576,256]{1,0:T(8,128)(2,1)S(1)}, u32[]{:S(2)}, u32[]{:S(2)}) collective-permute-start(bf16[576,256]{1,0:T(8,128)(2,1)S(1)} %bitcast.26), channel_id=1, source_target_pairs={{0,1},{1,0},{2,3},{3,2},{4,5},{5,4},{6,7},{7,6},{8,9},{9,8},{10,11... | collective-permute-start | bytes 884744 | tf_op jit(solution)/shard_map/ppermute | solution.py:217
  12.1 6.3 %collective-permute-start.7 = (s32[1,512]{1,0:T(1,128)S(1)}, s32[1,512]{1,0:T(1,128)S(1)}, u32[]{:S(2)}, u32[]{:S(2)}) collective-permute-start(s32[1,512]{1,0:T(1,128)S(1)} %pad_add_fusion.refs_4_), channel_id=1, source_target_pairs={{0,2},{1,3},{2,0},{3,1},{4,6},{5,7},{6,4},{7,5},{8,10},{9,11},{10,... | collective-permute-start | bytes 6152 | tf_op jit(solution)/shard_map/ppermute | solution.py:217
  14.6 2.2 %copy-start.2 = (bf16[512,4096]{1,0:T(8,128)(2,1)S(1)}, bf16[512,4096]{1,0:T(8,128)(2,1)}, u32[]{:S(2)}) copy-start(bf16[512,4096]{1,0:T(8,128)(2,1)} %refs_4_.1) | copy-start | bytes 12582916
  18.2 1.6 %collective-permute-start.5 = (bf16[576,256]{1,0:T(8,128)(2,1)S(1)}, bf16[576,256]{1,0:T(8,128)(2,1)S(1)}, u32[]{:S(2)}, u32[]{:S(2)}) collective-permute-start(bf16[576,256]{1,0:T(8,128)(2,1)S(1)} %collective-permute-done.4.refs_2_), channel_id=1, source_target_pairs={{0,1},{1,0},{2,3},{3,2},{4,5},{5,4},{6,7},{7,6},{8,9},{9,8},{10,11... | collective-permute-start | bytes 884744 | tf_op jit(solution)/shard_map/ppermute | solution.py:217
  21.4 9.3 %collective-permute-start.10 = (f32[4,4352]{1,0:T(4,128)S(1)}, f32[4,4352]{1,0:T(4,128)S(1)}, u32[]{:S(2)}, u32[]{:S(2)}) collective-permute-start(f32[4,4352]{1,0:T(4,128)S(1)} %attend.7), channel_id=1, source_target_pairs={{0,12},{1,13},{2,14},{3,15},{4,8},{5,9},{6,10},{7,11},{8,4},{9,5},... | collective-permute-start | bytes 208904 | tf_op jit(solution)/shard_map/ppermute | solution.py:217
  24.8 5.9 %collective-permute-start.9 = (f32[4,4352]{1,0:T(4,128)S(1)}, f32[4,4352]{1,0:T(4,128)S(1)}, u32[]{:S(2)}, u32[]{:S(2)}) collective-permute-start(f32[4,4352]{1,0:T(4,128)S(1)} %attend.6), channel_id=1, source_target_pairs={{0,8},{1,9},{2,10},{3,11},{4,12},{5,13},{6,14},{7,15},{8,0},{9,1},... | collective-permute-start | bytes 208904 | tf_op jit(solution)/shard_map/ppermute | solution.py:217
  26.4 5.7 %collective-permute-start.8 = (f32[4,4352]{1,0:T(4,128)S(1)}, f32[4,4352]{1,0:T(4,128)S(1)}, u32[]{:S(2)}, u32[]{:S(2)}) collective-permute-start(f32[4,4352]{1,0:T(4,128)S(1)} %attend.5), channel_id=1, source_target_pairs={{0,4},{1,5},{2,6},{3,7},{4,0},{5,1},{6,2},{7,3},{8,12},{9,13},{10,... | collective-permute-start | bytes 208904 | tf_op jit(solution)/shard_map/ppermute | solution.py:217

commit v4 on v3

v4 whole, which is shorter than its diff:
```python
import functools
import math

import jax
import jax.numpy as jnp
from jax import lax
from jax.experimental import pallas as pl
from jax.experimental.pallas import tpu as pltpu
from jax.sharding import PartitionSpec as P


H = 32
DN = 128
DR = 64
DV = 128
R = 512
META = 128
PAIRS = H // 2
LEAD = 2000000000
HIDDEN = -1e30
FLOOR = -1e29
VMEM = pl.BlockSpec(memory_space=pltpu.VMEM)
SMEM = pl.BlockSpec(memory_space=pltpu.SMEM)
SMALL = pltpu.CompilerParams(vmem_limit_bytes=2 * 1024 * 1024)
PARAMS = pltpu.CompilerParams(vmem_limit_bytes=24 * 1024 * 1024)


def iota(shape, axis):
    return lax.broadcasted_iota(jnp.int32, shape, axis)


def split(x):
    high = x.astype(jnp.bfloat16).astype(jnp.float32)
    return high, x - high


def diagonal(x):
    wide = jnp.concatenate([x, x], axis=0)
    own, half = x.shape[0], x.shape[1] // 2
    keep = (iota(wide.shape, 0) // own) == (iota(wide.shape, 1) // half)
    return jnp.where(keep, wide, 0.0)


def lead_kernel(out_ref):
    out_ref[...] = jnp.zeros_like(out_ref)


def lead(flops):
    return pl.pallas_call(
        lead_kernel,
        out_shape=jax.ShapeDtypeStruct((8, META), jnp.float32),
        out_specs=VMEM,
        compiler_params=SMALL,
        cost_estimate=pl.CostEstimate(flops=flops, transcendentals=0, bytes_accessed=4096),
        name="lead",
    )()


def pack_kernel(lead_ref, doc_ref, pos_ref, nope_ref, rope_ref, out_ref):
    rows = out_ref.shape[0]
    pos = pos_ref[...]
    meta = [doc_ref[...], lax.shift_right_logical(pos, 8), lax.bitwise_and(pos, 255)]
    meta.append(jnp.zeros((1, META - 3 * rows), jnp.int32))
    meta = jnp.concatenate(meta, axis=1).astype(jnp.float32)
    out_ref[:, : H * DN] = nope_ref[...]
    out_ref[:, H * DN : H * (DN + DR)] = rope_ref[...]
    out_ref[:, H * (DN + DR) :] = jnp.broadcast_to(meta, (rows, META)).astype(out_ref.dtype)


def pack(first, query_docs, query_pos, query_nope, query_rope):
    rows = query_nope.shape[0]
    width = query_nope.shape[1] + query_rope.shape[1] + META
    return pl.pallas_call(
        pack_kernel,
        out_shape=jax.ShapeDtypeStruct((rows, width), query_nope.dtype),
        in_specs=[VMEM] * 5,
        out_specs=VMEM,
        compiler_params=SMALL,
        name="pack",
    )(first, query_docs.reshape(1, rows), query_pos.reshape(1, rows), query_nope, query_rope)


def join_kernel(a_ref, b_ref, out_ref):
    out_ref[...] = jnp.concatenate([a_ref[...], b_ref[...]], axis=1)


def join(a, b):
    return pl.pallas_call(
        join_kernel,
        out_shape=jax.ShapeDtypeStruct((1, a.shape[1] + b.shape[1]), a.dtype),
        in_specs=[VMEM] * 2,
        out_specs=VMEM,
        compiler_params=SMALL,
        name="join",
    )(a, b)


def absorb_kernel(count, *refs):
    queries, (w_ref, _, a_ref, r_ref) = refs[:count], refs[count:]
    half = a_ref.shape[1] // 2
    step = 2 * half // PAIRS
    for duo in range(PAIRS // 2):
        found = []
        for pair in (2 * duo, 2 * duo + 1):
            cols = slice(pair * 2 * DN, (pair + 1) * 2 * DN)
            lhs = [diagonal(q[:, cols].astype(jnp.float32)) for q in queries]
            lhs = jnp.concatenate(lhs, axis=0).astype(jnp.bfloat16)
            found.append(
                lax.dot_general(
                    lhs, w_ref[:, cols], (((1,), (1,)), ((), ())), preferred_element_type=jnp.float32
                )
            )
        rows = slice(duo * step, (duo + 1) * step)
        low_rows = slice(half + duo * step, half + (duo + 1) * step)
        small = step // 2
        for g in range(count):
            own = slice(g * small, (g + 1) * small)
            high, low = split(jnp.concatenate([f[own] for f in found], axis=0))
            a_ref[g, rows] = high.astype(jnp.bfloat16)
            a_ref[g, low_rows] = low.astype(jnp.bfloat16)
            turned = []
            for pair in (2 * duo, 2 * duo + 1):
                cols = slice(H * DN + pair * 2 * DR, H * DN + (pair + 1) * 2 * DR)
                turned.append(diagonal(queries[g][:, cols].astype(jnp.float32)))
            r_ref[g, rows] = jnp.concatenate(turned, axis=0).astype(jnp.bfloat16)


def absorb(queries, w_uk, started):
    count = len(queries)
    rows = queries[0].shape[0] * H
    return pl.pallas_call(
        functools.partial(absorb_kernel, count),
        out_shape=(
            jax.ShapeDtypeStruct((count, 2 * rows, R), jnp.bfloat16),
            jax.ShapeDtypeStruct((count, rows, 2 * DR), jnp.bfloat16),
        ),
        in_specs=[VMEM] * (count + 2),
        out_specs=(VMEM, VMEM),
        compiler_params=PARAMS,
        name="absorb",
    )(*queries, w_uk, started)


def attend_kernel(near, count, first, me_ref, a_ref, r_ref, w_ref, *refs):
    queries, keys = refs[:count], refs[count : count + near]
    docs, outs = refs[count + near : -count], refs[-count:]
    rows = r_ref.shape[1]
    own = queries[0].shape[0]
    eight = 2 * own
    tokens = keys[0].shape[1]
    scale = 1.0 / math.sqrt(DN + DR)
    me = me_ref[0]
    group = range(count)

    spot = iota((eight, META), 0) % own
    lane = iota((eight, META), 1)
    limits = []
    for q in queries:
        meta = q[:1, H * (DN + DR) :].astype(jnp.float32)
        values = [
            jnp.sum(jnp.where(lane == spot + i * own, meta, 0.0), axis=1, keepdims=True)
            for i in range(3)
        ]
        limits.append((values[0], values[1] * 256.0 + values[2]))

    absorbed = jnp.concatenate([a_ref[first + g] for g in group], axis=0)
    turned = jnp.concatenate([r_ref[first + g] for g in group], axis=0)
    scores = [[] for _ in group]
    for k in range(near):
        latent = keys[k][:R, :]
        rope = keys[k][R:, :]
        both = jnp.dot(absorbed, latent, preferred_element_type=jnp.float32)
        turn = jnp.dot(
            turned, jnp.concatenate([rope, rope], axis=0), preferred_element_type=jnp.float32
        )
        place = lax.bitwise_xor(me, k) * tokens + iota((eight, tokens), 1)
        doc = docs[k // 2][:, (k % 2) * tokens : (k % 2 + 1) * tokens].astype(jnp.float32)
        for g in group:
            q_doc, q_pos = limits[g]
            visible = (doc == q_doc) & (place.astype(jnp.float32) <= q_pos)
            top = 2 * g * rows
            found = both[top : top + rows] + both[top + rows : top + 2 * rows]
            found = (found + turn[g * rows : (g + 1) * rows]) * scale
            found = found.reshape(rows // eight, eight, tokens)
            scores[g].append(jnp.where(visible[None], found, HIDDEN).reshape(rows, tokens))
    bests, totals = [], []
    for g in group:
        best = functools.reduce(jnp.maximum, scores[g])
        bests.append(jnp.maximum(jnp.max(best, axis=1, keepdims=True), FLOOR))
    mixed = None
    sums = [None for _ in group]
    for k in range(near):
        both = []
        for g in group:
            weights = jnp.exp(scores[g][k] - bests[g])
            sums[g] = weights if sums[g] is None else sums[g] + weights
            both += split(weights)
        both = jnp.concatenate(both, axis=0).astype(jnp.bfloat16)
        part = lax.dot_general(
            both, keys[k][:R, :], (((1,), (1,)), ((), ())), preferred_element_type=jnp.float32
        )
        mixed = part if mixed is None else mixed + part
    totals = [jnp.sum(s, axis=1, keepdims=True) for s in sums]
    halves = []
    for g in group:
        top = 2 * g * rows
        halves += split(mixed[top : top + rows] + mixed[top + rows : top + 2 * rows])
    stats = [jnp.zeros((eight, META), jnp.float32) for _ in group]
    for pair in range(PAIRS):
        take = slice(pair * eight, (pair + 1) * eight)
        cols = slice(pair * 2 * DV, (pair + 1) * 2 * DV)
        lhs = jnp.concatenate([h[take] for h in halves], axis=0).astype(jnp.bfloat16)
        res = jnp.dot(lhs, w_ref[:, cols], preferred_element_type=jnp.float32)
        for g in group:
            top = 2 * g * eight
            part = res[top : top + eight] + res[top + eight : top + 2 * eight]
            outs[g][:, cols] = jnp.concatenate([part[:own, :DV], part[own:, DV:]], axis=1)
            for base, value in ((0, bests[g]), (2 * PAIRS, totals[g])):
                at = base + pair + jnp.where(iota((eight, META), 0) < own, 0, PAIRS)
                stats[g] = jnp.where(lane == at, value[take], stats[g])
    for g in group:
        outs[g][:, H * DV :] = stats[g][:own] + stats[g][own:]


def attend(me, first, absorbed, turned, queries, w_uv, keys, docs):
    near, count = len(keys), len(queries)
    part = jax.ShapeDtypeStruct((queries[0].shape[0], H * DV + META), jnp.float32)
    return pl.pallas_call(
        functools.partial(attend_kernel, near, count, first),
        out_shape=(part,) * count,
        in_specs=[SMEM] + [VMEM] * (3 + count + near + len(docs)),
        out_specs=(VMEM,) * count,
        compiler_params=PARAMS,
        name="attend",
    )(me, absorbed, turned, w_uv, *queries, *keys, *docs)


def combine_kernel(count, *refs):
    parts, out_ref = refs[:count], refs[count]
    stats = [p[:, H * DV :] for p in parts]
    maxima = [s[:, :H] for s in stats]
    top = functools.reduce(jnp.maximum, maxima)
    factors = [jnp.exp(m - top) for m in maxima]
    total = functools.reduce(jnp.add, [f * s[:, H : 2 * H] for f, s in zip(factors, stats)])
    factors = [f / total for f in factors]
    for head in range(H):
        cols = slice(head * DV, (head + 1) * DV)
        lane = (head % 2) * PAIRS + head // 2
        terms = [p[:, cols] * f[:, lane : lane + 1] for p, f in zip(parts, factors)]
        out_ref[:, cols] = functools.reduce(jnp.add, terms).astype(out_ref.dtype)


def combine(parts):
    return pl.pallas_call(
        functools.partial(combine_kernel, len(parts)),
        out_shape=jax.ShapeDtypeStruct((parts[0].shape[0], H * DV), jnp.bfloat16),
        in_specs=[VMEM] * len(parts),
        out_specs=VMEM,
        compiler_params=PARAMS,
        name="combine",
    )(*parts)


def shards(size, query_nope, query_rope, cache, key_docs, query_docs, query_pos, w_uk, w_uv):
    near = math.gcd(size, 4)
    far = size // near
    me = lax.axis_index("col")

    def swap(x, mask):
        return lax.ppermute(x, "col", [(i, i ^ mask) for i in range(size)])

    block, doc = cache.T, key_docs.reshape(1, -1)
    keys, docs = {0: block}, [doc]
    if near == 4:
        keys[2] = swap(block, 2)
    if near > 1:
        keys[1] = swap(block, 1)
        docs = [join(doc, swap(doc, 1))]
    first = lead(LEAD)
    mine = pack(first, query_docs, query_pos, query_nope, query_rope)
    groups = [mine]
    for k in range(1, far):
        groups.append(swap(mine, near * k))
    if near == 4:
        docs.append(swap(docs[0], 2))
        keys[3] = swap(keys[2], 1)
    keys = [keys[k] for k in range(near)]
    started = lead(4 * LEAD)
    where = jnp.reshape(me, (1,)).astype(jnp.int32)
    parts = [None] * far
    for start in range(0, far, 4):
        some = groups[start : start + 4]
        absorbed, turned = absorb(some, w_uk, started)
        for first in range(len(some) - len(some) % 2, -1, -2):
            pick = some[first : first + 2]
            if not pick:
                continue
            found = attend(where, first, absorbed, turned, pick, w_uv, keys, docs)
            for g, part in enumerate(found):
                k = start + first + g
                parts[k] = part if k == 0 else swap(part, near * k)
    return combine(parts)


def solution(mesh):
    split_rows = P(("ga", "col"), None)
    split_flat = P(("ga", "col"))
    placed = (split_rows, split_rows, split_rows, split_flat, split_flat, split_flat, P(), P())
    size = mesh.shape["col"]

    def body(*arrays):
        return shards(size, *arrays)

    return jax.shard_map(body, mesh=mesh, in_specs=placed, out_specs=split_rows, check_vma=False)
```

time: 33.3 us -> 29.7 us (0.89)
  local copies, waits for them, and re-layouts: 5.42 us -> 2.21 us
  waiting for transfers between devices: 4.97 us -> 7.13 us
  other arithmetic: 1.49 us -> 0 us
  Pallas kernels: 8.7 us -> 7.32 us
  starting transfers between devices: 12.3 us -> 12.8 us
    unnamed x10 -> x16, local copies, waits for them, and re-layouts: 5.33 us -> 2.21 us
    ppermute x11, waiting for transfers between devices: 4.97 us -> 7.13 us  [swap(): return lax.ppermute(x, 'col', [(i, i ^ mask) for i in range(size)])]
    pallas_call x5 -> x6, Pallas kernels: 6.42 us -> 4.97 us  [the longest x2 4.88 us: attend(): pl.pallas_call(functools.partial(attend_kernel, near, count, first), out_...]
    concatenate x2 -> x0, other arithmetic: 0.8 us -> none  [the longest x1 0.8 us: shards(): jnp.concatenate([query_nope, query_rope, meta.astype(query_nope.dtype)],...]
    another operation x2 -> x0, other arithmetic: 0.69 us -> none  [shards(): meta = jnp.pad(jnp.stack(meta), ((0, own_rows - 3), (0, META - own_rows)))]
    ppermute x11, starting transfers between devices: 12.3 us -> 12.8 us  [swap(): return lax.ppermute(x, 'col', [(i, i ^ mask) for i in range(size)])]
  transfers between devices with their start and end apart: 11 -> 11, of which waited for: 3 -> 5; matrix products, arithmetic and copies ran while one was open for 5% -> 0% of each run, Pallas kernels for 19% -> 13%
where the time goes in v4:
time: 29.7 us; the launch traced here: 29.6 us
  starting transfers between devices  12.8 us (43%)
  Pallas kernels  7.32 us (25%)
  waiting for transfers between devices  7.13 us (24%)
  local copies, waits for them, and re-layouts  2.21 us (7%)
    ppermute x11, starting transfers between devices, swap(): return lax.ppermute(x, 'col', [(i, i ^ mask) for i in range(size)])  12.8 us
    ppermute x11, waiting for transfers between devices, swap(): return lax.ppermute(x, 'col', [(i, i ^ mask) for i in range(size)])  7.13 us
    pallas_call x2, Pallas kernels, attend(): pl.pallas_call(functools.partial(attend_kernel, near, count, first), out_...  4.88 us
    unnamed x16, local copies, waits for them, and re-layouts  2.21 us
    pallas_call x1, Pallas kernels, absorb(): pl.pallas_call(functools.partial(absorb_kernel, count), out_shape=(jax.Sh...  1.39 us
    pallas_call x1, Pallas kernels, combine(): pl.pallas_call(functools.partial(combine_kernel, len(parts)), out_shape=j...  0.96 us
  transfers between devices with their start and end apart: 11, of which 5 were waited for; matrix products, arithmetic and copies ran while one was open for 0% of the time, Pallas kernels for 13%

profile of v4, /device:TPU:0, one launch (start us, length us, event | category | flops | bytes accessed | tf_op | source)
XLA Modules:
  0.0 29.6 jit_solution(17553944923284887330)
XLA Ops:
  0.0 0.0 copy-start.2
  0.0 0.0 copy-start.6
  0.0 0.0 copy-start.7
  0.0 0.0 copy-start.3
  0.0 0.0 copy-start.4
  0.0 0.0 copy-start.5
  0.0 3.0 %collective-permute-start.4 = (bf16[576,256]{1,0:T(8,128)(2,1)}, bf16[576,256]{1,0:T(8,128)(2,1)S(1)}, u32[]{:S(2)}, u32[]{:S(2)}) collective-permute-start(bf16[576,256]{1,0:T(8,128)(2,1)} %bitcast.5), channel_id=1, source_target_pairs={{0,2},{1,3},{2,0},{3,1},{4,6},{5,7},{6,4},{7,5},{8,10},{9,11},{10,... | collective-permute-start | bytes 884744 | tf_op jit(solution)/shard_map/ppermute | solution.py:270
  3.1 0.0 copy-done.6
  3.1 0.0 copy-done.7
  3.1 0.0 copy-done.3
  3.1 0.0 copy-done.4
  3.1 0.1 pack.1.refs_0_
  3.2 1.6 %collective-permute-start = (bf16[4,6272]{1,0:T(4,128)(2,1)S(1)}, bf16[4,6272]{1,0:T(4,128)(2,1)S(1)}, u32[]{:S(2)}, u32[]{:S(2)}) collective-permute-start(bf16[4,6272]{1,0:T(4,128)(2,1)S(1)} %pack.1.refs_0_), channel_id=1, source_target_pairs={{0,4},{1,5},{2,6},{3,7},{4,0},{5,1},{6,2},{7,3},{8,12},{9,13},{10,... | collective-permute-start | bytes 150536 | tf_op jit(solution)/shard_map/ppermute | solution.py:270
  4.8 0.0 copy-done.5
  4.8 0.0 collective-permute-start.6
  4.8 2.6 %collective-permute-start.1 = (bf16[4,6272]{1,0:T(4,128)(2,1)S(1)}, bf16[4,6272]{1,0:T(4,128)(2,1)S(1)}, u32[]{:S(2)}, u32[]{:S(2)}) collective-permute-start(bf16[4,6272]{1,0:T(4,128)(2,1)S(1)} %pack.1.refs_0_), channel_id=1, source_target_pairs={{0,8},{1,9},{2,10},{3,11},{4,12},{5,13},{6,14},{7,15},{8,0},{9,1},... | collective-permute-start | bytes 150536 | tf_op jit(solution)/shard_map/ppermute | solution.py:270
  7.4 0.2 collective-permute-start.2
  7.6 0.0 collective-permute-done.6.b_ref
  7.6 0.0 copy-done.2
  7.6 0.1 collective-permute-start.3
  7.7 0.0 collective-permute-done.refs_1_
  7.7 0.8 %collective-permute-start.7 = (s32[1,512]{1,0:T(1,128)S(1)}, s32[1,512]{1,0:T(1,128)S(1)}, u32[]{:S(2)}, u32[]{:S(2)}) collective-permute-start(s32[1,512]{1,0:T(1,128)S(1)} %join.1.refs_6_), channel_id=1, source_target_pairs={{0,2},{1,3},{2,0},{3,1},{4,6},{5,7},{6,4},{7,5},{8,10},{9,11},{10,... | collective-permute-start | bytes 6152 | tf_op jit(solution)/shard_map/ppermute | solution.py:270
  8.4 1.8 %collective-permute-done.4.refs_4_ = bf16[576,256]{1,0:T(8,128)(2,1)S(1)} collective-permute-done((bf16[576,256]{1,0:T(8,128)(2,1)}, bf16[576,256]{1,0:T(8,128)(2,1)S(1)}, u32[]{:S(2)}, u32[]{:S(2)}) %collective-permute-start.4) | collective-permute-done | bytes 294944 | tf_op jit(solution)/shard_map/ppermute | solution.py:270
  10.3 0.0 collective-permute-start.5
  10.3 0.0 copy-start
  10.3 0.7 %collective-permute-done.1.refs_2_.refs_0_ = bf16[4,6272]{1,0:T(4,128)(2,1)S(1)} collective-permute-done((bf16[4,6272]{1,0:T(4,128)(2,1)S(1)}, bf16[4,6272]{1,0:T(4,128)(2,1)S(1)}, u32[]{:S(2)}, u32[]{:S(2)}) %collective-permute-start.1) | collective-permute-done | bytes 50208 | tf_op jit(solution)/shard_map/ppermute | solution.py:270
  11.0 2.2 %collective-permute-done.2.refs_3_.refs_1_ = bf16[4,6272]{1,0:T(4,128)(2,1)S(1)} collective-permute-done((bf16[4,6272]{1,0:T(4,128)(2,1)S(1)}, bf16[4,6272]{1,0:T(4,128)(2,1)S(1)}, u32[]{:S(2)}, u32[]{:S(2)}) %collective-permute-start.2) | collective-permute-done | bytes 50208 | tf_op jit(solution)/shard_map/ppermute | solution.py:270
  13.3 0.0 copy-start.1
  13.3 2.2 %copy-done.1 = bf16[512,4096]{1,0:T(8,128)(2,1)S(1)} copy-done((bf16[512,4096]{1,0:T(8,128)(2,1)S(1)}, bf16[512,4096]{1,0:T(8,128)(2,1)}, u32[]{:S(2)}) %copy-start.1) | copy-done | bytes 4194328
  15.4 1.4 %absorb.1 = (bf16[4,256,512]{2,1,0:T(8,128)(2,1)S(1)}, bf16[4,128,128]{2,1,0:T(8,128)(2,1)S(1)}) custom-call(bf16[4,6272]{1,0:T(4,128)(2,1)S(1)} %pack.1.refs_0_, bf16[4,6272]{1,0:T(4,128)(2,1)S(1)} %collective-permute-done.refs_1_, bf16[4,6272]{1,0:T(4,128)(2,1)S(1)} %collective-permute-done.1.refs_2_.refs_0_, ...), custom_call_target="tpu_custom_call" | custom-call | tf_op jit(solution)/shard_map/absorb/pallas_call | solution.py:131
  16.8 0.0 collective-permute-done.7.refs_7_
  16.8 0.0 collective-permute-done.3.refs_3_
  16.9 0.0 collective-permute-done.5.refs_5_
  16.9 0.0 copy-done
  16.9 2.4 %attend.3 = (f32[4,4224]{1,0:T(4,128)S(1)}, f32[4,4224]{1,0:T(4,128)S(1)}) custom-call(s32[1]{0:T(128)} %bitcast.me_ref, bf16[4,256,512]{2,1,0:T(8,128)(2,1)S(1)} %get-tuple-element.11.a_ref, bf16[4,128,128]{2,1,0:T(8,128)(2,1)S(1)} %get-tuple-element.12.r_ref, bf16[512,4096]{1,0:T(8,128)(2,1)S(1)} %copy-done, ...), custom_call_target="tpu_custom_call" | custom-call | tf_op jit(solution)/shard_map/attend/pallas_call | solution.py:228
  19.3 2.1 %collective-permute-start.10 = (f32[4,4224]{1,0:T(4,128)S(1)}, f32[4,4224]{1,0:T(4,128)S(1)}, u32[]{:S(2)}, u32[]{:S(2)}) collective-permute-start(f32[4,4224]{1,0:T(4,128)S(1)} %get-tuple-element.16), channel_id=1, source_target_pairs={{0,12},{1,13},{2,14},{3,15},{4,8},{5,9},{6,10},{7,11},{8,4},{9,5},... | collective-permute-start | bytes 202760 | tf_op jit(solution)/shard_map/ppermute | solution.py:270
  21.5 0.0 collective-permute-start.9
  21.5 2.4 %attend.2 = (f32[4,4224]{1,0:T(4,128)S(1)}, f32[4,4224]{1,0:T(4,128)S(1)}) custom-call(s32[1]{0:T(128)} %bitcast.me_ref, bf16[4,256,512]{2,1,0:T(8,128)(2,1)S(1)} %get-tuple-element.11.a_ref, bf16[4,128,128]{2,1,0:T(8,128)(2,1)S(1)} %get-tuple-element.12.r_ref, bf16[512,4096]{1,0:T(8,128)(2,1)S(1)} %copy-done, bf16[4,6272]{1,0:T(4,128)(2,1)S(1)} %pack.1.refs_0_, ...), custom_call_target="tpu_custom_call" | custom-call | tf_op jit(solution)/shard_map/attend/pallas_call | solution.py:228
  23.9 2.4 %collective-permute-start.8 = (f32[4,4224]{1,0:T(4,128)S(1)}, f32[4,4224]{1,0:T(4,128)S(1)}, u32[]{:S(2)}, u32[]{:S(2)}) collective-permute-start(f32[4,4224]{1,0:T(4,128)S(1)} %get-tuple-element.14), channel_id=1, source_target_pairs={{0,4},{1,5},{2,6},{3,7},{4,0},{5,1},{6,2},{7,3},{8,12},{9,13},{10,... | collective-permute-start | bytes 202760 | tf_op jit(solution)/shard_map/ppermute | solution.py:270
  26.3 0.0 collective-permute-done.10.refs_3_
  26.3 1.4 %collective-permute-done.9.refs_2_ = f32[4,4224]{1,0:T(4,128)S(1)} collective-permute-done((f32[4,4224]{1,0:T(4,128)S(1)}, f32[4,4224]{1,0:T(4,128)S(1)}, u32[]{:S(2)}, u32[]{:S(2)}) %collective-permute-start.9) | collective-permute-done | bytes 67616 | tf_op jit(solution)/shard_map/ppermute | solution.py:270
  27.7 0.9 %collective-permute-done.8.refs_1_ = f32[4,4224]{1,0:T(4,128)S(1)} collective-permute-done((f32[4,4224]{1,0:T(4,128)S(1)}, f32[4,4224]{1,0:T(4,128)S(1)}, u32[]{:S(2)}, u32[]{:S(2)}) %collective-permute-start.8) | collective-permute-done | bytes 67616 | tf_op jit(solution)/shard_map/ppermute | solution.py:270
  28.6 1.0 %combine.1 = bf16[4,4096]{1,0:T(4,128)(2,1)} custom-call(f32[4,4224]{1,0:T(4,128)S(1)} %get-tuple-element.13.refs_0_, f32[4,4224]{1,0:T(4,128)S(1)} %collective-permute-done.8.refs_1_, f32[4,4224]{1,0:T(4,128)S(1)} %collective-permute-done.9.refs_2_, f32[4,4224]{1,0:T(4,128)S(1)} %collective-permute-done.10.refs_3_), custom_call_target="tpu_custom_call" | custom-call | tf_op jit(solution)/shard_map/combine/pallas_call | solution.py:254
  (3 shorter events, 0.0 us)
Async XLA Ops:
  0.0 7.6 %copy-start.2 = (bf16[256,576]{0,1:T(8,128)(2,1)S(1)}, bf16[256,576]{0,1:T(8,128)(2,1)}, u32[]{:S(2)}) copy-start(bf16[256,576]{0,1:T(8,128)(2,1)} %param.10) | copy-start | bytes 884740
  0.0 3.1 %copy-start.6 = (s32[4]{0:T(128)S(1)}, s32[4]{0:T(128)}, u32[]{:S(2)}) copy-start(s32[4]{0:T(128)} %param.12) | copy-start | bytes 52
  0.0 3.1 %copy-start.7 = (s32[4]{0:T(128)S(1)}, s32[4]{0:T(128)}, u32[]{:S(2)}) copy-start(s32[4]{0:T(128)} %param.13) | copy-start | bytes 52
  0.0 3.1 %copy-start.3 = (bf16[4,4096]{1,0:T(4,128)(2,1)S(1)}, bf16[4,4096]{1,0:T(4,128)(2,1)}, u32[]{:S(2)}) copy-start(bf16[4,4096]{1,0:T(4,128)(2,1)} %nope_ref.1) | copy-start | bytes 98308
  0.0 3.1 %copy-start.4 = (bf16[4,2048]{1,0:T(4,128)(2,1)S(1)}, bf16[4,2048]{1,0:T(4,128)(2,1)}, u32[]{:S(2)}) copy-start(bf16[4,2048]{1,0:T(4,128)(2,1)} %rope_ref.1) | copy-start | bytes 49156
  0.0 4.7 %copy-start.5 = (s32[256]{0:T(256)S(1)}, s32[256]{0:T(256)}, u32[]{:S(2)}) copy-start(s32[256]{0:T(256)} %param.11) | copy-start | bytes 3076
  0.0 10.3 %collective-permute-start.4 = (bf16[576,256]{1,0:T(8,128)(2,1)}, bf16[576,256]{1,0:T(8,128)(2,1)S(1)}, u32[]{:S(2)}, u32[]{:S(2)}) collective-permute-start(bf16[576,256]{1,0:T(8,128)(2,1)} %bitcast.5), channel_id=1, source_target_pairs={{0,2},{1,3},{2,0},{3,1},{4,6},{5,7},{6,4},{7,5},{8,10},{9,11},{10,... | collective-permute-start | bytes 884744 | tf_op jit(solution)/shard_map/ppermute | solution.py:270
  3.2 4.5 %collective-permute-start = (bf16[4,6272]{1,0:T(4,128)(2,1)S(1)}, bf16[4,6272]{1,0:T(4,128)(2,1)S(1)}, u32[]{:S(2)}, u32[]{:S(2)}) collective-permute-start(bf16[4,6272]{1,0:T(4,128)(2,1)S(1)} %pack.1.refs_0_), channel_id=1, source_target_pairs={{0,4},{1,5},{2,6},{3,7},{4,0},{5,1},{6,2},{7,3},{8,12},{9,13},{10,... | collective-permute-start | bytes 150536 | tf_op jit(solution)/shard_map/ppermute | solution.py:270
  4.8 2.8 %collective-permute-start.6 = (s32[1,256]{1,0:T(1,128)S(1)}, s32[1,256]{1,0:T(1,128)S(1)}, u32[]{:S(2)}, u32[]{:S(2)}) collective-permute-start(s32[1,256]{1,0:T(1,128)S(1)} %bitcast.9), channel_id=1, source_target_pairs={{0,1},{1,0},{2,3},{3,2},{4,5},{5,4},{6,7},{7,6},{8,9},{9,8},{10,11... | collective-permute-start | bytes 3080 | tf_op jit(solution)/shard_map/ppermute | solution.py:270
  4.8 6.3 %collective-permute-start.1 = (bf16[4,6272]{1,0:T(4,128)(2,1)S(1)}, bf16[4,6272]{1,0:T(4,128)(2,1)S(1)}, u32[]{:S(2)}, u32[]{:S(2)}) collective-permute-start(bf16[4,6272]{1,0:T(4,128)(2,1)S(1)} %pack.1.refs_0_), channel_id=1, source_target_pairs={{0,8},{1,9},{2,10},{3,11},{4,12},{5,13},{6,14},{7,15},{8,0},{9,1},... | collective-permute-start | bytes 150536 | tf_op jit(solution)/shard_map/ppermute | solution.py:270
  7.4 5.9 %collective-permute-start.2 = (bf16[4,6272]{1,0:T(4,128)(2,1)S(1)}, bf16[4,6272]{1,0:T(4,128)(2,1)S(1)}, u32[]{:S(2)}, u32[]{:S(2)}) collective-permute-start(bf16[4,6272]{1,0:T(4,128)(2,1)S(1)} %pack.1.refs_0_), channel_id=1, source_target_pairs={{0,12},{1,13},{2,14},{3,15},{4,8},{5,9},{6,10},{7,11},{8,4},{9,5},... | collective-permute-start | bytes 150536 | tf_op jit(solution)/shard_map/ppermute | solution.py:270
  7.6 9.3 %collective-permute-start.3 = (bf16[576,256]{1,0:T(8,128)(2,1)S(1)}, bf16[576,256]{1,0:T(8,128)(2,1)S(1)}, u32[]{:S(2)}, u32[]{:S(2)}) collective-permute-start(bf16[576,256]{1,0:T(8,128)(2,1)S(1)} %bitcast.6), channel_id=1, source_target_pairs={{0,1},{1,0},{2,3},{3,2},{4,5},{5,4},{6,7},{7,6},{8,9},{9,8},{10,11... | collective-permute-start | bytes 884744 | tf_op jit(solution)/shard_map/ppermute | solution.py:270
  7.7 9.2 %collective-permute-start.7 = (s32[1,512]{1,0:T(1,128)S(1)}, s32[1,512]{1,0:T(1,128)S(1)}, u32[]{:S(2)}, u32[]{:S(2)}) collective-permute-start(s32[1,512]{1,0:T(1,128)S(1)} %join.1.refs_6_), channel_id=1, source_target_pairs={{0,2},{1,3},{2,0},{3,1},{4,6},{5,7},{6,4},{7,5},{8,10},{9,11},{10,... | collective-permute-start | bytes 6152 | tf_op jit(solution)/shard_map/ppermute | solution.py:270
  10.3 6.6 %collective-permute-start.5 = (bf16[576,256]{1,0:T(8,128)(2,1)S(1)}, bf16[576,256]{1,0:T(8,128)(2,1)S(1)}, u32[]{:S(2)}, u32[]{:S(2)}) collective-permute-start(bf16[576,256]{1,0:T(8,128)(2,1)S(1)} %collective-permute-done.4.refs_4_), channel_id=1, source_target_pairs={{0,1},{1,0},{2,3},{3,2},{4,5},{5,4},{6,7},{7,6},{8,9},{9,8},{10,11... | collective-permute-start | bytes 884744 | tf_op jit(solution)/shard_map/ppermute | solution.py:270
  10.3 6.6 %copy-start = (bf16[512,4096]{1,0:T(8,128)(2,1)S(1)}, bf16[512,4096]{1,0:T(8,128)(2,1)}, u32[]{:S(2)}) copy-start(bf16[512,4096]{1,0:T(8,128)(2,1)} %w_ref.3) | copy-start | bytes 12582916
  13.3 2.2 %copy-start.1 = (bf16[512,4096]{1,0:T(8,128)(2,1)S(1)}, bf16[512,4096]{1,0:T(8,128)(2,1)}, u32[]{:S(2)}) copy-start(bf16[512,4096]{1,0:T(8,128)(2,1)} %refs_4_.1) | copy-start | bytes 12582916
  19.3 7.0 %collective-permute-start.10 = (f32[4,4224]{1,0:T(4,128)S(1)}, f32[4,4224]{1,0:T(4,128)S(1)}, u32[]{:S(2)}, u32[]{:S(2)}) collective-permute-start(f32[4,4224]{1,0:T(4,128)S(1)} %get-tuple-element.16), channel_id=1, source_target_pairs={{0,12},{1,13},{2,14},{3,15},{4,8},{5,9},{6,10},{7,11},{8,4},{9,5},... | collective-permute-start | bytes 202760 | tf_op jit(solution)/shard_map/ppermute | solution.py:270
  21.5 6.2 %collective-permute-start.9 = (f32[4,4224]{1,0:T(4,128)S(1)}, f32[4,4224]{1,0:T(4,128)S(1)}, u32[]{:S(2)}, u32[]{:S(2)}) collective-permute-start(f32[4,4224]{1,0:T(4,128)S(1)} %get-tuple-element.15), channel_id=1, source_target_pairs={{0,8},{1,9},{2,10},{3,11},{4,12},{5,13},{6,14},{7,15},{8,0},{9,1},... | collective-permute-start | bytes 202760 | tf_op jit(solution)/shard_map/ppermute | solution.py:270
  23.9 4.7 %collective-permute-start.8 = (f32[4,4224]{1,0:T(4,128)S(1)}, f32[4,4224]{1,0:T(4,128)S(1)}, u32[]{:S(2)}, u32[]{:S(2)}) collective-permute-start(f32[4,4224]{1,0:T(4,128)S(1)} %get-tuple-element.14), channel_id=1, source_target_pairs={{0,4},{1,5},{2,6},{3,7},{4,0},{5,1},{6,2},{7,3},{8,12},{9,13},{10,... | collective-permute-start | bytes 202760 | tf_op jit(solution)/shard_map/ppermute | solution.py:270

commit v5 on v4

--- a/solution.py
+++ b/solution.py
@@ -291,10 +291,11 @@
     for start in range(0, far, 4):
         some = groups[start : start + 4]
         absorbed, turned = absorb(some, w_uk, started)
-        for first in range(len(some) - len(some) % 2, -1, -2):
-            pick = some[first : first + 2]
-            if not pick:
+        cuts = [(1, len(some)), (0, 1)] if start == 0 else [(0, len(some))]
+        for first, end in cuts:
+            if first >= end:
                 continue
+            pick = some[first:end]
             found = attend(where, first, absorbed, turned, pick, w_uv, keys, docs)
             for g, part in enumerate(found):
                 k = start + first + g

time: 29.7 us -> 29.1 us (0.980)
  waiting for transfers between devices: 7.13 us -> 6.74 us
    ppermute x11, waiting for transfers between devices: 7.13 us -> 6.74 us  [swap(): return lax.ppermute(x, 'col', [(i, i ^ mask) for i in range(size)])]
  transfers between devices with their start and end apart: 11 -> 11, of which waited for: 5 -> 5; matrix products, arithmetic and copies ran while one was open for 0% -> 0% of each run, Pallas kernels for 13% -> 11%
where the time goes in v5:
time: 29.1 us; the launch traced here: 29 us
  starting transfers between devices  12.7 us (44%)
  Pallas kernels  7.21 us (25%)
  waiting for transfers between devices  6.74 us (23%)
  local copies, waits for them, and re-layouts  2.21 us (8%)
    ppermute x11, starting transfers between devices, swap(): return lax.ppermute(x, 'col', [(i, i ^ mask) for i in range(size)])  12.7 us
    ppermute x11, waiting for transfers between devices, swap(): return lax.ppermute(x, 'col', [(i, i ^ mask) for i in range(size)])  6.74 us
    pallas_call x2, Pallas kernels, attend(): pl.pallas_call(functools.partial(attend_kernel, near, count, first), out_...  4.78 us
    unnamed x16, local copies, waits for them, and re-layouts  2.21 us
    pallas_call x1, Pallas kernels, absorb(): pl.pallas_call(functools.partial(absorb_kernel, count), out_shape=(jax.Sh...  1.39 us
    pallas_call x1, Pallas kernels, combine(): pl.pallas_call(functools.partial(combine_kernel, len(parts)), out_shape=j...  0.96 us
  transfers between devices with their start and end apart: 11, of which 5 were waited for; matrix products, arithmetic and copies ran while one was open for 0% of the time, Pallas kernels for 11%

profile of v5, /device:TPU:0, one launch (start us, length us, event | category | flops | bytes accessed | tf_op | source)
XLA Modules:
  0.0 29.0 jit_solution(13578670009281488450)
XLA Ops:
  0.0 0.0 copy-start.2
  0.0 0.0 copy-start.6
  0.0 0.0 copy-start.7
  0.0 0.0 copy-start.3
  0.0 0.0 copy-start.4
  0.0 0.0 copy-start.5
  0.0 3.0 %collective-permute-start.4 = (bf16[576,256]{1,0:T(8,128)(2,1)}, bf16[576,256]{1,0:T(8,128)(2,1)S(1)}, u32[]{:S(2)}, u32[]{:S(2)}) collective-permute-start(bf16[576,256]{1,0:T(8,128)(2,1)} %bitcast.5), channel_id=1, source_target_pairs={{0,2},{1,3},{2,0},{3,1},{4,6},{5,7},{6,4},{7,5},{8,10},{9,11},{10,... | collective-permute-start | bytes 884744 | tf_op jit(solution)/shard_map/ppermute | solution.py:270
  3.1 0.0 copy-done.6
  3.1 0.0 copy-done.7
  3.1 0.0 copy-done.3
  3.1 0.0 copy-done.4
  3.1 0.1 pack.1.refs_0_
  3.2 1.6 %collective-permute-start = (bf16[4,6272]{1,0:T(4,128)(2,1)S(1)}, bf16[4,6272]{1,0:T(4,128)(2,1)S(1)}, u32[]{:S(2)}, u32[]{:S(2)}) collective-permute-start(bf16[4,6272]{1,0:T(4,128)(2,1)S(1)} %pack.1.refs_0_), channel_id=1, source_target_pairs={{0,4},{1,5},{2,6},{3,7},{4,0},{5,1},{6,2},{7,3},{8,12},{9,13},{10,... | collective-permute-start | bytes 150536 | tf_op jit(solution)/shard_map/ppermute | solution.py:270
  4.8 0.0 copy-done.5
  4.8 0.0 collective-permute-start.6
  4.8 2.6 %collective-permute-start.1 = (bf16[4,6272]{1,0:T(4,128)(2,1)S(1)}, bf16[4,6272]{1,0:T(4,128)(2,1)S(1)}, u32[]{:S(2)}, u32[]{:S(2)}) collective-permute-start(bf16[4,6272]{1,0:T(4,128)(2,1)S(1)} %pack.1.refs_0_), channel_id=1, source_target_pairs={{0,8},{1,9},{2,10},{3,11},{4,12},{5,13},{6,14},{7,15},{8,0},{9,1},... | collective-permute-start | bytes 150536 | tf_op jit(solution)/shard_map/ppermute | solution.py:270
  7.4 0.2 collective-permute-start.2
  7.6 0.0 collective-permute-done.6.b_ref
  7.6 0.0 copy-done.2
  7.6 0.1 collective-permute-start.3
  7.7 0.0 collective-permute-done.refs_1_.refs_0_
  7.7 0.8 %collective-permute-start.7 = (s32[1,512]{1,0:T(1,128)S(1)}, s32[1,512]{1,0:T(1,128)S(1)}, u32[]{:S(2)}, u32[]{:S(2)}) collective-permute-start(s32[1,512]{1,0:T(1,128)S(1)} %join.1.refs_5_.refs_7_), channel_id=1, source_target_pairs={{0,2},{1,3},{2,0},{3,1},{4,6},{5,7},{6,4},{7,5},{8,10},{9,11},{10,... | collective-permute-start | bytes 6152 | tf_op jit(solution)/shard_map/ppermute | solution.py:270
  8.4 1.8 %collective-permute-done.4.refs_3_.refs_5_ = bf16[576,256]{1,0:T(8,128)(2,1)S(1)} collective-permute-done((bf16[576,256]{1,0:T(8,128)(2,1)}, bf16[576,256]{1,0:T(8,128)(2,1)S(1)}, u32[]{:S(2)}, u32[]{:S(2)}) %collective-permute-start.4) | collective-permute-done | bytes 294944 | tf_op jit(solution)/shard_map/ppermute | solution.py:270
  10.3 0.0 collective-permute-start.5
  10.3 0.0 copy-start
  10.3 0.7 %collective-permute-done.1.refs_2_.refs_1_ = bf16[4,6272]{1,0:T(4,128)(2,1)S(1)} collective-permute-done((bf16[4,6272]{1,0:T(4,128)(2,1)S(1)}, bf16[4,6272]{1,0:T(4,128)(2,1)S(1)}, u32[]{:S(2)}, u32[]{:S(2)}) %collective-permute-start.1) | collective-permute-done | bytes 50208 | tf_op jit(solution)/shard_map/ppermute | solution.py:270
  11.0 2.2 %collective-permute-done.2.refs_3_.refs_2_ = bf16[4,6272]{1,0:T(4,128)(2,1)S(1)} collective-permute-done((bf16[4,6272]{1,0:T(4,128)(2,1)S(1)}, bf16[4,6272]{1,0:T(4,128)(2,1)S(1)}, u32[]{:S(2)}, u32[]{:S(2)}) %collective-permute-start.2) | collective-permute-done | bytes 50208 | tf_op jit(solution)/shard_map/ppermute | solution.py:270
  13.3 0.0 copy-start.1
  13.3 2.2 %copy-done.1 = bf16[512,4096]{1,0:T(8,128)(2,1)S(1)} copy-done((bf16[512,4096]{1,0:T(8,128)(2,1)S(1)}, bf16[512,4096]{1,0:T(8,128)(2,1)}, u32[]{:S(2)}) %copy-start.1) | copy-done | bytes 4194328
  15.4 1.4 %absorb.1 = (bf16[4,256,512]{2,1,0:T(8,128)(2,1)S(1)}, bf16[4,128,128]{2,1,0:T(8,128)(2,1)S(1)}) custom-call(bf16[4,6272]{1,0:T(4,128)(2,1)S(1)} %pack.1.refs_0_, bf16[4,6272]{1,0:T(4,128)(2,1)S(1)} %collective-permute-done.refs_1_.refs_0_, bf16[4,6272]{1,0:T(4,128)(2,1)S(1)} %collective-permute-done.1.refs_2_.refs_1_, ...), custom_call_target="tpu_custom_call" | custom-call | tf_op jit(solution)/shard_map/absorb/pallas_call | solution.py:131
  16.8 0.0 collective-permute-done.7.refs_6_.refs_8_
  16.8 0.0 collective-permute-done.3.refs_2_.refs_4_
  16.9 0.0 collective-permute-done.5.refs_4_.refs_6_
  16.9 0.0 copy-done
  16.9 3.2 %attend.3 = (f32[4,4224]{1,0:T(4,128)S(1)}, f32[4,4224]{1,0:T(4,128)S(1)}, f32[4,4224]{1,0:T(4,128)S(1)}) custom-call(s32[1]{0:T(128)} %bitcast.me_ref, bf16[4,256,512]{2,1,0:T(8,128)(2,1)S(1)} %get-tuple-element.10.a_ref, bf16[4,128,128]{2,1,0:T(8,128)(2,1)S(1)} %get-tuple-element.11.r_ref, bf16[512,4096]{1,0:T(8,128)(2,1)S(1)} %copy-done, ...), custom_call_target="tpu_custom_call" | custom-call | tf_op jit(solution)/shard_map/attend/pallas_call | solution.py:228
  20.1 2.1 %collective-permute-start.10 = (f32[4,4224]{1,0:T(4,128)S(1)}, f32[4,4224]{1,0:T(4,128)S(1)}, u32[]{:S(2)}, u32[]{:S(2)}) collective-permute-start(f32[4,4224]{1,0:T(4,128)S(1)} %get-tuple-element.14), channel_id=1, source_target_pairs={{0,12},{1,13},{2,14},{3,15},{4,8},{5,9},{6,10},{7,11},{8,4},{9,5},... | collective-permute-start | bytes 202760 | tf_op jit(solution)/shard_map/ppermute | solution.py:270
  22.2 0.0 collective-permute-start.8
  22.2 2.3 %collective-permute-start.9 = (f32[4,4224]{1,0:T(4,128)S(1)}, f32[4,4224]{1,0:T(4,128)S(1)}, u32[]{:S(2)}, u32[]{:S(2)}) collective-permute-start(f32[4,4224]{1,0:T(4,128)S(1)} %get-tuple-element.13), channel_id=1, source_target_pairs={{0,8},{1,9},{2,10},{3,11},{4,12},{5,13},{6,14},{7,15},{8,0},{9,1},... | collective-permute-start | bytes 202760 | tf_op jit(solution)/shard_map/ppermute | solution.py:270
  24.5 1.6 %attend.2.refs_0_ = f32[4,4224]{1,0:T(4,128)S(1)} custom-call(s32[1]{0:T(128)} %bitcast.me_ref, bf16[4,256,512]{2,1,0:T(8,128)(2,1)S(1)} %get-tuple-element.10.a_ref, bf16[4,128,128]{2,1,0:T(8,128)(2,1)S(1)} %get-tuple-element.11.r_ref, bf16[512,4096]{1,0:T(8,128)(2,1)S(1)} %copy-done, bf16[4,6272]{1,0:T(4,128)(2,1)S(1)} %pack.1.refs_0_, ...), custom_call_target="tpu_custom_call" | custom-call | tf_op jit(solution)/shard_map/attend/pallas_call | solution.py:228
  26.1 0.4 %collective-permute-done.10.refs_3_ = f32[4,4224]{1,0:T(4,128)S(1)} collective-permute-done((f32[4,4224]{1,0:T(4,128)S(1)}, f32[4,4224]{1,0:T(4,128)S(1)}, u32[]{:S(2)}, u32[]{:S(2)}) %collective-permute-start.10) | collective-permute-done | bytes 67616 | tf_op jit(solution)/shard_map/ppermute | solution.py:270
  26.5 1.6 %collective-permute-done.8.refs_1_ = f32[4,4224]{1,0:T(4,128)S(1)} collective-permute-done((f32[4,4224]{1,0:T(4,128)S(1)}, f32[4,4224]{1,0:T(4,128)S(1)}, u32[]{:S(2)}, u32[]{:S(2)}) %collective-permute-start.8) | collective-permute-done | bytes 67616 | tf_op jit(solution)/shard_map/ppermute | solution.py:270
  28.0 0.0 collective-permute-done.9.refs_2_
  28.0 1.0 %combine.1 = bf16[4,4096]{1,0:T(4,128)(2,1)} custom-call(f32[4,4224]{1,0:T(4,128)S(1)} %attend.2.refs_0_, f32[4,4224]{1,0:T(4,128)S(1)} %collective-permute-done.8.refs_1_, f32[4,4224]{1,0:T(4,128)S(1)} %collective-permute-done.9.refs_2_, f32[4,4224]{1,0:T(4,128)S(1)} %collective-permute-done.10.refs_3_), custom_call_target="tpu_custom_call" | custom-call | tf_op jit(solution)/shard_map/combine/pallas_call | solution.py:254
  (3 shorter events, 0.0 us)
Async XLA Ops:
  0.0 7.6 %copy-start.2 = (bf16[256,576]{0,1:T(8,128)(2,1)S(1)}, bf16[256,576]{0,1:T(8,128)(2,1)}, u32[]{:S(2)}) copy-start(bf16[256,576]{0,1:T(8,128)(2,1)} %param.10) | copy-start | bytes 884740
  0.0 3.1 %copy-start.6 = (s32[4]{0:T(128)S(1)}, s32[4]{0:T(128)}, u32[]{:S(2)}) copy-start(s32[4]{0:T(128)} %param.12) | copy-start | bytes 52
  0.0 3.1 %copy-start.7 = (s32[4]{0:T(128)S(1)}, s32[4]{0:T(128)}, u32[]{:S(2)}) copy-start(s32[4]{0:T(128)} %param.13) | copy-start | bytes 52
  0.0 3.1 %copy-start.3 = (bf16[4,4096]{1,0:T(4,128)(2,1)S(1)}, bf16[4,4096]{1,0:T(4,128)(2,1)}, u32[]{:S(2)}) copy-start(bf16[4,4096]{1,0:T(4,128)(2,1)} %nope_ref.1) | copy-start | bytes 98308
  0.0 3.1 %copy-start.4 = (bf16[4,2048]{1,0:T(4,128)(2,1)S(1)}, bf16[4,2048]{1,0:T(4,128)(2,1)}, u32[]{:S(2)}) copy-start(bf16[4,2048]{1,0:T(4,128)(2,1)} %rope_ref.1) | copy-start | bytes 49156
  0.0 4.7 %copy-start.5 = (s32[256]{0:T(256)S(1)}, s32[256]{0:T(256)}, u32[]{:S(2)}) copy-start(s32[256]{0:T(256)} %param.11) | copy-start | bytes 3076
  0.0 10.3 %collective-permute-start.4 = (bf16[576,256]{1,0:T(8,128)(2,1)}, bf16[576,256]{1,0:T(8,128)(2,1)S(1)}, u32[]{:S(2)}, u32[]{:S(2)}) collective-permute-start(bf16[576,256]{1,0:T(8,128)(2,1)} %bitcast.5), channel_id=1, source_target_pairs={{0,2},{1,3},{2,0},{3,1},{4,6},{5,7},{6,4},{7,5},{8,10},{9,11},{10,... | collective-permute-start | bytes 884744 | tf_op jit(solution)/shard_map/ppermute | solution.py:270
  3.2 4.5 %collective-permute-start = (bf16[4,6272]{1,0:T(4,128)(2,1)S(1)}, bf16[4,6272]{1,0:T(4,128)(2,1)S(1)}, u32[]{:S(2)}, u32[]{:S(2)}) collective-permute-start(bf16[4,6272]{1,0:T(4,128)(2,1)S(1)} %pack.1.refs_0_), channel_id=1, source_target_pairs={{0,4},{1,5},{2,6},{3,7},{4,0},{5,1},{6,2},{7,3},{8,12},{9,13},{10,... | collective-permute-start | bytes 150536 | tf_op jit(solution)/shard_map/ppermute | solution.py:270
  4.8 2.8 %collective-permute-start.6 = (s32[1,256]{1,0:T(1,128)S(1)}, s32[1,256]{1,0:T(1,128)S(1)}, u32[]{:S(2)}, u32[]{:S(2)}) collective-permute-start(s32[1,256]{1,0:T(1,128)S(1)} %bitcast.9), channel_id=1, source_target_pairs={{0,1},{1,0},{2,3},{3,2},{4,5},{5,4},{6,7},{7,6},{8,9},{9,8},{10,11... | collective-permute-start | bytes 3080 | tf_op jit(solution)/shard_map/ppermute | solution.py:270
  4.8 6.3 %collective-permute-start.1 = (bf16[4,6272]{1,0:T(4,128)(2,1)S(1)}, bf16[4,6272]{1,0:T(4,128)(2,1)S(1)}, u32[]{:S(2)}, u32[]{:S(2)}) collective-permute-start(bf16[4,6272]{1,0:T(4,128)(2,1)S(1)} %pack.1.refs_0_), channel_id=1, source_target_pairs={{0,8},{1,9},{2,10},{3,11},{4,12},{5,13},{6,14},{7,15},{8,0},{9,1},... | collective-permute-start | bytes 150536 | tf_op jit(solution)/shard_map/ppermute | solution.py:270
  7.4 5.9 %collective-permute-start.2 = (bf16[4,6272]{1,0:T(4,128)(2,1)S(1)}, bf16[4,6272]{1,0:T(4,128)(2,1)S(1)}, u32[]{:S(2)}, u32[]{:S(2)}) collective-permute-start(bf16[4,6272]{1,0:T(4,128)(2,1)S(1)} %pack.1.refs_0_), channel_id=1, source_target_pairs={{0,12},{1,13},{2,14},{3,15},{4,8},{5,9},{6,10},{7,11},{8,4},{9,5},... | collective-permute-start | bytes 150536 | tf_op jit(solution)/shard_map/ppermute | solution.py:270
  7.6 9.3 %collective-permute-start.3 = (bf16[576,256]{1,0:T(8,128)(2,1)S(1)}, bf16[576,256]{1,0:T(8,128)(2,1)S(1)}, u32[]{:S(2)}, u32[]{:S(2)}) collective-permute-start(bf16[576,256]{1,0:T(8,128)(2,1)S(1)} %bitcast.6), channel_id=1, source_target_pairs={{0,1},{1,0},{2,3},{3,2},{4,5},{5,4},{6,7},{7,6},{8,9},{9,8},{10,11... | collective-permute-start | bytes 884744 | tf_op jit(solution)/shard_map/ppermute | solution.py:270
  7.7 9.2 %collective-permute-start.7 = (s32[1,512]{1,0:T(1,128)S(1)}, s32[1,512]{1,0:T(1,128)S(1)}, u32[]{:S(2)}, u32[]{:S(2)}) collective-permute-start(s32[1,512]{1,0:T(1,128)S(1)} %join.1.refs_5_.refs_7_), channel_id=1, source_target_pairs={{0,2},{1,3},{2,0},{3,1},{4,6},{5,7},{6,4},{7,5},{8,10},{9,11},{10,... | collective-permute-start | bytes 6152 | tf_op jit(solution)/shard_map/ppermute | solution.py:270
  10.3 6.6 %collective-permute-start.5 = (bf16[576,256]{1,0:T(8,128)(2,1)S(1)}, bf16[576,256]{1,0:T(8,128)(2,1)S(1)}, u32[]{:S(2)}, u32[]{:S(2)}) collective-permute-start(bf16[576,256]{1,0:T(8,128)(2,1)S(1)} %collective-permute-done.4.refs_3_.refs_5_), channel_id=1, source_target_pairs={{0,1},{1,0},{2,3},{3,2},{4,5},{5,4},{6,7},{7,6},{8,9},{9,8},{10,11... | collective-permute-start | bytes 884744 | tf_op jit(solution)/shard_map/ppermute | solution.py:270
  10.3 6.6 %copy-start = (bf16[512,4096]{1,0:T(8,128)(2,1)S(1)}, bf16[512,4096]{1,0:T(8,128)(2,1)}, u32[]{:S(2)}) copy-start(bf16[512,4096]{1,0:T(8,128)(2,1)} %w_ref.3) | copy-start | bytes 12582916
  13.3 2.2 %copy-start.1 = (bf16[512,4096]{1,0:T(8,128)(2,1)S(1)}, bf16[512,4096]{1,0:T(8,128)(2,1)}, u32[]{:S(2)}) copy-start(bf16[512,4096]{1,0:T(8,128)(2,1)} %refs_4_.1) | copy-start | bytes 12582916
  20.1 6.4 %collective-permute-start.10 = (f32[4,4224]{1,0:T(4,128)S(1)}, f32[4,4224]{1,0:T(4,128)S(1)}, u32[]{:S(2)}, u32[]{:S(2)}) collective-permute-start(f32[4,4224]{1,0:T(4,128)S(1)} %get-tuple-element.14), channel_id=1, source_target_pairs={{0,12},{1,13},{2,14},{3,15},{4,8},{5,9},{6,10},{7,11},{8,4},{9,5},... | collective-permute-start | bytes 202760 | tf_op jit(solution)/shard_map/ppermute | solution.py:270
  22.2 5.9 %collective-permute-start.8 = (f32[4,4224]{1,0:T(4,128)S(1)}, f32[4,4224]{1,0:T(4,128)S(1)}, u32[]{:S(2)}, u32[]{:S(2)}) collective-permute-start(f32[4,4224]{1,0:T(4,128)S(1)} %get-tuple-element.12), channel_id=1, source_target_pairs={{0,4},{1,5},{2,6},{3,7},{4,0},{5,1},{6,2},{7,3},{8,12},{9,13},{10,... | collective-permute-start | bytes 202760 | tf_op jit(solution)/shard_map/ppermute | solution.py:270
  22.2 5.9 %collective-permute-start.9 = (f32[4,4224]{1,0:T(4,128)S(1)}, f32[4,4224]{1,0:T(4,128)S(1)}, u32[]{:S(2)}, u32[]{:S(2)}) collective-permute-start(f32[4,4224]{1,0:T(4,128)S(1)} %get-tuple-element.13), channel_id=1, source_target_pairs={{0,8},{1,9},{2,10},{3,11},{4,12},{5,13},{6,14},{7,15},{8,0},{9,1},... | collective-permute-start | bytes 202760 | tf_op jit(solution)/shard_map/ppermute | solution.py:270

commit v6 on v5

--- a/solution.py
+++ b/solution.py
@@ -235,19 +235,50 @@
     )(me, absorbed, turned, w_uv, *queries, *keys, *docs)
 
 
-def combine_kernel(count, *refs):
-    parts, out_ref = refs[:count], refs[count]
+def weigh(parts):
     stats = [p[:, H * DV :] for p in parts]
     maxima = [s[:, :H] for s in stats]
     top = functools.reduce(jnp.maximum, maxima)
     factors = [jnp.exp(m - top) for m in maxima]
     total = functools.reduce(jnp.add, [f * s[:, H : 2 * H] for f, s in zip(factors, stats)])
+    return top, factors, total
+
+
+def blend(parts, factors, head):
+    lane = (head % 2) * PAIRS + head // 2
+    cols = slice(head * DV, (head + 1) * DV)
+    return functools.reduce(
+        jnp.add, [p[:, cols] * f[:, lane : lane + 1] for p, f in zip(parts, factors)]
+    )
+
+
+def merge_kernel(count, *refs):
+    parts, out_ref = refs[:count], refs[count]
+    top, factors, total = weigh(parts)
+    for head in range(H):
+        out_ref[:, head * DV : (head + 1) * DV] = blend(parts, factors, head)
+    rest = jnp.zeros((out_ref.shape[0], META - 2 * H), jnp.float32)
+    out_ref[:, H * DV :] = jnp.concatenate([top, total, rest], axis=1)
+
+
+def merge(parts):
+    return pl.pallas_call(
+        functools.partial(merge_kernel, len(parts)),
+        out_shape=jax.ShapeDtypeStruct(parts[0].shape, jnp.float32),
+        in_specs=[VMEM] * len(parts),
+        out_specs=VMEM,
+        compiler_params=PARAMS,
+        name="merge",
+    )(*parts)
+
+
+def combine_kernel(count, *refs):
+    parts, out_ref = refs[:count], refs[count]
+    _, factors, total = weigh(parts)
     factors = [f / total for f in factors]
     for head in range(H):
-        cols = slice(head * DV, (head + 1) * DV)
-        lane = (head % 2) * PAIRS + head // 2
-        terms = [p[:, cols] * f[:, lane : lane + 1] for p, f in zip(parts, factors)]
-        out_ref[:, cols] = functools.reduce(jnp.add, terms).astype(out_ref.dtype)
+        value = blend(parts, factors, head)
+        out_ref[:, head * DV : (head + 1) * DV] = value.astype(out_ref.dtype)
 
 
 def combine(parts):
@@ -291,7 +322,7 @@
     for start in range(0, far, 4):
         some = groups[start : start + 4]
         absorbed, turned = absorb(some, w_uk, started)
-        cuts = [(1, len(some)), (0, 1)] if start == 0 else [(0, len(some))]
+        cuts = [(2, len(some)), (1, 2), (0, 1)] if start == 0 else [(0, len(some))]
         for first, end in cuts:
             if first >= end:
                 continue
@@ -300,6 +331,8 @@
             for g, part in enumerate(found):
                 k = start + first + g
                 parts[k] = part if k == 0 else swap(part, near * k)
+    if far > 2:
+        parts = [merge(parts[:1] + parts[2:]), parts[1]]
     return combine(parts)
 
 

time: 29.1 us -> 29 us (level)
  Pallas kernels: 7.21 us -> 8.22 us
  starting transfers between devices: 12.7 us -> 11.9 us
    ppermute x11, starting transfers between devices: 12.7 us -> 11.9 us  [swap(): return lax.ppermute(x, 'col', [(i, i ^ mask) for i in range(size)])]
    pallas_call x2 -> x3, Pallas kernels: 4.78 us -> 5.65 us  [attend(): pl.pallas_call(functools.partial(attend_kernel, near, count, first), out_...]
  transfers between devices with their start and end apart: 11 -> 11, of which waited for: 5 -> 5; matrix products, arithmetic and copies ran while one was open for 0% -> 0% of each run, Pallas kernels for 11% -> 17%
where the time goes in v6:
time: 29 us; the launch traced here: 28.9 us
  starting transfers between devices  11.9 us (41%)
  Pallas kernels  8.22 us (28%)
  waiting for transfers between devices  6.5 us (22%)
  local copies, waits for them, and re-layouts  2.21 us (8%)
    ppermute x11, starting transfers between devices, swap(): return lax.ppermute(x, 'col', [(i, i ^ mask) for i in range(size)])  11.9 us
    ppermute x11, waiting for transfers between devices, swap(): return lax.ppermute(x, 'col', [(i, i ^ mask) for i in range(size)])  6.5 us
    pallas_call x3, Pallas kernels, attend(): pl.pallas_call(functools.partial(attend_kernel, near, count, first), out_...  5.65 us
    unnamed x16, local copies, waits for them, and re-layouts  2.21 us
    pallas_call x1, Pallas kernels, absorb(): pl.pallas_call(functools.partial(absorb_kernel, count), out_shape=(jax.Sh...  1.39 us
    pallas_call x1, Pallas kernels, combine(): pl.pallas_call(functools.partial(combine_kernel, len(parts)), out_shape=j...  0.87 us
  transfers between devices with their start and end apart: 11, of which 5 were waited for; matrix products, arithmetic and copies ran while one was open for 0% of the time, Pallas kernels for 17%

profile of v6, /device:TPU:0, one launch (start us, length us, event | category | flops | bytes accessed | tf_op | source)
XLA Modules:
  0.0 28.9 jit_solution(14147247210395650181)
XLA Ops:
  0.0 0.0 copy-start.2
  0.0 0.0 copy-start.6
  0.0 0.0 copy-start.7
  0.0 0.0 copy-start.3
  0.0 0.0 copy-start.4
  0.0 0.0 copy-start.5
  0.0 3.0 %collective-permute-start.4 = (bf16[576,256]{1,0:T(8,128)(2,1)}, bf16[576,256]{1,0:T(8,128)(2,1)S(1)}, u32[]{:S(2)}, u32[]{:S(2)}) collective-permute-start(bf16[576,256]{1,0:T(8,128)(2,1)} %bitcast.5), channel_id=1, source_target_pairs={{0,2},{1,3},{2,0},{3,1},{4,6},{5,7},{6,4},{7,5},{8,10},{9,11},{10,... | collective-permute-start | bytes 884744 | tf_op jit(solution)/shard_map/ppermute | solution.py:301
  3.1 0.0 copy-done.6
  3.1 0.0 copy-done.7
  3.1 0.0 copy-done.3
  3.1 0.0 copy-done.4
  3.1 0.1 pack.1.refs_0_
  3.2 1.6 %collective-permute-start = (bf16[4,6272]{1,0:T(4,128)(2,1)S(1)}, bf16[4,6272]{1,0:T(4,128)(2,1)S(1)}, u32[]{:S(2)}, u32[]{:S(2)}) collective-permute-start(bf16[4,6272]{1,0:T(4,128)(2,1)S(1)} %pack.1.refs_0_), channel_id=1, source_target_pairs={{0,4},{1,5},{2,6},{3,7},{4,0},{5,1},{6,2},{7,3},{8,12},{9,13},{10,... | collective-permute-start | bytes 150536 | tf_op jit(solution)/shard_map/ppermute | solution.py:301
  4.8 0.0 copy-done.5
  4.8 0.0 collective-permute-start.6
  4.8 2.6 %collective-permute-start.1 = (bf16[4,6272]{1,0:T(4,128)(2,1)S(1)}, bf16[4,6272]{1,0:T(4,128)(2,1)S(1)}, u32[]{:S(2)}, u32[]{:S(2)}) collective-permute-start(bf16[4,6272]{1,0:T(4,128)(2,1)S(1)} %pack.1.refs_0_), channel_id=1, source_target_pairs={{0,8},{1,9},{2,10},{3,11},{4,12},{5,13},{6,14},{7,15},{8,0},{9,1},... | collective-permute-start | bytes 150536 | tf_op jit(solution)/shard_map/ppermute | solution.py:301
  7.4 0.2 collective-permute-start.2
  7.6 0.0 collective-permute-done.6.b_ref
  7.6 0.0 copy-done.2
  7.6 0.1 collective-permute-start.3
  7.7 0.0 collective-permute-done.refs_1_.refs_0_
  7.7 0.8 %collective-permute-start.7 = (s32[1,512]{1,0:T(1,128)S(1)}, s32[1,512]{1,0:T(1,128)S(1)}, u32[]{:S(2)}, u32[]{:S(2)}) collective-permute-start(s32[1,512]{1,0:T(1,128)S(1)} %join.1.refs_5_.refs_6_), channel_id=1, source_target_pairs={{0,2},{1,3},{2,0},{3,1},{4,6},{5,7},{6,4},{7,5},{8,10},{9,11},{10,... | collective-permute-start | bytes 6152 | tf_op jit(solution)/shard_map/ppermute | solution.py:301
  8.4 1.8 %collective-permute-done.4.refs_3_.refs_4_ = bf16[576,256]{1,0:T(8,128)(2,1)S(1)} collective-permute-done((bf16[576,256]{1,0:T(8,128)(2,1)}, bf16[576,256]{1,0:T(8,128)(2,1)S(1)}, u32[]{:S(2)}, u32[]{:S(2)}) %collective-permute-start.4) | collective-permute-done | bytes 294944 | tf_op jit(solution)/shard_map/ppermute | solution.py:301
  10.3 0.0 collective-permute-start.5
  10.3 0.0 copy-start
  10.3 0.7 %collective-permute-done.1.refs_2_.refs_0_ = bf16[4,6272]{1,0:T(4,128)(2,1)S(1)} collective-permute-done((bf16[4,6272]{1,0:T(4,128)(2,1)S(1)}, bf16[4,6272]{1,0:T(4,128)(2,1)S(1)}, u32[]{:S(2)}, u32[]{:S(2)}) %collective-permute-start.1) | collective-permute-done | bytes 50208 | tf_op jit(solution)/shard_map/ppermute | solution.py:301
  11.0 2.2 %collective-permute-done.2.refs_3_.refs_1_ = bf16[4,6272]{1,0:T(4,128)(2,1)S(1)} collective-permute-done((bf16[4,6272]{1,0:T(4,128)(2,1)S(1)}, bf16[4,6272]{1,0:T(4,128)(2,1)S(1)}, u32[]{:S(2)}, u32[]{:S(2)}) %collective-permute-start.2) | collective-permute-done | bytes 50208 | tf_op jit(solution)/shard_map/ppermute | solution.py:301
  13.3 0.0 copy-start.1
  13.3 2.2 %copy-done.1 = bf16[512,4096]{1,0:T(8,128)(2,1)S(1)} copy-done((bf16[512,4096]{1,0:T(8,128)(2,1)S(1)}, bf16[512,4096]{1,0:T(8,128)(2,1)}, u32[]{:S(2)}) %copy-start.1) | copy-done | bytes 4194328
  15.4 1.4 %absorb.1 = (bf16[4,256,512]{2,1,0:T(8,128)(2,1)S(1)}, bf16[4,128,128]{2,1,0:T(8,128)(2,1)S(1)}) custom-call(bf16[4,6272]{1,0:T(4,128)(2,1)S(1)} %pack.1.refs_0_, bf16[4,6272]{1,0:T(4,128)(2,1)S(1)} %collective-permute-done.refs_1_.refs_0_, bf16[4,6272]{1,0:T(4,128)(2,1)S(1)} %collective-permute-done.1.refs_2_.refs_0_, ...), custom_call_target="tpu_custom_call" | custom-call | tf_op jit(solution)/shard_map/absorb/pallas_call | solution.py:131
  16.8 0.0 collective-permute-done.7.refs_6_.refs_7_
  16.8 0.0 collective-permute-done.3.refs_2_.refs_3_
  16.9 0.0 collective-permute-done.5.refs_4_.refs_5_
  16.9 0.0 copy-done
  16.9 2.4 %attend.4 = (f32[4,4224]{1,0:T(4,128)S(1)}, f32[4,4224]{1,0:T(4,128)S(1)}) custom-call(s32[1]{0:T(128)} %bitcast.me_ref, bf16[4,256,512]{2,1,0:T(8,128)(2,1)S(1)} %get-tuple-element.9.a_ref, bf16[4,128,128]{2,1,0:T(8,128)(2,1)S(1)} %get-tuple-element.10.r_ref, bf16[512,4096]{1,0:T(8,128)(2,1)S(1)} %copy-done, ...), custom_call_target="tpu_custom_call" | custom-call | tf_op jit(solution)/shard_map/attend/pallas_call | solution.py:228
  19.3 1.5 %collective-permute-start.8 = (f32[4,4224]{1,0:T(4,128)S(1)}, f32[4,4224]{1,0:T(4,128)S(1)}, u32[]{:S(2)}, u32[]{:S(2)}) collective-permute-start(f32[4,4224]{1,0:T(4,128)S(1)} %get-tuple-element.11), channel_id=1, source_target_pairs={{0,8},{1,9},{2,10},{3,11},{4,12},{5,13},{6,14},{7,15},{8,0},{9,1},... | collective-permute-start | bytes 202760 | tf_op jit(solution)/shard_map/ppermute | solution.py:301
  20.8 0.7 %collective-permute-start.9 = (f32[4,4224]{1,0:T(4,128)S(1)}, f32[4,4224]{1,0:T(4,128)S(1)}, u32[]{:S(2)}, u32[]{:S(2)}) collective-permute-start(f32[4,4224]{1,0:T(4,128)S(1)} %get-tuple-element.12), channel_id=1, source_target_pairs={{0,12},{1,13},{2,14},{3,15},{4,8},{5,9},{6,10},{7,11},{8,4},{9,5},... | collective-permute-start | bytes 202760 | tf_op jit(solution)/shard_map/ppermute | solution.py:301
  21.5 1.6 %attend.5 = f32[4,4224]{1,0:T(4,128)S(1)} custom-call(s32[1]{0:T(128)} %bitcast.me_ref, bf16[4,256,512]{2,1,0:T(8,128)(2,1)S(1)} %get-tuple-element.9.a_ref, bf16[4,128,128]{2,1,0:T(8,128)(2,1)S(1)} %get-tuple-element.10.r_ref, bf16[512,4096]{1,0:T(8,128)(2,1)S(1)} %copy-done, bf16[4,6272]{1,0:T(4,128)(2,1)S(1)} %collective-permute-done.refs_1_.refs_0_, ...), custom_call_target="tpu_custom_call" | custom-call | tf_op jit(solution)/shard_map/attend/pallas_call | solution.py:228
  23.1 1.4 %collective-permute-start.10 = (f32[4,4224]{1,0:T(4,128)S(1)}, f32[4,4224]{1,0:T(4,128)S(1)}, u32[]{:S(2)}, u32[]{:S(2)}) collective-permute-start(f32[4,4224]{1,0:T(4,128)S(1)} %attend.5), channel_id=1, source_target_pairs={{0,4},{1,5},{2,6},{3,7},{4,0},{5,1},{6,2},{7,3},{8,12},{9,13},{10,... | collective-permute-start | bytes 202760 | tf_op jit(solution)/shard_map/ppermute | solution.py:301
  24.5 1.6 %attend.3.refs_0_ = f32[4,4224]{1,0:T(4,128)S(1)} custom-call(s32[1]{0:T(128)} %bitcast.me_ref, bf16[4,256,512]{2,1,0:T(8,128)(2,1)S(1)} %get-tuple-element.9.a_ref, bf16[4,128,128]{2,1,0:T(8,128)(2,1)S(1)} %get-tuple-element.10.r_ref, bf16[512,4096]{1,0:T(8,128)(2,1)S(1)} %copy-done, bf16[4,6272]{1,0:T(4,128)(2,1)S(1)} %pack.1.refs_0_, ...), custom_call_target="tpu_custom_call" | custom-call | tf_op jit(solution)/shard_map/attend/pallas_call | solution.py:228
  26.1 0.0 collective-permute-done.8.refs_1_
  26.1 1.1 %collective-permute-done.9.refs_2_ = f32[4,4224]{1,0:T(4,128)S(1)} collective-permute-done((f32[4,4224]{1,0:T(4,128)S(1)}, f32[4,4224]{1,0:T(4,128)S(1)}, u32[]{:S(2)}, u32[]{:S(2)}) %collective-permute-start.9) | collective-permute-done | bytes 67616 | tf_op jit(solution)/shard_map/ppermute | solution.py:301
  27.3 0.2 merge.1.refs_0_
  27.5 0.5 %collective-permute-done.10.refs_1_ = f32[4,4224]{1,0:T(4,128)S(1)} collective-permute-done((f32[4,4224]{1,0:T(4,128)S(1)}, f32[4,4224]{1,0:T(4,128)S(1)}, u32[]{:S(2)}, u32[]{:S(2)}) %collective-permute-start.10) | collective-permute-done | bytes 67616 | tf_op jit(solution)/shard_map/ppermute | solution.py:301
  28.0 0.9 %combine.1 = bf16[4,4096]{1,0:T(4,128)(2,1)} custom-call(f32[4,4224]{1,0:T(4,128)S(1)} %merge.1.refs_0_, f32[4,4224]{1,0:T(4,128)S(1)} %collective-permute-done.10.refs_1_), custom_call_target="tpu_custom_call" | custom-call | tf_op jit(solution)/shard_map/combine/pallas_call | solution.py:285
  (3 shorter events, 0.0 us)
Async XLA Ops:
  0.0 7.6 %copy-start.2 = (bf16[256,576]{0,1:T(8,128)(2,1)S(1)}, bf16[256,576]{0,1:T(8,128)(2,1)}, u32[]{:S(2)}) copy-start(bf16[256,576]{0,1:T(8,128)(2,1)} %param.10) | copy-start | bytes 884740
  0.0 3.1 %copy-start.6 = (s32[4]{0:T(128)S(1)}, s32[4]{0:T(128)}, u32[]{:S(2)}) copy-start(s32[4]{0:T(128)} %param.12) | copy-start | bytes 52
  0.0 3.1 %copy-start.7 = (s32[4]{0:T(128)S(1)}, s32[4]{0:T(128)}, u32[]{:S(2)}) copy-start(s32[4]{0:T(128)} %param.13) | copy-start | bytes 52
  0.0 3.1 %copy-start.3 = (bf16[4,4096]{1,0:T(4,128)(2,1)S(1)}, bf16[4,4096]{1,0:T(4,128)(2,1)}, u32[]{:S(2)}) copy-start(bf16[4,4096]{1,0:T(4,128)(2,1)} %nope_ref.1) | copy-start | bytes 98308
  0.0 3.1 %copy-start.4 = (bf16[4,2048]{1,0:T(4,128)(2,1)S(1)}, bf16[4,2048]{1,0:T(4,128)(2,1)}, u32[]{:S(2)}) copy-start(bf16[4,2048]{1,0:T(4,128)(2,1)} %rope_ref.1) | copy-start | bytes 49156
  0.0 4.7 %copy-start.5 = (s32[256]{0:T(256)S(1)}, s32[256]{0:T(256)}, u32[]{:S(2)}) copy-start(s32[256]{0:T(256)} %param.11) | copy-start | bytes 3076
  0.0 10.3 %collective-permute-start.4 = (bf16[576,256]{1,0:T(8,128)(2,1)}, bf16[576,256]{1,0:T(8,128)(2,1)S(1)}, u32[]{:S(2)}, u32[]{:S(2)}) collective-permute-start(bf16[576,256]{1,0:T(8,128)(2,1)} %bitcast.5), channel_id=1, source_target_pairs={{0,2},{1,3},{2,0},{3,1},{4,6},{5,7},{6,4},{7,5},{8,10},{9,11},{10,... | collective-permute-start | bytes 884744 | tf_op jit(solution)/shard_map/ppermute | solution.py:301
  3.2 4.5 %collective-permute-start = (bf16[4,6272]{1,0:T(4,128)(2,1)S(1)}, bf16[4,6272]{1,0:T(4,128)(2,1)S(1)}, u32[]{:S(2)}, u32[]{:S(2)}) collective-permute-start(bf16[4,6272]{1,0:T(4,128)(2,1)S(1)} %pack.1.refs_0_), channel_id=1, source_target_pairs={{0,4},{1,5},{2,6},{3,7},{4,0},{5,1},{6,2},{7,3},{8,12},{9,13},{10,... | collective-permute-start | bytes 150536 | tf_op jit(solution)/shard_map/ppermute | solution.py:301
  4.8 2.8 %collective-permute-start.6 = (s32[1,256]{1,0:T(1,128)S(1)}, s32[1,256]{1,0:T(1,128)S(1)}, u32[]{:S(2)}, u32[]{:S(2)}) collective-permute-start(s32[1,256]{1,0:T(1,128)S(1)} %bitcast.10), channel_id=1, source_target_pairs={{0,1},{1,0},{2,3},{3,2},{4,5},{5,4},{6,7},{7,6},{8,9},{9,8},{10,11... | collective-permute-start | bytes 3080 | tf_op jit(solution)/shard_map/ppermute | solution.py:301
  4.8 6.3 %collective-permute-start.1 = (bf16[4,6272]{1,0:T(4,128)(2,1)S(1)}, bf16[4,6272]{1,0:T(4,128)(2,1)S(1)}, u32[]{:S(2)}, u32[]{:S(2)}) collective-permute-start(bf16[4,6272]{1,0:T(4,128)(2,1)S(1)} %pack.1.refs_0_), channel_id=1, source_target_pairs={{0,8},{1,9},{2,10},{3,11},{4,12},{5,13},{6,14},{7,15},{8,0},{9,1},... | collective-permute-start | bytes 150536 | tf_op jit(solution)/shard_map/ppermute | solution.py:301
  7.4 5.9 %collective-permute-start.2 = (bf16[4,6272]{1,0:T(4,128)(2,1)S(1)}, bf16[4,6272]{1,0:T(4,128)(2,1)S(1)}, u32[]{:S(2)}, u32[]{:S(2)}) collective-permute-start(bf16[4,6272]{1,0:T(4,128)(2,1)S(1)} %pack.1.refs_0_), channel_id=1, source_target_pairs={{0,12},{1,13},{2,14},{3,15},{4,8},{5,9},{6,10},{7,11},{8,4},{9,5},... | collective-permute-start | bytes 150536 | tf_op jit(solution)/shard_map/ppermute | solution.py:301
  7.6 9.3 %collective-permute-start.3 = (bf16[576,256]{1,0:T(8,128)(2,1)S(1)}, bf16[576,256]{1,0:T(8,128)(2,1)S(1)}, u32[]{:S(2)}, u32[]{:S(2)}) collective-permute-start(bf16[576,256]{1,0:T(8,128)(2,1)S(1)} %bitcast.6), channel_id=1, source_target_pairs={{0,1},{1,0},{2,3},{3,2},{4,5},{5,4},{6,7},{7,6},{8,9},{9,8},{10,11... | collective-permute-start | bytes 884744 | tf_op jit(solution)/shard_map/ppermute | solution.py:301
  7.7 9.2 %collective-permute-start.7 = (s32[1,512]{1,0:T(1,128)S(1)}, s32[1,512]{1,0:T(1,128)S(1)}, u32[]{:S(2)}, u32[]{:S(2)}) collective-permute-start(s32[1,512]{1,0:T(1,128)S(1)} %join.1.refs_5_.refs_6_), channel_id=1, source_target_pairs={{0,2},{1,3},{2,0},{3,1},{4,6},{5,7},{6,4},{7,5},{8,10},{9,11},{10,... | collective-permute-start | bytes 6152 | tf_op jit(solution)/shard_map/ppermute | solution.py:301
  10.3 6.6 %collective-permute-start.5 = (bf16[576,256]{1,0:T(8,128)(2,1)S(1)}, bf16[576,256]{1,0:T(8,128)(2,1)S(1)}, u32[]{:S(2)}, u32[]{:S(2)}) collective-permute-start(bf16[576,256]{1,0:T(8,128)(2,1)S(1)} %collective-permute-done.4.refs_3_.refs_4_), channel_id=1, source_target_pairs={{0,1},{1,0},{2,3},{3,2},{4,5},{5,4},{6,7},{7,6},{8,9},{9,8},{10,11... | collective-permute-start | bytes 884744 | tf_op jit(solution)/shard_map/ppermute | solution.py:301
  10.3 6.6 %copy-start = (bf16[512,4096]{1,0:T(8,128)(2,1)S(1)}, bf16[512,4096]{1,0:T(8,128)(2,1)}, u32[]{:S(2)}) copy-start(bf16[512,4096]{1,0:T(8,128)(2,1)} %w_ref.5) | copy-start | bytes 12582916
  13.3 2.2 %copy-start.1 = (bf16[512,4096]{1,0:T(8,128)(2,1)S(1)}, bf16[512,4096]{1,0:T(8,128)(2,1)}, u32[]{:S(2)}) copy-start(bf16[512,4096]{1,0:T(8,128)(2,1)} %refs_4_.1) | copy-start | bytes 12582916
  19.3 6.8 %collective-permute-start.8 = (f32[4,4224]{1,0:T(4,128)S(1)}, f32[4,4224]{1,0:T(4,128)S(1)}, u32[]{:S(2)}, u32[]{:S(2)}) collective-permute-start(f32[4,4224]{1,0:T(4,128)S(1)} %get-tuple-element.11), channel_id=1, source_target_pairs={{0,8},{1,9},{2,10},{3,11},{4,12},{5,13},{6,14},{7,15},{8,0},{9,1},... | collective-permute-start | bytes 202760 | tf_op jit(solution)/shard_map/ppermute | solution.py:301
  20.8 6.5 %collective-permute-start.9 = (f32[4,4224]{1,0:T(4,128)S(1)}, f32[4,4224]{1,0:T(4,128)S(1)}, u32[]{:S(2)}, u32[]{:S(2)}) collective-permute-start(f32[4,4224]{1,0:T(4,128)S(1)} %get-tuple-element.12), channel_id=1, source_target_pairs={{0,12},{1,13},{2,14},{3,15},{4,8},{5,9},{6,10},{7,11},{8,4},{9,5},... | collective-permute-start | bytes 202760 | tf_op jit(solution)/shard_map/ppermute | solution.py:301
  23.1 4.9 %collective-permute-start.10 = (f32[4,4224]{1,0:T(4,128)S(1)}, f32[4,4224]{1,0:T(4,128)S(1)}, u32[]{:S(2)}, u32[]{:S(2)}) collective-permute-start(f32[4,4224]{1,0:T(4,128)S(1)} %attend.5), channel_id=1, source_target_pairs={{0,4},{1,5},{2,6},{3,7},{4,0},{5,1},{6,2},{7,3},{8,12},{9,13},{10,... | collective-permute-start | bytes 202760 | tf_op jit(solution)/shard_map/ppermute | solution.py:301

commit v7 on v6

--- a/solution.py
+++ b/solution.py
@@ -247,9 +247,16 @@
 def blend(parts, factors, head):
     lane = (head % 2) * PAIRS + head // 2
     cols = slice(head * DV, (head + 1) * DV)
-    return functools.reduce(
-        jnp.add, [p[:, cols] * f[:, lane : lane + 1] for p, f in zip(parts, factors)]
-    )
+    rows = parts[0].shape[0]
+    found = None
+    for i in range(0, len(parts), 2):
+        pair = jnp.concatenate([p[:, cols] for p in parts[i : i + 2]], axis=0)
+        factor = jnp.concatenate(factors[i : i + 2], axis=0)[:, lane : lane + 1]
+        term = pair * factor
+        halves = [term[j : j + rows] for j in range(0, term.shape[0], rows)]
+        term = functools.reduce(jnp.add, halves)
+        found = term if found is None else found + term
+    return found
 
 
 def merge_kernel(count, *refs):

time: 29 us -> 29 us (level)
  no operation moved by 1% of the time
where the time goes in v7:
time: 29 us; the launch traced here: 28.9 us
  starting transfers between devices  11.9 us (41%)
  Pallas kernels  8.13 us (28%)
  waiting for transfers between devices  6.54 us (23%)
  local copies, waits for them, and re-layouts  2.21 us (8%)
    ppermute x11, starting transfers between devices, swap(): return lax.ppermute(x, 'col', [(i, i ^ mask) for i in range(size)])  11.9 us
    ppermute x11, waiting for transfers between devices, swap(): return lax.ppermute(x, 'col', [(i, i ^ mask) for i in range(size)])  6.54 us
    pallas_call x3, Pallas kernels, attend(): pl.pallas_call(functools.partial(attend_kernel, near, count, first), out_...  5.65 us
    unnamed x16, local copies, waits for them, and re-layouts  2.21 us
    pallas_call x1, Pallas kernels, absorb(): pl.pallas_call(functools.partial(absorb_kernel, count), out_shape=(jax.Sh...  1.39 us
    pallas_call x1, Pallas kernels, combine(): pl.pallas_call(functools.partial(combine_kernel, len(parts)), out_shape=j...  0.82 us
  transfers between devices with their start and end apart: 11, of which 5 were waited for; matrix products, arithmetic and copies ran while one was open for 0% of the time, Pallas kernels for 17%

profile of v7, /device:TPU:0, one launch (start us, length us, event | category | flops | bytes accessed | tf_op | source)
XLA Modules:
  0.0 28.9 jit_solution(14312758655914529395)
XLA Ops:
  0.0 0.0 copy-start.2
  0.0 0.0 copy-start.6
  0.0 0.0 copy-start.7
  0.0 0.0 copy-start.3
  0.0 0.0 copy-start.4
  0.0 0.0 copy-start.5
  0.0 3.0 %collective-permute-start.4 = (bf16[576,256]{1,0:T(8,128)(2,1)}, bf16[576,256]{1,0:T(8,128)(2,1)S(1)}, u32[]{:S(2)}, u32[]{:S(2)}) collective-permute-start(bf16[576,256]{1,0:T(8,128)(2,1)} %bitcast.5), channel_id=1, source_target_pairs={{0,2},{1,3},{2,0},{3,1},{4,6},{5,7},{6,4},{7,5},{8,10},{9,11},{10,... | collective-permute-start | bytes 884744 | tf_op jit(solution)/shard_map/ppermute | solution.py:308
  3.1 0.0 copy-done.6
  3.1 0.0 copy-done.7
  3.1 0.0 copy-done.3
  3.1 0.0 copy-done.4
  3.1 0.1 pack.1.refs_0_
  3.2 1.6 %collective-permute-start = (bf16[4,6272]{1,0:T(4,128)(2,1)S(1)}, bf16[4,6272]{1,0:T(4,128)(2,1)S(1)}, u32[]{:S(2)}, u32[]{:S(2)}) collective-permute-start(bf16[4,6272]{1,0:T(4,128)(2,1)S(1)} %pack.1.refs_0_), channel_id=1, source_target_pairs={{0,4},{1,5},{2,6},{3,7},{4,0},{5,1},{6,2},{7,3},{8,12},{9,13},{10,... | collective-permute-start | bytes 150536 | tf_op jit(solution)/shard_map/ppermute | solution.py:308
  4.8 0.0 copy-done.5
  4.8 0.0 collective-permute-start.6
  4.8 2.6 %collective-permute-start.1 = (bf16[4,6272]{1,0:T(4,128)(2,1)S(1)}, bf16[4,6272]{1,0:T(4,128)(2,1)S(1)}, u32[]{:S(2)}, u32[]{:S(2)}) collective-permute-start(bf16[4,6272]{1,0:T(4,128)(2,1)S(1)} %pack.1.refs_0_), channel_id=1, source_target_pairs={{0,8},{1,9},{2,10},{3,11},{4,12},{5,13},{6,14},{7,15},{8,0},{9,1},... | collective-permute-start | bytes 150536 | tf_op jit(solution)/shard_map/ppermute | solution.py:308
  7.4 0.2 collective-permute-start.2
  7.6 0.0 collective-permute-done.6.b_ref
  7.6 0.0 copy-done.2
  7.6 0.1 collective-permute-start.3
  7.7 0.0 collective-permute-done.refs_1_.refs_0_
  7.7 0.8 %collective-permute-start.7 = (s32[1,512]{1,0:T(1,128)S(1)}, s32[1,512]{1,0:T(1,128)S(1)}, u32[]{:S(2)}, u32[]{:S(2)}) collective-permute-start(s32[1,512]{1,0:T(1,128)S(1)} %join.1.refs_5_.refs_6_), channel_id=1, source_target_pairs={{0,2},{1,3},{2,0},{3,1},{4,6},{5,7},{6,4},{7,5},{8,10},{9,11},{10,... | collective-permute-start | bytes 6152 | tf_op jit(solution)/shard_map/ppermute | solution.py:308
  8.4 1.8 %collective-permute-done.4.refs_3_.refs_4_ = bf16[576,256]{1,0:T(8,128)(2,1)S(1)} collective-permute-done((bf16[576,256]{1,0:T(8,128)(2,1)}, bf16[576,256]{1,0:T(8,128)(2,1)S(1)}, u32[]{:S(2)}, u32[]{:S(2)}) %collective-permute-start.4) | collective-permute-done | bytes 294944 | tf_op jit(solution)/shard_map/ppermute | solution.py:308
  10.3 0.0 collective-permute-start.5
  10.3 0.0 copy-start
  10.3 0.7 %collective-permute-done.1.refs_2_.refs_0_ = bf16[4,6272]{1,0:T(4,128)(2,1)S(1)} collective-permute-done((bf16[4,6272]{1,0:T(4,128)(2,1)S(1)}, bf16[4,6272]{1,0:T(4,128)(2,1)S(1)}, u32[]{:S(2)}, u32[]{:S(2)}) %collective-permute-start.1) | collective-permute-done | bytes 50208 | tf_op jit(solution)/shard_map/ppermute | solution.py:308
  11.0 2.2 %collective-permute-done.2.refs_3_.refs_1_ = bf16[4,6272]{1,0:T(4,128)(2,1)S(1)} collective-permute-done((bf16[4,6272]{1,0:T(4,128)(2,1)S(1)}, bf16[4,6272]{1,0:T(4,128)(2,1)S(1)}, u32[]{:S(2)}, u32[]{:S(2)}) %collective-permute-start.2) | collective-permute-done | bytes 50208 | tf_op jit(solution)/shard_map/ppermute | solution.py:308
  13.3 0.0 copy-start.1
  13.3 2.2 %copy-done.1 = bf16[512,4096]{1,0:T(8,128)(2,1)S(1)} copy-done((bf16[512,4096]{1,0:T(8,128)(2,1)S(1)}, bf16[512,4096]{1,0:T(8,128)(2,1)}, u32[]{:S(2)}) %copy-start.1) | copy-done | bytes 4194328
  15.4 1.4 %absorb.1 = (bf16[4,256,512]{2,1,0:T(8,128)(2,1)S(1)}, bf16[4,128,128]{2,1,0:T(8,128)(2,1)S(1)}) custom-call(bf16[4,6272]{1,0:T(4,128)(2,1)S(1)} %pack.1.refs_0_, bf16[4,6272]{1,0:T(4,128)(2,1)S(1)} %collective-permute-done.refs_1_.refs_0_, bf16[4,6272]{1,0:T(4,128)(2,1)S(1)} %collective-permute-done.1.refs_2_.refs_0_, ...), custom_call_target="tpu_custom_call" | custom-call | tf_op jit(solution)/shard_map/absorb/pallas_call | solution.py:131
  16.8 0.0 collective-permute-done.7.refs_6_.refs_7_
  16.8 0.0 collective-permute-done.3.refs_2_.refs_3_
  16.9 0.0 collective-permute-done.5.refs_4_.refs_5_
  16.9 0.0 copy-done
  16.9 2.4 %attend.4 = (f32[4,4224]{1,0:T(4,128)S(1)}, f32[4,4224]{1,0:T(4,128)S(1)}) custom-call(s32[1]{0:T(128)} %bitcast.me_ref, bf16[4,256,512]{2,1,0:T(8,128)(2,1)S(1)} %get-tuple-element.9.a_ref, bf16[4,128,128]{2,1,0:T(8,128)(2,1)S(1)} %get-tuple-element.10.r_ref, bf16[512,4096]{1,0:T(8,128)(2,1)S(1)} %copy-done, ...), custom_call_target="tpu_custom_call" | custom-call | tf_op jit(solution)/shard_map/attend/pallas_call | solution.py:228
  19.3 1.5 %collective-permute-start.8 = (f32[4,4224]{1,0:T(4,128)S(1)}, f32[4,4224]{1,0:T(4,128)S(1)}, u32[]{:S(2)}, u32[]{:S(2)}) collective-permute-start(f32[4,4224]{1,0:T(4,128)S(1)} %get-tuple-element.11), channel_id=1, source_target_pairs={{0,8},{1,9},{2,10},{3,11},{4,12},{5,13},{6,14},{7,15},{8,0},{9,1},... | collective-permute-start | bytes 202760 | tf_op jit(solution)/shard_map/ppermute | solution.py:308
  20.8 0.7 %collective-permute-start.9 = (f32[4,4224]{1,0:T(4,128)S(1)}, f32[4,4224]{1,0:T(4,128)S(1)}, u32[]{:S(2)}, u32[]{:S(2)}) collective-permute-start(f32[4,4224]{1,0:T(4,128)S(1)} %get-tuple-element.12), channel_id=1, source_target_pairs={{0,12},{1,13},{2,14},{3,15},{4,8},{5,9},{6,10},{7,11},{8,4},{9,5},... | collective-permute-start | bytes 202760 | tf_op jit(solution)/shard_map/ppermute | solution.py:308
  21.5 1.6 %attend.5 = f32[4,4224]{1,0:T(4,128)S(1)} custom-call(s32[1]{0:T(128)} %bitcast.me_ref, bf16[4,256,512]{2,1,0:T(8,128)(2,1)S(1)} %get-tuple-element.9.a_ref, bf16[4,128,128]{2,1,0:T(8,128)(2,1)S(1)} %get-tuple-element.10.r_ref, bf16[512,4096]{1,0:T(8,128)(2,1)S(1)} %copy-done, bf16[4,6272]{1,0:T(4,128)(2,1)S(1)} %collective-permute-done.refs_1_.refs_0_, ...), custom_call_target="tpu_custom_call" | custom-call | tf_op jit(solution)/shard_map/attend/pallas_call | solution.py:228
  23.1 1.4 %collective-permute-start.10 = (f32[4,4224]{1,0:T(4,128)S(1)}, f32[4,4224]{1,0:T(4,128)S(1)}, u32[]{:S(2)}, u32[]{:S(2)}) collective-permute-start(f32[4,4224]{1,0:T(4,128)S(1)} %attend.5), channel_id=1, source_target_pairs={{0,4},{1,5},{2,6},{3,7},{4,0},{5,1},{6,2},{7,3},{8,12},{9,13},{10,... | collective-permute-start | bytes 202760 | tf_op jit(solution)/shard_map/ppermute | solution.py:308
  24.5 1.6 %attend.3.refs_0_ = f32[4,4224]{1,0:T(4,128)S(1)} custom-call(s32[1]{0:T(128)} %bitcast.me_ref, bf16[4,256,512]{2,1,0:T(8,128)(2,1)S(1)} %get-tuple-element.9.a_ref, bf16[4,128,128]{2,1,0:T(8,128)(2,1)S(1)} %get-tuple-element.10.r_ref, bf16[512,4096]{1,0:T(8,128)(2,1)S(1)} %copy-done, bf16[4,6272]{1,0:T(4,128)(2,1)S(1)} %pack.1.refs_0_, ...), custom_call_target="tpu_custom_call" | custom-call | tf_op jit(solution)/shard_map/attend/pallas_call | solution.py:228
  26.1 0.0 collective-permute-done.8.refs_1_
  26.1 1.1 %collective-permute-done.9.refs_2_ = f32[4,4224]{1,0:T(4,128)S(1)} collective-permute-done((f32[4,4224]{1,0:T(4,128)S(1)}, f32[4,4224]{1,0:T(4,128)S(1)}, u32[]{:S(2)}, u32[]{:S(2)}) %collective-permute-start.9) | collective-permute-done | bytes 67616 | tf_op jit(solution)/shard_map/ppermute | solution.py:308
  27.3 0.2 merge.1.refs_0_
  27.4 0.6 %collective-permute-done.10.refs_1_ = f32[4,4224]{1,0:T(4,128)S(1)} collective-permute-done((f32[4,4224]{1,0:T(4,128)S(1)}, f32[4,4224]{1,0:T(4,128)S(1)}, u32[]{:S(2)}, u32[]{:S(2)}) %collective-permute-start.10) | collective-permute-done | bytes 67616 | tf_op jit(solution)/shard_map/ppermute | solution.py:308
  28.0 0.8 %combine.1 = bf16[4,4096]{1,0:T(4,128)(2,1)} custom-call(f32[4,4224]{1,0:T(4,128)S(1)} %merge.1.refs_0_, f32[4,4224]{1,0:T(4,128)S(1)} %collective-permute-done.10.refs_1_), custom_call_target="tpu_custom_call" | custom-call | tf_op jit(solution)/shard_map/combine/pallas_call | solution.py:292
  (3 shorter events, 0.0 us)
Async XLA Ops:
  0.0 7.6 %copy-start.2 = (bf16[256,576]{0,1:T(8,128)(2,1)S(1)}, bf16[256,576]{0,1:T(8,128)(2,1)}, u32[]{:S(2)}) copy-start(bf16[256,576]{0,1:T(8,128)(2,1)} %param.10) | copy-start | bytes 884740
  0.0 3.1 %copy-start.6 = (s32[4]{0:T(128)S(1)}, s32[4]{0:T(128)}, u32[]{:S(2)}) copy-start(s32[4]{0:T(128)} %param.12) | copy-start | bytes 52
  0.0 3.1 %copy-start.7 = (s32[4]{0:T(128)S(1)}, s32[4]{0:T(128)}, u32[]{:S(2)}) copy-start(s32[4]{0:T(128)} %param.13) | copy-start | bytes 52
  0.0 3.1 %copy-start.3 = (bf16[4,4096]{1,0:T(4,128)(2,1)S(1)}, bf16[4,4096]{1,0:T(4,128)(2,1)}, u32[]{:S(2)}) copy-start(bf16[4,4096]{1,0:T(4,128)(2,1)} %nope_ref.1) | copy-start | bytes 98308
  0.0 3.1 %copy-start.4 = (bf16[4,2048]{1,0:T(4,128)(2,1)S(1)}, bf16[4,2048]{1,0:T(4,128)(2,1)}, u32[]{:S(2)}) copy-start(bf16[4,2048]{1,0:T(4,128)(2,1)} %rope_ref.1) | copy-start | bytes 49156
  0.0 4.7 %copy-start.5 = (s32[256]{0:T(256)S(1)}, s32[256]{0:T(256)}, u32[]{:S(2)}) copy-start(s32[256]{0:T(256)} %param.11) | copy-start | bytes 3076
  0.0 10.3 %collective-permute-start.4 = (bf16[576,256]{1,0:T(8,128)(2,1)}, bf16[576,256]{1,0:T(8,128)(2,1)S(1)}, u32[]{:S(2)}, u32[]{:S(2)}) collective-permute-start(bf16[576,256]{1,0:T(8,128)(2,1)} %bitcast.5), channel_id=1, source_target_pairs={{0,2},{1,3},{2,0},{3,1},{4,6},{5,7},{6,4},{7,5},{8,10},{9,11},{10,... | collective-permute-start | bytes 884744 | tf_op jit(solution)/shard_map/ppermute | solution.py:308
  3.2 4.5 %collective-permute-start = (bf16[4,6272]{1,0:T(4,128)(2,1)S(1)}, bf16[4,6272]{1,0:T(4,128)(2,1)S(1)}, u32[]{:S(2)}, u32[]{:S(2)}) collective-permute-start(bf16[4,6272]{1,0:T(4,128)(2,1)S(1)} %pack.1.refs_0_), channel_id=1, source_target_pairs={{0,4},{1,5},{2,6},{3,7},{4,0},{5,1},{6,2},{7,3},{8,12},{9,13},{10,... | collective-permute-start | bytes 150536 | tf_op jit(solution)/shard_map/ppermute | solution.py:308
  4.8 2.8 %collective-permute-start.6 = (s32[1,256]{1,0:T(1,128)S(1)}, s32[1,256]{1,0:T(1,128)S(1)}, u32[]{:S(2)}, u32[]{:S(2)}) collective-permute-start(s32[1,256]{1,0:T(1,128)S(1)} %bitcast.10), channel_id=1, source_target_pairs={{0,1},{1,0},{2,3},{3,2},{4,5},{5,4},{6,7},{7,6},{8,9},{9,8},{10,11... | collective-permute-start | bytes 3080 | tf_op jit(solution)/shard_map/ppermute | solution.py:308
  4.8 6.3 %collective-permute-start.1 = (bf16[4,6272]{1,0:T(4,128)(2,1)S(1)}, bf16[4,6272]{1,0:T(4,128)(2,1)S(1)}, u32[]{:S(2)}, u32[]{:S(2)}) collective-permute-start(bf16[4,6272]{1,0:T(4,128)(2,1)S(1)} %pack.1.refs_0_), channel_id=1, source_target_pairs={{0,8},{1,9},{2,10},{3,11},{4,12},{5,13},{6,14},{7,15},{8,0},{9,1},... | collective-permute-start | bytes 150536 | tf_op jit(solution)/shard_map/ppermute | solution.py:308
  7.4 5.9 %collective-permute-start.2 = (bf16[4,6272]{1,0:T(4,128)(2,1)S(1)}, bf16[4,6272]{1,0:T(4,128)(2,1)S(1)}, u32[]{:S(2)}, u32[]{:S(2)}) collective-permute-start(bf16[4,6272]{1,0:T(4,128)(2,1)S(1)} %pack.1.refs_0_), channel_id=1, source_target_pairs={{0,12},{1,13},{2,14},{3,15},{4,8},{5,9},{6,10},{7,11},{8,4},{9,5},... | collective-permute-start | bytes 150536 | tf_op jit(solution)/shard_map/ppermute | solution.py:308
  7.6 9.3 %collective-permute-start.3 = (bf16[576,256]{1,0:T(8,128)(2,1)S(1)}, bf16[576,256]{1,0:T(8,128)(2,1)S(1)}, u32[]{:S(2)}, u32[]{:S(2)}) collective-permute-start(bf16[576,256]{1,0:T(8,128)(2,1)S(1)} %bitcast.6), channel_id=1, source_target_pairs={{0,1},{1,0},{2,3},{3,2},{4,5},{5,4},{6,7},{7,6},{8,9},{9,8},{10,11... | collective-permute-start | bytes 884744 | tf_op jit(solution)/shard_map/ppermute | solution.py:308
  7.7 9.2 %collective-permute-start.7 = (s32[1,512]{1,0:T(1,128)S(1)}, s32[1,512]{1,0:T(1,128)S(1)}, u32[]{:S(2)}, u32[]{:S(2)}) collective-permute-start(s32[1,512]{1,0:T(1,128)S(1)} %join.1.refs_5_.refs_6_), channel_id=1, source_target_pairs={{0,2},{1,3},{2,0},{3,1},{4,6},{5,7},{6,4},{7,5},{8,10},{9,11},{10,... | collective-permute-start | bytes 6152 | tf_op jit(solution)/shard_map/ppermute | solution.py:308
  10.3 6.6 %collective-permute-start.5 = (bf16[576,256]{1,0:T(8,128)(2,1)S(1)}, bf16[576,256]{1,0:T(8,128)(2,1)S(1)}, u32[]{:S(2)}, u32[]{:S(2)}) collective-permute-start(bf16[576,256]{1,0:T(8,128)(2,1)S(1)} %collective-permute-done.4.refs_3_.refs_4_), channel_id=1, source_target_pairs={{0,1},{1,0},{2,3},{3,2},{4,5},{5,4},{6,7},{7,6},{8,9},{9,8},{10,11... | collective-permute-start | bytes 884744 | tf_op jit(solution)/shard_map/ppermute | solution.py:308
  10.3 6.6 %copy-start = (bf16[512,4096]{1,0:T(8,128)(2,1)S(1)}, bf16[512,4096]{1,0:T(8,128)(2,1)}, u32[]{:S(2)}) copy-start(bf16[512,4096]{1,0:T(8,128)(2,1)} %w_ref.5) | copy-start | bytes 12582916
  13.3 2.2 %copy-start.1 = (bf16[512,4096]{1,0:T(8,128)(2,1)S(1)}, bf16[512,4096]{1,0:T(8,128)(2,1)}, u32[]{:S(2)}) copy-start(bf16[512,4096]{1,0:T(8,128)(2,1)} %refs_4_.1) | copy-start | bytes 12582916
  19.3 6.8 %collective-permute-start.8 = (f32[4,4224]{1,0:T(4,128)S(1)}, f32[4,4224]{1,0:T(4,128)S(1)}, u32[]{:S(2)}, u32[]{:S(2)}) collective-permute-start(f32[4,4224]{1,0:T(4,128)S(1)} %get-tuple-element.11), channel_id=1, source_target_pairs={{0,8},{1,9},{2,10},{3,11},{4,12},{5,13},{6,14},{7,15},{8,0},{9,1},... | collective-permute-start | bytes 202760 | tf_op jit(solution)/shard_map/ppermute | solution.py:308
  20.8 6.5 %collective-permute-start.9 = (f32[4,4224]{1,0:T(4,128)S(1)}, f32[4,4224]{1,0:T(4,128)S(1)}, u32[]{:S(2)}, u32[]{:S(2)}) collective-permute-start(f32[4,4224]{1,0:T(4,128)S(1)} %get-tuple-element.12), channel_id=1, source_target_pairs={{0,12},{1,13},{2,14},{3,15},{4,8},{5,9},{6,10},{7,11},{8,4},{9,5},... | collective-permute-start | bytes 202760 | tf_op jit(solution)/shard_map/ppermute | solution.py:308
  23.1 4.9 %collective-permute-start.10 = (f32[4,4224]{1,0:T(4,128)S(1)}, f32[4,4224]{1,0:T(4,128)S(1)}, u32[]{:S(2)}, u32[]{:S(2)}) collective-permute-start(f32[4,4224]{1,0:T(4,128)S(1)} %attend.5), channel_id=1, source_target_pairs={{0,4},{1,5},{2,6},{3,7},{4,0},{5,1},{6,2},{7,3},{8,12},{9,13},{10,... | collective-permute-start | bytes 202760 | tf_op jit(solution)/shard_map/ppermute | solution.py:308
